TPU v7x, 128 devices: a whole 4x4x4 slice. The times are simulated.
128 devices in a mesh: blk: 64 (over y, x, z_lo, core), dim: 2 (over z_hi).
Axes of the slice: x: 4, y: 4, z: 4 (z_hi: 2, z_lo: 2; z = z_hi * 2 + z_lo), core: 2. Of those that a mesh axis runs over, the one named last changes fastest.
Arguments:
- points: bfloat16 [65536, 1024], P('blk', 'dim'), may hold values from -6 to 6
- owner: int32 [65536, 1], P('blk'), may hold values from 0 to 63; in each aligned block of 1024 rows (0 to 1023, 1024 to 2047, ...) at most 32 rows name the same one
- member: int32 [65536], P('blk'), may hold values from 0 to 8191
- centroids: bfloat16 [524288, 1024], P('blk', 'dim'), may hold values from -3 to 3
Outputs:
- new_centroids: bfloat16 [524288, 1024], P('blk', 'dim')
- nearest: float32 [65536], P('blk')
Inputs may be any that keep to these rules, and one draw needn't show every extreme that they name: In the rows of one index of blk, no owner value occurs more than 32 times, and some value occurs exactly 32 times.
All inputs are finite; a program needn't handle non-finite values.
Results may differ from a plain program's by a relative error of at most 0.0004.
Values may be sent and summed in bfloat16 or wider, within the bound.
No kernel may reach another device: no remote copies, remote signals or barrier semaphores. Data moves between devices by JAX's collectives and lax.ppermute only.
A program may use at most 128 MiB of HBM per device.

v0:
```python
import functools

import jax
import jax.numpy as jnp
from jax import lax
from jax.experimental import pallas as pl
from jax.experimental.pallas import tpu as pltpu
from jax.sharding import PartitionSpec as P


D = 1024
CYCLE = 2
LANES = 128
META = 8
TILE = 256
CHUNKS = (1024, 1024, 1024, 512, 512)
COLS = 512
BF16 = jnp.bfloat16
F32 = jnp.float32
I32 = jnp.int32


def iota(shape, dim):
    return lax.broadcasted_iota(I32, shape, dim)


def pack_kernel(lane_ref, owner_ref, member_ref, pts_ref, out_ref, slot_ref, high_ref, low_ref, *, slots):
    count, width = pts_ref.shape
    tiles = width // LANES
    blocks = high_ref.shape[0]
    group = TILE // slots
    step = pl.program_id(0)

    @pl.when(step == 0)
    def _():
        owner = owner_ref[...]
        is_owner = owner == iota((blocks, count), 0)
        weights = jnp.where(is_owner, 1.0, 0.0).astype(BF16)
        before = jnp.where(iota((count, count), 0) < iota((count, count), 1), 1.0, 0.0)
        earlier = jnp.dot(weights, before.astype(BF16), preferred_element_type=F32)
        place = jnp.sum(jnp.where(is_owner, earlier, 0.0), axis=0, keepdims=True).astype(I32)
        slot_ref[...] = owner * slots + place
        member = member_ref[...]
        lane = jnp.where(iota((LANES, count), 0) == place + lane_ref[0], 1.0, 0.0).astype(BF16)

        def spread(row):
            return lax.dot_general(
                jnp.where(is_owner, row.astype(F32), 0.0).astype(BF16),
                lane,
                (((1,), (1,)), ((), ())),
                preferred_element_type=F32,
            )

        high_ref[...] = spread((member >> 6) + 1)
        low_ref[...] = spread(member & 63)

    row = iota((group, META, LANES), 1)
    mine = pl.ds(pl.multiple_of(step * group, group), group)
    high, low = high_ref[mine, :], low_ref[mine, :]
    out_ref[:, slots * tiles :, :] = jnp.where(
        row == 0, high[:, None, :], jnp.where(row == 1, low[:, None, :], 0.0)
    ).astype(BF16)
    pick = jnp.where(iota((TILE, count), 0) + step * TILE == slot_ref[...], 1.0, 0.0).astype(BF16)
    placed = jnp.dot(pick, pts_ref[...], preferred_element_type=F32).astype(BF16)
    for o in range(group):
        for t in range(tiles):
            out_ref[o, t * slots : (t + 1) * slots, :] = placed[
                o * slots : (o + 1) * slots, t * LANES : (t + 1) * LANES
            ]


def pack(lane, owner, member, points, blocks, slots):
    count, width = points.shape
    rows = slots * (width // LANES) + META
    group = TILE // slots
    whole = lambda i: (0, 0)
    return pl.pallas_call(
        functools.partial(pack_kernel, slots=slots),
        out_shape=jax.ShapeDtypeStruct((blocks, rows, LANES), BF16),
        grid=(blocks // group,),
        in_specs=[
            pl.BlockSpec(memory_space=pltpu.SMEM),
            pl.BlockSpec((1, count), whole),
            pl.BlockSpec((1, count), whole),
            pl.BlockSpec((count, width), whole),
        ],
        out_specs=pl.BlockSpec((group, rows, LANES), lambda i: (i, 0, 0)),
        scratch_shapes=[
            pltpu.VMEM((1, count), I32),
            pltpu.VMEM((blocks, LANES), F32),
            pltpu.VMEM((blocks, LANES), F32),
        ],
        compiler_params=pltpu.CompilerParams(
            dimension_semantics=("arbitrary",), vmem_limit_bytes=60 << 20
        ),
        cost_estimate=pl.CostEstimate(
            flops=2 * blocks * slots * count * width, bytes_accessed=6 << 20, transcendentals=0
        ),
        name="pack",
    )(lane, owner, member, points)


def update_kernel(first_ref, got_ref, old_ref, *refs, blocks, slots, chained):
    if chained:
        refs = refs[1:]
    out_ref, part_ref, rows_ref, list_ref = refs
    step = pl.program_id(0)
    width = old_ref.shape[1]
    tiles = width // LANES
    share = LANES // slots
    strips = blocks // share

    @pl.when(step == 0)
    def _():
        for o in range(blocks):
            for t in range(tiles):
                rows_ref[o * slots : (o + 1) * slots, t * LANES : (t + 1) * LANES] = got_ref[
                    o, t * slots : (t + 1) * slots, :
                ]
        meta = got_ref[:, slots * tiles :, :].astype(F32)
        row = iota(meta.shape, 1)
        number = jnp.sum(
            jnp.where(row == 0, meta * 64.0, jnp.where(row == 1, meta, 0.0)), axis=1
        )
        number = jnp.sum(number.reshape(strips, share, LANES), axis=1)
        list_ref[...] = number.astype(I32) - 64

    want = iota((TILE, LANES), 0) + (first_ref[0] + step) * TILE
    picks = []
    total = jnp.zeros((TILE, LANES), F32)
    for g in range(strips):
        hit = jnp.where(list_ref[g : g + 1, :] == want, 1.0, 0.0)
        total = total + hit
        picks.append(hit.astype(BF16))
    sums = jnp.dot(jnp.concatenate(picks, axis=1), rows_ref[...], preferred_element_type=F32)
    counts = jnp.sum(total, axis=1, keepdims=True)
    new = ((sums + old_ref[...].astype(F32)) / (counts + 1.0)).astype(BF16)
    out_ref[...] = new
    part_ref[...] = new


def update(first, got, centroids, so_far, count, blocks, slots):
    lists, width = centroids.shape
    tile = lambda i, first: (first[0] + i, 0)
    chained = so_far is not None
    in_specs = [
        pl.BlockSpec(got.shape, lambda i, first: (0, 0, 0), pipeline_mode=pl.Buffered(1)),
        pl.BlockSpec((TILE, width), tile),
    ]
    args = [first, got, centroids]
    if chained:
        in_specs.append(pl.BlockSpec(memory_space=pl.ANY))
        args.append(so_far)
    return pl.pallas_call(
        functools.partial(update_kernel, blocks=blocks, slots=slots, chained=chained),
        out_shape=(
            jax.ShapeDtypeStruct((lists, width), BF16),
            jax.ShapeDtypeStruct((count, width), BF16),
        ),
        grid_spec=pltpu.PrefetchScalarGridSpec(
            num_scalar_prefetch=1,
            grid=(count // TILE,),
            in_specs=in_specs,
            out_specs=(
                pl.BlockSpec((TILE, width), tile),
                pl.BlockSpec((TILE, width), lambda i, first: (i, 0)),
            ),
            scratch_shapes=[
                pltpu.VMEM((blocks * slots, width), BF16),
                pltpu.VMEM((blocks * slots // LANES, LANES), I32),
            ],
        ),
        input_output_aliases={3: 0} if chained else {},
        compiler_params=pltpu.CompilerParams(
            dimension_semantics=("arbitrary",), vmem_limit_bytes=24 << 20
        ),
        cost_estimate=pl.CostEstimate(
            flops=2 * count * blocks * slots * width,
            bytes_accessed=got.size * 2 + count * width * 6,
            transcendentals=0,
        ),
        name="update",
    )(*args)


def search_kernel(own_ref, other_ref, *refs, first, last):
    sections = CYCLE + 1
    points, refs = refs[: 2 * sections], refs[2 * sections :]
    if not first:
        before_ref, refs = refs[0], refs[1:]
    if last:
        outs, best_ref = refs[:sections], refs[sections]
    else:
        best_ref = refs[0]
    step = pl.program_id(0)
    count = points[0].shape[1]

    @pl.when(step == 0)
    def _():
        best_ref[...] = jnp.full_like(best_ref, -jnp.inf) if first else before_ref[...]

    own, other = own_ref[...], other_ref[...]
    own_f, other_f = own.astype(F32), other.astype(F32)
    half = 0.5 * (
        jnp.sum(own_f * own_f, axis=1, keepdims=True)
        + jnp.sum(other_f * other_f, axis=1, keepdims=True)
    )
    for s in range(sections):
        for c in range(0, count, COLS):
            score = jnp.dot(own, points[2 * s][:, c : c + COLS], preferred_element_type=F32)
            score += jnp.dot(other, points[2 * s + 1][:, c : c + COLS], preferred_element_type=F32)
            score -= half
            top = jnp.max(score.reshape(-1, 8, COLS), axis=0)
            at = slice(s * count + c, s * count + c + COLS)
            best_ref[:, at] = jnp.maximum(best_ref[:, at], top)

    if last:

        @pl.when(step == pl.num_programs(0) - 1)
        def _():
            for s in range(sections):
                outs[s][...] = jnp.max(
                    best_ref[:, s * count : (s + 1) * count], axis=0, keepdims=True
                )


def search(own, offset, other, points, before, last):
    chunk, width = other.shape
    sections = CYCLE + 1
    count = points[0].shape[1]
    tile = TILE if chunk % (2 * TILE) else 2 * TILE
    whole = lambda i: (0, 0)
    in_specs = [
        pl.BlockSpec((tile, width), lambda i: (i + offset // tile, 0)),
        pl.BlockSpec((tile, width), lambda i: (i, 0)),
    ]
    in_specs += [pl.BlockSpec((width, count), whole, pipeline_mode=pl.Buffered(1))] * len(points)
    args = [own, other, *points]
    best = (8, sections * count)
    if before is not None:
        in_specs.append(pl.BlockSpec(best, whole))
        args.append(before)
    scratch = []
    if last:
        out_shape = [jax.ShapeDtypeStruct((1, count), F32)] * sections
        out_specs = [pl.BlockSpec((1, count), whole)] * sections
        scratch = [pltpu.VMEM(best, F32)]
    else:
        out_shape = jax.ShapeDtypeStruct(best, F32)
        out_specs = pl.BlockSpec(best, whole)
    return pl.pallas_call(
        functools.partial(search_kernel, first=before is None, last=last),
        out_shape=out_shape,
        grid=(chunk // tile,),
        in_specs=in_specs,
        out_specs=out_specs,
        scratch_shapes=scratch,
        compiler_params=pltpu.CompilerParams(
            dimension_semantics=("arbitrary",), vmem_limit_bytes=28 << 20
        ),
        cost_estimate=pl.CostEstimate(
            flops=4 * chunk * width * sections * count,
            bytes_accessed=len(points) * width * count * 2 + chunk * width * 4,
            transcendentals=0,
        ),
        name="search",
    )(*args)


def step(points, owner, member, centroids):
    lists, width = centroids.shape
    count = points.shape[0]
    blocks = lax.axis_size("blk")
    slots = 2 * count // blocks
    both = ("blk", "dim")
    mine = lax.axis_index("blk")
    side = lax.axis_index("dim")
    ids = [(b, d) for b in range(blocks) for d in range(2)]

    def fetch(x, source):
        route = []
        for b, d in ids:
            sb, sd = source(b, d)
            route.append(((sb % blocks) * 2 + sd, b * 2 + d))
        return lax.ppermute(x, both, route)

    near_own = fetch(points, lambda b, d: (b ^ 2, d))
    near_other = fetch(points, lambda b, d: (b ^ 2, 1 - d))

    lane = ((mine % (LANES // slots)) * slots).astype(I32).reshape(1)
    sent = pack(lane, owner.reshape(1, count), member.reshape(1, count), points, blocks, slots)
    got = lax.all_to_all(sent, "blk", split_axis=0, concat_axis=0, tiled=True)

    own_0 = points.T
    near_own, near_other = near_own.T, near_other.T
    part = width // 2
    first_part = fetch(near_other[:part], lambda b, d: (b ^ 2, d))
    second_part = fetch(near_own[part:], lambda b, d: (b ^ 2, 1 - d))
    onward = lambda b, d: (b + 4 if b & 2 else b, d)
    own_2 = fetch(near_own, onward)
    other_2 = fetch(near_other, onward)
    other_0 = jnp.concatenate([first_part, second_part], axis=0)
    even = mine % 2 == 0
    own_1 = fetch(jnp.where(even, own_2, own_0), lambda b, d: (b ^ 1, d))
    other_1 = fetch(jnp.where(even, other_2, other_0), lambda b, d: (b ^ 1, d))
    visitors = [own_0, other_0, own_1, other_1, own_2, other_2]
    squares = jnp.sum(jnp.square(own_0.astype(F32)), axis=0) + jnp.sum(
        jnp.square(other_0.astype(F32)), axis=0
    )

    old = pltpu.with_memory_space_constraint(centroids, pltpu.HBM)
    half_tiles = lists // 2 // TILE
    new_centroids = None
    arrived = []
    done = 0
    for chunk in CHUNKS:
        first = ((1 - side) * half_tiles + done // TILE).astype(I32).reshape(1)
        new_centroids, part = update(first, got, old, new_centroids, chunk, blocks, slots)
        arrived.append(fetch(part, lambda b, d: (b, 1 - d)))
        done += chunk
    first = (side * half_tiles).astype(I32).reshape(1)
    new_centroids, own_half = update(
        first, got, old, new_centroids, lists // 2, blocks, slots
    )

    best = None
    done = 0
    for n, chunk in enumerate(CHUNKS):
        best = search(own_half, done, arrived[n], visitors, best, n == len(CHUNKS) - 1)
        done += chunk
    best = [x.reshape(count) for x in best]
    top = jnp.maximum(best[0], fetch(best[0], lambda b, d: (b, 1 - d)))
    for s in range(1, CYCLE + 1):
        for flip in (0, 1):
            top = jnp.maximum(top, fetch(best[s], lambda b, d: (b - s, d ^ flip)))
    nearest = (squares - 2.0 * top) / D
    return new_centroids, nearest


def solution(mesh):
    in_specs = (P("blk", "dim"), P("blk", None), P("blk"), P("blk", "dim"))
    out_specs = (P("blk", "dim"), P("blk"))
    return jax.shard_map(step, mesh=mesh, in_specs=in_specs, out_specs=out_specs, check_vma=False)
```

profile of v0, /device:TPU:24, one launch (start us, length us, event | category | flops | bytes accessed | tf_op | source)
XLA Modules:
  0.0 214.2 jit_solution(10282789726037106611)
XLA Ops:
  0.6 1.5 copy.11
  2.1 4.1 %collective-permute-start = (bf16[1024,512]{0,1:T(8,128)(2,1)S(1)}, bf16[1024,512]{0,1:T(8,128)(2,1)}, u32[]{:S(2)}, u32[]{:S(2)}) collective-permute-start(bf16[1024,512]{0,1:T(8,128)(2,1)S(1)} %copy.11), channel_id=1, source_target_pairs={{5,0},{4,1},{7,2},{6,3},{1,4},{0,5},{3,6},{2,7},{13,8},{12,9},{15,... | collective-permute-start | bytes 3145736 | tf_op jit(solution)/shard_map/ppermute | solution.py:285
  6.2 0.0 collective-permute-start.2
  6.2 6.9 %pack.1 = bf16[64,136,128]{2,1,0:T(8,128)(2,1)} custom-call(s32[1]{0:T(128)} %bitcast.1.lane_ref, s32[1,1024]{1,0:T(1,128)} %bitcast.28, s32[1,1024]{1,0:T(1,128)} %bitcast.29, bf16[1024,512]{1,0:T(8,128)(2,1)} %pts_ref.1), custom_call_target="tpu_custom_call" | custom-call | flops 2147483648 | bytes 6291456 | tf_op jit(solution)/shard_map/pack/pallas_call | solution.py:77
  13.1 9.4 %all-to-all-start = ((bf16[64,136,128]{2,1,0:T(8,128)(2,1)}), bf16[64,136,128]{2,1,0:T(8,128)(2,1)S(1)}, u32[]{:S(2)}, u32[]{:S(2)}) async-start(bf16[64,136,128]{2,1,0:T(8,128)(2,1)} %pack.1), calls=%async_computation | async-start | bytes 4456448 | tf_op jit(solution)/shard_map/all_to_all | solution.py:292
  22.5 7.0 %collective-permute-done = bf16[1024,512]{0,1:T(8,128)(2,1)} collective-permute-done((bf16[1024,512]{0,1:T(8,128)(2,1)S(1)}, bf16[1024,512]{0,1:T(8,128)(2,1)}, u32[]{:S(2)}, u32[]{:S(2)}) %collective-permute-start) | collective-permute-done | bytes 1048608 | tf_op jit(solution)/shard_map/ppermute | solution.py:285
  29.5 9.5 %collective-permute-start.7 = (bf16[512,1024]{1,0:T(8,128)(2,1)}, bf16[512,1024]{1,0:T(8,128)(2,1)}, u32[]{:S(2)}, u32[]{:S(2)}) collective-permute-start(bf16[512,1024]{1,0:T(8,128)(2,1)} %bitcast.10), channel_id=1, source_target_pairs={{0,0},{1,1},{2,2},{3,3},{12,4},{13,5},{14,6},{15,7},{8,8},{9,9},{1... | collective-permute-start | bytes 3145736 | tf_op jit(solution)/shard_map/ppermute | solution.py:285
  39.0 1.9 slice.8
  40.8 0.0 collective-permute-start.1
  40.8 13.9 %collective-permute-done.2 = bf16[1024,512]{0,1:T(8,128)(2,1)} collective-permute-done((bf16[1024,512]{0,1:T(8,128)(2,1)S(1)}, bf16[1024,512]{0,1:T(8,128)(2,1)}, u32[]{:S(2)}, u32[]{:S(2)}) %collective-permute-start.2) | collective-permute-done | bytes 1048608 | tf_op jit(solution)/shard_map/ppermute | solution.py:285
  54.8 9.4 %collective-permute-start.5 = (bf16[512,1024]{1,0:T(8,128)(2,1)}, bf16[512,1024]{1,0:T(8,128)(2,1)}, u32[]{:S(2)}, u32[]{:S(2)}) collective-permute-start(bf16[512,1024]{1,0:T(8,128)(2,1)} %bitcast.11), channel_id=1, source_target_pairs={{0,0},{1,1},{2,2},{3,3},{12,4},{13,5},{14,6},{15,7},{8,8},{9,9},{1... | collective-permute-start | bytes 3145736 | tf_op jit(solution)/shard_map/ppermute | solution.py:285
  64.2 1.9 slice.9
  66.1 0.2 multiply_reduce_fusion.1
  66.3 0.0 collective-permute-done.1
  66.3 1.1 constant_dynamic-update-slice_fusion.1
  67.4 11.3 %collective-permute-done.3 = bf16[256,1024]{1,0:T(8,128)(2,1)} collective-permute-done((bf16[256,1024]{1,0:T(8,128)(2,1)}, bf16[256,1024]{1,0:T(8,128)(2,1)}, u32[]{:S(2)}, u32[]{:S(2)}) %collective-permute-start.3) | collective-permute-done | bytes 524320 | tf_op jit(solution)/shard_map/ppermute | solution.py:285
  78.7 1.1 constant_dynamic-update-slice_fusion.refs_1_
  79.8 2.7 %broadcast_select_fusion = bf16[512,1024]{1,0:T(8,128)(2,1)} fusion(bf16[512,1024]{1,0:T(8,128)(2,1)} %collective-permute-done.7.refs_5_, bf16[512,1024]{1,0:T(8,128)(2,1)S(1)} %constant_dynamic-update-slice_fusion.refs_1_, pred[]{:T(512)S(6)} %eq.6), kind=kLoop, calls=%fused_computation.2 | loop fusion | flops 524288 | bytes 3145729 | tf_op jit(solution)/shard_map/jit(_where)/select_n | solution.py:305
  82.5 2.3 %broadcast_select_fusion.1 = bf16[512,1024]{1,0:T(8,128)(2,1)} fusion(bf16[512,1024]{1,0:T(8,128)(2,1)} %collective-permute-done.5.refs_4_, pred[]{:T(512)S(6)} %eq.6, bf16[1024,512]{0,1:T(8,128)(2,1)S(1)} %copy.11), kind=kLoop, calls=%fused_computation.3 | loop fusion | flops 524288 | bytes 3145729 | tf_op jit(solution)/shard_map/jit(_where)/select_n | solution.py:304
  84.8 0.0 collective-permute-start.6
  84.8 0.0 all-to-all-done.got_ref
  84.8 5.6 %update.6 = (bf16[8192,512]{1,0:T(8,128)(2,1)}, bf16[1024,512]{1,0:T(8,128)(2,1)S(1)}) custom-call(s32[1]{0:T(128)} %bitcast.8.first_ref, bf16[64,136,128]{2,1,0:T(8,128)(2,1)S(1)} %all-to-all-done.got_ref, bf16[8192,512]{1,0:T(8,128)(2,1)} %old_ref.11), custom_call_target="tpu_custom_call" | custom-call | flops 2147483648 | bytes 5373952 | tf_op jit(solution)/shard_map/update/pallas_call | solution.py:154
  90.4 5.6 %update.7 = (bf16[8192,512]{1,0:T(8,128)(2,1)}, bf16[1024,512]{1,0:T(8,128)(2,1)S(1)}) custom-call(s32[1]{0:T(128)} %bitcast.7.first_ref, bf16[64,136,128]{2,1,0:T(8,128)(2,1)S(1)} %all-to-all-done.got_ref, bf16[8192,512]{1,0:T(8,128)(2,1)} %old_ref.11, bf16[8192,512]{1,0:T(8,128)(2,1)} %get-tuple-element.17.refs_0_), custom_call_target="tpu_custom_call", output_to_operand_aliasing={{0}: (3, {})} | custom-call | flops 2147483648 | bytes 5373952 | tf_op jit(solution)/shard_map/update/pallas_call | solution.py:154
  96.0 3.5 %collective-permute-start.11 = (bf16[1024,512]{1,0:T(8,128)(2,1)S(1)}, bf16[1024,512]{1,0:T(8,128)(2,1)S(1)}, u32[]{:S(2)}, u32[]{:S(2)}) collective-permute-start(bf16[1024,512]{1,0:T(8,128)(2,1)S(1)} %get-tuple-element.27), channel_id=1, source_target_pairs={{1,0},{0,1},{3,2},{2,3},{5,4},{4,5},{7,6},{6,7},{9,8},{8,9},{11,10... | collective-permute-start | bytes 3145736 | tf_op jit(solution)/shard_map/ppermute | solution.py:285
  99.5 5.5 %update.8 = (bf16[8192,512]{1,0:T(8,128)(2,1)}, bf16[1024,512]{1,0:T(8,128)(2,1)S(1)}) custom-call(s32[1]{0:T(128)} %bitcast.6.first_ref, bf16[64,136,128]{2,1,0:T(8,128)(2,1)S(1)} %all-to-all-done.got_ref, bf16[8192,512]{1,0:T(8,128)(2,1)} %old_ref.11, bf16[8192,512]{1,0:T(8,128)(2,1)} %get-tuple-element.18.refs_0_), custom_call_target="tpu_custom_call", output_to_operand_aliasing={{0}: (3, {})} | custom-call | flops 2147483648 | bytes 5373952 | tf_op jit(solution)/shard_map/update/pallas_call | solution.py:154
  105.0 0.0 collective-permute-start.10
  105.0 3.7 %update.9 = (bf16[8192,512]{1,0:T(8,128)(2,1)}, bf16[512,512]{1,0:T(8,128)(2,1)S(1)}) custom-call(s32[1]{0:T(128)} %bitcast.5.first_ref, bf16[64,136,128]{2,1,0:T(8,128)(2,1)S(1)} %all-to-all-done.got_ref, bf16[8192,512]{1,0:T(8,128)(2,1)} %old_ref.11, bf16[8192,512]{1,0:T(8,128)(2,1)} %get-tuple-element.19.refs_0_), custom_call_target="tpu_custom_call", output_to_operand_aliasing={{0}: (3, {})} | custom-call | flops 1073741824 | bytes 3801088 | tf_op jit(solution)/shard_map/update/pallas_call | solution.py:154
  108.7 3.7 %update.10 = (bf16[8192,512]{1,0:T(8,128)(2,1)}, bf16[512,512]{1,0:T(8,128)(2,1)S(1)}) custom-call(s32[1]{0:T(128)} %bitcast.4.first_ref, bf16[64,136,128]{2,1,0:T(8,128)(2,1)S(1)} %all-to-all-done.got_ref, bf16[8192,512]{1,0:T(8,128)(2,1)} %old_ref.11, bf16[8192,512]{1,0:T(8,128)(2,1)} %get-tuple-element.20.refs_0_), custom_call_target="tpu_custom_call", output_to_operand_aliasing={{0}: (3, {})} | custom-call | flops 1073741824 | bytes 3801088 | tf_op jit(solution)/shard_map/update/pallas_call | solution.py:154
  112.4 16.7 %update.11 = (bf16[8192,512]{1,0:T(8,128)(2,1)}, bf16[4096,512]{1,0:T(8,128)(2,1)S(1)}) custom-call(s32[1]{0:T(128)} %bitcast.first_ref, bf16[64,136,128]{2,1,0:T(8,128)(2,1)S(1)} %all-to-all-done.got_ref, bf16[8192,512]{1,0:T(8,128)(2,1)} %old_ref.11, bf16[8192,512]{1,0:T(8,128)(2,1)} %get-tuple-element.21.refs_0_), custom_call_target="tpu_custom_call", output_to_operand_aliasing={{0}: (3, {})} | custom-call | flops 8589934592 | bytes 14811136 | tf_op jit(solution)/shard_map/update/pallas_call | solution.py:154
  129.2 0.0 collective-permute-done.8.refs_3_
  129.2 3.5 %collective-permute-start.9 = (bf16[512,512]{1,0:T(8,128)(2,1)S(1)}, bf16[512,512]{1,0:T(8,128)(2,1)S(1)}, u32[]{:S(2)}, u32[]{:S(2)}) collective-permute-start(bf16[512,512]{1,0:T(8,128)(2,1)S(1)} %get-tuple-element.25), channel_id=1, source_target_pairs={{1,0},{0,1},{3,2},{2,3},{5,4},{4,5},{7,6},{6,7},{9,8},{8,9},{11,10... | collective-permute-start | bytes 1572872 | tf_op jit(solution)/shard_map/ppermute | solution.py:285
  132.7 0.0 collective-permute-done.6.refs_2_
  132.7 0.1 collective-permute-start.4
  132.8 9.1 %search.5.refs_6_ = f32[8,3072]{1,0:T(8,128)S(1)} custom-call(bf16[4096,512]{1,0:T(8,128)(2,1)S(1)} %get-tuple-element.23.own_ref, bf16[1024,512]{1,0:T(8,128)(2,1)S(1)} %collective-permute-done.12.other_ref, bf16[512,1024]{1,0:T(8,128)(2,1)S(1)} %bitcast.17, bf16[512,1024]{1,0:T(8,128)(2,1)S(1)} %copy-done.1, ...), custom_call_target="tpu_custom_call" | custom-call | flops 6442450944 | bytes 8388608 | tf_op jit(solution)/shard_map/search/pallas_call | solution.py:251
  141.9 9.1 %search.6.refs_6_ = f32[8,3072]{1,0:T(8,128)S(1)} custom-call(bf16[4096,512]{1,0:T(8,128)(2,1)S(1)} %get-tuple-element.23.own_ref, bf16[1024,512]{1,0:T(8,128)(2,1)S(1)} %collective-permute-done.11.other_ref, bf16[512,1024]{1,0:T(8,128)(2,1)S(1)} %bitcast.18, bf16[512,1024]{1,0:T(8,128)(2,1)S(1)} %copy-done.1, ...), custom_call_target="tpu_custom_call" | custom-call | flops 6442450944 | bytes 8388608 | tf_op jit(solution)/shard_map/search/pallas_call | solution.py:251
  151.0 11.9 %collective-permute-done.10.other_ref = bf16[1024,512]{1,0:T(8,128)(2,1)S(1)} collective-permute-done((bf16[1024,512]{1,0:T(8,128)(2,1)S(1)}, bf16[1024,512]{1,0:T(8,128)(2,1)S(1)}, u32[]{:S(2)}, u32[]{:S(2)}) %collective-permute-start.10) | collective-permute-done | bytes 1048608 | tf_op jit(solution)/shard_map/ppermute | solution.py:285
  162.9 9.3 %search.7.refs_6_ = f32[8,3072]{1,0:T(8,128)S(1)} custom-call(bf16[4096,512]{1,0:T(8,128)(2,1)S(1)} %get-tuple-element.23.own_ref, bf16[1024,512]{1,0:T(8,128)(2,1)S(1)} %collective-permute-done.10.other_ref, bf16[512,1024]{1,0:T(8,128)(2,1)S(1)} %bitcast.19, bf16[512,1024]{1,0:T(8,128)(2,1)S(1)} %copy-done.1, ...), custom_call_target="tpu_custom_call" | custom-call | flops 6442450944 | bytes 8388608 | tf_op jit(solution)/shard_map/search/pallas_call | solution.py:251
  172.2 1.9 collective-permute-done.9.other_ref
  174.1 5.6 %search.8.refs_6_ = f32[8,3072]{1,0:T(8,128)S(1)} custom-call(bf16[4096,512]{1,0:T(8,128)(2,1)S(1)} %get-tuple-element.23.own_ref, bf16[512,512]{1,0:T(8,128)(2,1)S(1)} %collective-permute-done.9.other_ref, bf16[512,1024]{1,0:T(8,128)(2,1)S(1)} %bitcast.20, bf16[512,1024]{1,0:T(8,128)(2,1)S(1)} %copy-done.1, ...), custom_call_target="tpu_custom_call" | custom-call | flops 3221225472 | bytes 7340032 | tf_op jit(solution)/shard_map/search/pallas_call | solution.py:251
  179.7 5.2 %collective-permute-done.4.other_ref = bf16[512,512]{1,0:T(8,128)(2,1)S(1)} collective-permute-done((bf16[512,512]{1,0:T(8,128)(2,1)S(1)}, bf16[512,512]{1,0:T(8,128)(2,1)S(1)}, u32[]{:S(2)}, u32[]{:S(2)}) %collective-permute-start.4) | collective-permute-done | bytes 524320 | tf_op jit(solution)/shard_map/ppermute | solution.py:285
  184.9 5.6 %search.9 = (f32[1,1024]{1,0:T(1,128)S(1)}, f32[1,1024]{1,0:T(1,128)S(1)}, f32[1,1024]{1,0:T(1,128)S(1)}) custom-call(bf16[4096,512]{1,0:T(8,128)(2,1)S(1)} %get-tuple-element.23.own_ref, bf16[512,512]{1,0:T(8,128)(2,1)S(1)} %collective-permute-done.4.other_ref, bf16[512,1024]{1,0:T(8,128)(2,1)S(1)} %bitcast.21, bf16[512,1024]{1,0:T(8,128)(2,1)S(1)} %copy-done.1, ...), custom_call_target="tpu_custom_call" | custom-call | flops 3221225472 | bytes 7340032 | tf_op jit(solution)/shard_map/search/pallas_call | solution.py:251
  190.5 0.1 collective-permute-start.14
  190.6 13.3 %collective-permute-start.15 = (f32[1024]{0:T(1024)S(1)}, f32[1024]{0:T(1024)S(1)}, u32[]{:S(2)}, u32[]{:S(2)}) collective-permute-start(f32[1024]{0:T(1024)S(1)} %bitcast.27), channel_id=1, source_target_pairs={{127,0},{126,1},{1,2},{0,3},{3,4},{2,5},{5,6},{4,7},{7,8},{6,9},{9... | collective-permute-start | bytes 12296 | tf_op jit(solution)/shard_map/ppermute | solution.py:285
  203.9 4.6 %collective-permute-start.17 = (f32[1024]{0:T(1024)S(1)}, f32[1024]{0:T(1024)S(1)}, u32[]{:S(2)}, u32[]{:S(2)}) collective-permute-start(f32[1024]{0:T(1024)S(1)} %bitcast.25), channel_id=1, source_target_pairs={{125,0},{124,1},{127,2},{126,3},{1,4},{0,5},{3,6},{2,7},{5,8},{4,9... | collective-permute-start | bytes 12296 | tf_op jit(solution)/shard_map/ppermute | solution.py:285
  208.5 0.9 collective-permute-start.13
  209.4 0.2 multiply_reduce_fusion
  209.6 4.0 %collective-permute-done.13 = f32[1024]{0:T(1024)S(1)} collective-permute-done((f32[1024]{0:T(1024)S(1)}, f32[1024]{0:T(1024)S(1)}, u32[]{:S(2)}, u32[]{:S(2)}) %collective-permute-start.13) | collective-permute-done | bytes 4128 | tf_op jit(solution)/shard_map/ppermute | solution.py:285
  213.6 0.6 subtract_multiply_fusion
  (16 shorter events, 0.0 us)
Async XLA Ops:
  2.1 27.4 %collective-permute-start = (bf16[1024,512]{0,1:T(8,128)(2,1)S(1)}, bf16[1024,512]{0,1:T(8,128)(2,1)}, u32[]{:S(2)}, u32[]{:S(2)}) collective-permute-start(bf16[1024,512]{0,1:T(8,128)(2,1)S(1)} %copy.11), channel_id=1, source_target_pairs={{5,0},{4,1},{7,2},{6,3},{1,4},{0,5},{3,6},{2,7},{13,8},{12,9},{15,... | collective-permute-start | bytes 3145736 | tf_op jit(solution)/shard_map/ppermute | solution.py:285
  6.2 48.5 %collective-permute-start.2 = (bf16[1024,512]{0,1:T(8,128)(2,1)S(1)}, bf16[1024,512]{0,1:T(8,128)(2,1)}, u32[]{:S(2)}, u32[]{:S(2)}) collective-permute-start(bf16[1024,512]{0,1:T(8,128)(2,1)S(1)} %copy.11), channel_id=1, source_target_pairs={{4,0},{5,1},{6,2},{7,3},{0,4},{1,5},{2,6},{3,7},{12,8},{13,9},{14,... | collective-permute-start | bytes 3145736 | tf_op jit(solution)/shard_map/ppermute | solution.py:285
  13.1 71.7 %all-to-all-start = ((bf16[64,136,128]{2,1,0:T(8,128)(2,1)}), bf16[64,136,128]{2,1,0:T(8,128)(2,1)S(1)}, u32[]{:S(2)}, u32[]{:S(2)}) async-start(bf16[64,136,128]{2,1,0:T(8,128)(2,1)} %pack.1), calls=%async_computation | async-start | bytes 4456448 | tf_op jit(solution)/shard_map/all_to_all | solution.py:292
  29.5 50.3 %collective-permute-start.7 = (bf16[512,1024]{1,0:T(8,128)(2,1)}, bf16[512,1024]{1,0:T(8,128)(2,1)}, u32[]{:S(2)}, u32[]{:S(2)}) collective-permute-start(bf16[512,1024]{1,0:T(8,128)(2,1)} %bitcast.10), channel_id=1, source_target_pairs={{0,0},{1,1},{2,2},{3,3},{12,4},{13,5},{14,6},{15,7},{8,8},{9,9},{1... | collective-permute-start | bytes 3145736 | tf_op jit(solution)/shard_map/ppermute | solution.py:285
  40.8 25.5 %collective-permute-start.1 = (bf16[256,1024]{1,0:T(8,128)(2,1)}, bf16[256,1024]{1,0:T(8,128)(2,1)}, u32[]{:S(2)}, u32[]{:S(2)}) collective-permute-start(bf16[256,1024]{1,0:T(8,128)(2,1)} %slice.8), channel_id=1, source_target_pairs={{4,0},{5,1},{6,2},{7,3},{0,4},{1,5},{2,6},{3,7},{12,8},{13,9},{14,... | collective-permute-start | bytes 1572872 | tf_op jit(solution)/shard_map/ppermute | solution.py:285
  54.8 27.8 %collective-permute-start.5 = (bf16[512,1024]{1,0:T(8,128)(2,1)}, bf16[512,1024]{1,0:T(8,128)(2,1)}, u32[]{:S(2)}, u32[]{:S(2)}) collective-permute-start(bf16[512,1024]{1,0:T(8,128)(2,1)} %bitcast.11), channel_id=1, source_target_pairs={{0,0},{1,1},{2,2},{3,3},{12,4},{13,5},{14,6},{15,7},{8,8},{9,9},{1... | collective-permute-start | bytes 3145736 | tf_op jit(solution)/shard_map/ppermute | solution.py:285
  66.1 12.6 %collective-permute-start.3 = (bf16[256,1024]{1,0:T(8,128)(2,1)}, bf16[256,1024]{1,0:T(8,128)(2,1)}, u32[]{:S(2)}, u32[]{:S(2)}) collective-permute-start(bf16[256,1024]{1,0:T(8,128)(2,1)} %slice.9), channel_id=1, source_target_pairs={{5,0},{4,1},{7,2},{6,3},{1,4},{0,5},{3,6},{2,7},{13,8},{12,9},{15,... | collective-permute-start | bytes 1572872 | tf_op jit(solution)/shard_map/ppermute | solution.py:285
  79.8 5.0 %copy-start = (bf16[512,1024]{1,0:T(8,128)(2,1)}, bf16[512,1024]{1,0:T(8,128)(2,1)S(1)}, u32[]{:S(2)}) copy-start(bf16[512,1024]{1,0:T(8,128)(2,1)S(1)} %constant_dynamic-update-slice_fusion.refs_1_) | copy-start | bytes 3145732
  82.5 46.7 %collective-permute-start.8 = (bf16[512,1024]{1,0:T(8,128)(2,1)}, bf16[512,1024]{1,0:T(8,128)(2,1)}, u32[]{:S(2)}, u32[]{:S(2)}) collective-permute-start(bf16[512,1024]{1,0:T(8,128)(2,1)} %broadcast_select_fusion), channel_id=1, source_target_pairs={{2,0},{3,1},{0,2},{1,3},{6,4},{7,5},{4,6},{5,7},{10,8},{11,9},{8,1... | collective-permute-start | bytes 3145736 | tf_op jit(solution)/shard_map/ppermute | solution.py:285
  84.8 47.9 %collective-permute-start.6 = (bf16[512,1024]{1,0:T(8,128)(2,1)}, bf16[512,1024]{1,0:T(8,128)(2,1)}, u32[]{:S(2)}, u32[]{:S(2)}) collective-permute-start(bf16[512,1024]{1,0:T(8,128)(2,1)} %broadcast_select_fusion.1), channel_id=1, source_target_pairs={{2,0},{3,1},{0,2},{1,3},{6,4},{7,5},{4,6},{5,7},{10,8},{11,9},{8,1... | collective-permute-start | bytes 3145736 | tf_op jit(solution)/shard_map/ppermute | solution.py:285
  90.4 42.4 %collective-permute-start.12 = (bf16[1024,512]{1,0:T(8,128)(2,1)S(1)}, bf16[1024,512]{1,0:T(8,128)(2,1)S(1)}, u32[]{:S(2)}, u32[]{:S(2)}) collective-permute-start(bf16[1024,512]{1,0:T(8,128)(2,1)S(1)} %get-tuple-element.28), channel_id=1, source_target_pairs={{1,0},{0,1},{3,2},{2,3},{5,4},{4,5},{7,6},{6,7},{9,8},{8,9},{11,10... | collective-permute-start | bytes 3145736 | tf_op jit(solution)/shard_map/ppermute | solution.py:285
  96.0 45.9 %collective-permute-start.11 = (bf16[1024,512]{1,0:T(8,128)(2,1)S(1)}, bf16[1024,512]{1,0:T(8,128)(2,1)S(1)}, u32[]{:S(2)}, u32[]{:S(2)}) collective-permute-start(bf16[1024,512]{1,0:T(8,128)(2,1)S(1)} %get-tuple-element.27), channel_id=1, source_target_pairs={{1,0},{0,1},{3,2},{2,3},{5,4},{4,5},{7,6},{6,7},{9,8},{8,9},{11,10... | collective-permute-start | bytes 3145736 | tf_op jit(solution)/shard_map/ppermute | solution.py:285
  105.0 57.9 %collective-permute-start.10 = (bf16[1024,512]{1,0:T(8,128)(2,1)S(1)}, bf16[1024,512]{1,0:T(8,128)(2,1)S(1)}, u32[]{:S(2)}, u32[]{:S(2)}) collective-permute-start(bf16[1024,512]{1,0:T(8,128)(2,1)S(1)} %get-tuple-element.26), channel_id=1, source_target_pairs={{1,0},{0,1},{3,2},{2,3},{5,4},{4,5},{7,6},{6,7},{9,8},{8,9},{11,10... | collective-permute-start | bytes 3145736 | tf_op jit(solution)/shard_map/ppermute | solution.py:285
  112.4 20.3 %copy-start.1 = (bf16[512,1024]{1,0:T(8,128)(2,1)S(1)}, bf16[512,1024]{1,0:T(8,128)(2,1)}, u32[]{:S(2)}) copy-start(bf16[512,1024]{1,0:T(8,128)(2,1)} %copy-done) | copy-start | bytes 3145732
  129.2 44.9 %collective-permute-start.9 = (bf16[512,512]{1,0:T(8,128)(2,1)S(1)}, bf16[512,512]{1,0:T(8,128)(2,1)S(1)}, u32[]{:S(2)}, u32[]{:S(2)}) collective-permute-start(bf16[512,512]{1,0:T(8,128)(2,1)S(1)} %get-tuple-element.25), channel_id=1, source_target_pairs={{1,0},{0,1},{3,2},{2,3},{5,4},{4,5},{7,6},{6,7},{9,8},{8,9},{11,10... | collective-permute-start | bytes 1572872 | tf_op jit(solution)/shard_map/ppermute | solution.py:285
  132.7 52.2 %collective-permute-start.4 = (bf16[512,512]{1,0:T(8,128)(2,1)S(1)}, bf16[512,512]{1,0:T(8,128)(2,1)S(1)}, u32[]{:S(2)}, u32[]{:S(2)}) collective-permute-start(bf16[512,512]{1,0:T(8,128)(2,1)S(1)} %get-tuple-element.24), channel_id=1, source_target_pairs={{1,0},{0,1},{3,2},{2,3},{5,4},{4,5},{7,6},{6,7},{9,8},{8,9},{11,10... | collective-permute-start | bytes 1572872 | tf_op jit(solution)/shard_map/ppermute | solution.py:285
  190.5 23.1 %collective-permute-start.14 = (f32[1024]{0:T(1024)S(1)}, f32[1024]{0:T(1024)S(1)}, u32[]{:S(2)}, u32[]{:S(2)}) collective-permute-start(f32[1024]{0:T(1024)S(1)} %bitcast.26), channel_id=1, source_target_pairs={{126,0},{127,1},{0,2},{1,3},{2,4},{3,5},{4,6},{5,7},{6,8},{7,9},{8... | collective-permute-start | bytes 12296 | tf_op jit(solution)/shard_map/ppermute | solution.py:285
  190.6 23.0 %collective-permute-start.15 = (f32[1024]{0:T(1024)S(1)}, f32[1024]{0:T(1024)S(1)}, u32[]{:S(2)}, u32[]{:S(2)}) collective-permute-start(f32[1024]{0:T(1024)S(1)} %bitcast.27), channel_id=1, source_target_pairs={{127,0},{126,1},{1,2},{0,3},{3,4},{2,5},{5,6},{4,7},{7,8},{6,9},{9... | collective-permute-start | bytes 12296 | tf_op jit(solution)/shard_map/ppermute | solution.py:285
  203.9 9.7 %collective-permute-start.16 = (f32[1024]{0:T(1024)S(1)}, f32[1024]{0:T(1024)S(1)}, u32[]{:S(2)}, u32[]{:S(2)}) collective-permute-start(f32[1024]{0:T(1024)S(1)} %bitcast.24), channel_id=1, source_target_pairs={{124,0},{125,1},{126,2},{127,3},{0,4},{1,5},{2,6},{3,7},{4,8},{5,9... | collective-permute-start | bytes 12296 | tf_op jit(solution)/shard_map/ppermute | solution.py:285
  203.9 9.7 %collective-permute-start.17 = (f32[1024]{0:T(1024)S(1)}, f32[1024]{0:T(1024)S(1)}, u32[]{:S(2)}, u32[]{:S(2)}) collective-permute-start(f32[1024]{0:T(1024)S(1)} %bitcast.25), channel_id=1, source_target_pairs={{125,0},{124,1},{127,2},{126,3},{1,4},{0,5},{3,6},{2,7},{5,8},{4,9... | collective-permute-start | bytes 12296 | tf_op jit(solution)/shard_map/ppermute | solution.py:285
  208.5 5.1 %collective-permute-start.13 = (f32[1024]{0:T(1024)S(1)}, f32[1024]{0:T(1024)S(1)}, u32[]{:S(2)}, u32[]{:S(2)}) collective-permute-start(f32[1024]{0:T(1024)S(1)} %bitcast.22), channel_id=1, source_target_pairs={{1,0},{0,1},{3,2},{2,3},{5,4},{4,5},{7,6},{6,7},{9,8},{8,9},{11,10... | collective-permute-start | bytes 12296 | tf_op jit(solution)/shard_map/ppermute | solution.py:285
where the time goes:
time: 217 us; the launch traced here: 214 us
  Pallas kernels  86.4 us (40%)
  starting transfers between devices  58.4 us (27%)
  waiting for transfers between devices  55.2 us (25%)
  local copies, waits for them, and re-layouts  7.4 us (3%)
  other arithmetic  6.1 us (3%)
    ppermute x18, waiting for transfers between devices, fetch(): return lax.ppermute(x, both, route)  55.2 us
    ppermute x18, starting transfers between devices, fetch(): return lax.ppermute(x, both, route)  49 us
    pallas_call x6, Pallas kernels, update(): pl.pallas_call(functools.partial(update_kernel, blocks=blocks, slots=slot...  40.8 us
    pallas_call x5, Pallas kernels, search(): pl.pallas_call(functools.partial(search_kernel, first=before is None, las...  38.7 us
    all_to_all x1, starting transfers between devices, step(): got = lax.all_to_all(sent, 'blk', split_axis=0, concat_axis=0, tiled=True)  9.38 us
    pallas_call x1, Pallas kernels, pack(): pl.pallas_call(functools.partial(pack_kernel, slots=slots), out_shape=jax...  6.89 us
  transfers between devices with their start and end apart: 19, of which 7 were waited for; matrix products, arithmetic and copies ran while one was open for 5% of the time, Pallas kernels for 38%

commit v1 on v0

--- a/solution.py
+++ b/solution.py
@@ -13,8 +13,9 @@
 LANES = 128
 META = 8
 TILE = 256
-CHUNKS = (1024, 1024, 1024, 512, 512)
+CHUNKS = (512, 1024, 1024, 1024, 512)
 COLS = 512
+PACK_STEPS = 2
 BF16 = jnp.bfloat16
 F32 = jnp.float32
 I32 = jnp.int32
@@ -28,7 +29,7 @@
     count, width = pts_ref.shape
     tiles = width // LANES
     blocks = high_ref.shape[0]
-    group = TILE // slots
+    group = out_ref.shape[0]
     step = pl.program_id(0)
 
     @pl.when(step == 0)
@@ -60,19 +61,22 @@
     out_ref[:, slots * tiles :, :] = jnp.where(
         row == 0, high[:, None, :], jnp.where(row == 1, low[:, None, :], 0.0)
     ).astype(BF16)
-    pick = jnp.where(iota((TILE, count), 0) + step * TILE == slot_ref[...], 1.0, 0.0).astype(BF16)
-    placed = jnp.dot(pick, pts_ref[...], preferred_element_type=F32).astype(BF16)
-    for o in range(group):
-        for t in range(tiles):
-            out_ref[o, t * slots : (t + 1) * slots, :] = placed[
-                o * slots : (o + 1) * slots, t * LANES : (t + 1) * LANES
-            ]
+    part = TILE // slots
+    for p in range(group // part):
+        want = iota((TILE, count), 0) + (step * group + p * part) * slots
+        pick = jnp.where(want == slot_ref[...], 1.0, 0.0).astype(BF16)
+        placed = jnp.dot(pick, pts_ref[...], preferred_element_type=F32).astype(BF16)
+        for o in range(part):
+            for t in range(tiles):
+                out_ref[p * part + o, t * slots : (t + 1) * slots, :] = placed[
+                    o * slots : (o + 1) * slots, t * LANES : (t + 1) * LANES
+                ]
 
 
 def pack(lane, owner, member, points, blocks, slots):
     count, width = points.shape
     rows = slots * (width // LANES) + META
-    group = TILE // slots
+    group = blocks // PACK_STEPS
     whole = lambda i: (0, 0)
     return pl.pallas_call(
         functools.partial(pack_kernel, slots=slots),
@@ -277,9 +281,11 @@
     side = lax.axis_index("dim")
     ids = [(b, d) for b in range(blocks) for d in range(2)]
 
-    def fetch(x, source):
+    def fetch(x, source, odd=False):
         route = []
         for b, d in ids:
+            if odd and not b & 2:
+                continue
             sb, sd = source(b, d)
             route.append(((sb % blocks) * 2 + sd, b * 2 + d))
         return lax.ppermute(x, both, route)
@@ -296,9 +302,10 @@
     part = width // 2
     first_part = fetch(near_other[:part], lambda b, d: (b ^ 2, d))
     second_part = fetch(near_own[part:], lambda b, d: (b ^ 2, 1 - d))
-    onward = lambda b, d: (b + 4 if b & 2 else b, d)
-    own_2 = fetch(near_own, onward)
-    other_2 = fetch(near_other, onward)
+    far = lambda b, d: (b + 4, d)
+    odd = (mine // 2) % 2 == 1
+    own_2 = jnp.where(odd, fetch(near_own, far, odd=True), near_own)
+    other_2 = jnp.where(odd, fetch(near_other, far, odd=True), near_other)
     other_0 = jnp.concatenate([first_part, second_part], axis=0)
     even = mine % 2 == 0
     own_1 = fetch(jnp.where(even, own_2, own_0), lambda b, d: (b ^ 1, d))

time: 217 us -> 212 us (0.977)
  the two profiles are of different devices: /device:TPU:24 before, /device:TPU:8 now
where the time goes in v1:
time: 212 us; the launch traced here: 211 us
  Pallas kernels  81.7 us (39%)
  waiting for transfers between devices  57.4 us (27%)
  starting transfers between devices  56.7 us (27%)
  local copies, waits for them, and re-layouts  7.41 us (3%)
  other arithmetic  7.08 us (3%)
    ppermute x18, waiting for transfers between devices, fetch(): return lax.ppermute(x, both, route)  57.4 us
    ppermute x18, starting transfers between devices, fetch(): return lax.ppermute(x, both, route)  47.3 us
    pallas_call x6, Pallas kernels, update(): pl.pallas_call(functools.partial(update_kernel, blocks=blocks, slots=slot...  40.8 us
    pallas_call x5, Pallas kernels, search(): pl.pallas_call(functools.partial(search_kernel, first=before is None, las...  35.5 us
    all_to_all x1, starting transfers between devices, step(): got = lax.all_to_all(sent, 'blk', split_axis=0, concat_axis=0, tiled=True)  9.4 us
    pallas_call x1, Pallas kernels, pack(): pl.pallas_call(functools.partial(pack_kernel, slots=slots), out_shape=jax...  5.37 us
  transfers between devices with their start and end apart: 19, of which 8 were waited for; matrix products, arithmetic and copies ran while one was open for 6% of the time, Pallas kernels for 36%

profile of v1, /device:TPU:8, one launch (start us, length us, event | category | flops | bytes accessed | tf_op | source)
XLA Modules:
  0.0 211.1 jit_solution(13250767009444342562)
XLA Ops:
  0.6 1.5 copy.11
  2.1 4.1 %collective-permute-start = (bf16[1024,512]{0,1:T(8,128)(2,1)S(1)}, bf16[1024,512]{0,1:T(8,128)(2,1)}, u32[]{:S(2)}, u32[]{:S(2)}) collective-permute-start(bf16[1024,512]{0,1:T(8,128)(2,1)S(1)} %copy.11), channel_id=1, source_target_pairs={{5,0},{4,1},{7,2},{6,3},{1,4},{0,5},{3,6},{2,7},{13,8},{12,9},{15,... | collective-permute-start | bytes 3145736 | tf_op jit(solution)/shard_map/ppermute | solution.py:291
  6.2 5.4 %pack.1 = bf16[64,136,128]{2,1,0:T(8,128)(2,1)} custom-call(s32[1]{0:T(128)} %bitcast.1.lane_ref, s32[1,1024]{1,0:T(1,128)} %bitcast.32, s32[1,1024]{1,0:T(1,128)} %bitcast.33, bf16[1024,512]{1,0:T(8,128)(2,1)} %pts_ref.1), custom_call_target="tpu_custom_call" | custom-call | flops 2147483648 | bytes 6291456 | tf_op jit(solution)/shard_map/pack/pallas_call | solution.py:81
  11.6 9.4 %all-to-all-start = ((bf16[64,136,128]{2,1,0:T(8,128)(2,1)}), bf16[64,136,128]{2,1,0:T(8,128)(2,1)S(1)}, u32[]{:S(2)}, u32[]{:S(2)}) async-start(bf16[64,136,128]{2,1,0:T(8,128)(2,1)} %pack.1), calls=%async_computation | async-start | bytes 4456448 | tf_op jit(solution)/shard_map/all_to_all | solution.py:298
  21.0 8.5 %collective-permute-done = bf16[1024,512]{0,1:T(8,128)(2,1)} collective-permute-done((bf16[1024,512]{0,1:T(8,128)(2,1)S(1)}, bf16[1024,512]{0,1:T(8,128)(2,1)}, u32[]{:S(2)}, u32[]{:S(2)}) %collective-permute-start) | collective-permute-done | bytes 1048608 | tf_op jit(solution)/shard_map/ppermute | solution.py:291
  29.5 1.6 collective-permute-start.7
  31.1 1.9 slice.8
  33.0 2.7 %collective-permute-start.1 = (bf16[256,1024]{1,0:T(8,128)(2,1)}, bf16[256,1024]{1,0:T(8,128)(2,1)}, u32[]{:S(2)}, u32[]{:S(2)}) collective-permute-start(bf16[256,1024]{1,0:T(8,128)(2,1)} %slice.8), channel_id=1, source_target_pairs={{4,0},{5,1},{6,2},{7,3},{0,4},{1,5},{2,6},{3,7},{12,8},{13,9},{14,... | collective-permute-start | bytes 1572872 | tf_op jit(solution)/shard_map/ppermute | solution.py:291
  35.7 19.0 %collective-permute-done.2 = bf16[1024,512]{0,1:T(8,128)(2,1)} collective-permute-done((bf16[1024,512]{0,1:T(8,128)(2,1)S(1)}, bf16[1024,512]{0,1:T(8,128)(2,1)}, u32[]{:S(2)}, u32[]{:S(2)}) %collective-permute-start.2) | collective-permute-done | bytes 1048608 | tf_op jit(solution)/shard_map/ppermute | solution.py:291
  54.8 1.6 collective-permute-start.5
  56.4 1.9 slice.9
  58.2 3.0 %collective-permute-start.3 = (bf16[256,1024]{1,0:T(8,128)(2,1)}, bf16[256,1024]{1,0:T(8,128)(2,1)}, u32[]{:S(2)}, u32[]{:S(2)}) collective-permute-start(bf16[256,1024]{1,0:T(8,128)(2,1)} %slice.9), channel_id=1, source_target_pairs={{5,0},{4,1},{7,2},{6,3},{1,4},{0,5},{3,6},{2,7},{13,8},{12,9},{15,... | collective-permute-start | bytes 1572872 | tf_op jit(solution)/shard_map/ppermute | solution.py:291
  61.3 0.2 multiply_reduce_fusion.1
  61.5 4.5 %collective-permute-done.1 = bf16[256,1024]{1,0:T(8,128)(2,1)} collective-permute-done((bf16[256,1024]{1,0:T(8,128)(2,1)}, bf16[256,1024]{1,0:T(8,128)(2,1)}, u32[]{:S(2)}, u32[]{:S(2)}) %collective-permute-start.1) | collective-permute-done | bytes 524320 | tf_op jit(solution)/shard_map/ppermute | solution.py:291
  66.1 1.1 constant_dynamic-update-slice_fusion.1
  67.2 4.1 %collective-permute-done.3 = bf16[256,1024]{1,0:T(8,128)(2,1)} collective-permute-done((bf16[256,1024]{1,0:T(8,128)(2,1)}, bf16[256,1024]{1,0:T(8,128)(2,1)}, u32[]{:S(2)}, u32[]{:S(2)}) %collective-permute-start.3) | collective-permute-done | bytes 524320 | tf_op jit(solution)/shard_map/ppermute | solution.py:291
  71.3 1.1 constant_dynamic-update-slice_fusion.refs_1_
  72.4 3.2 %broadcast_select_fusion.2 = (bf16[512,1024]{1,0:T(8,128)(2,1)}, bf16[512,1024]{1,0:T(8,128)(2,1)}) fusion(bf16[512,1024]{1,0:T(8,128)(2,1)S(1)} %constant_dynamic-update-slice_fusion.refs_1_, pred[]{:T(512)S(6)} %eq.10, bf16[512,1024]{1,0:T(8,128)(2,1)} %collective-permute-done.7, bf16[1024,512]{0,1:T(8,128)(2,1)} %collective-permute-done, pred[]{:T(512)S(6)} %eq.11), kind=kLoop, calls=%fused_computation.4 | loop fusion | flops 1048576 | bytes 5242882 | tf_op jit(solution)/shard_map/jit(_where)/select_n | solution.py:312
  75.5 0.0 collective-permute-start.8
  75.5 0.0 collective-permute-done.5
  75.5 2.8 %broadcast_select_fusion.3 = (bf16[512,1024]{1,0:T(8,128)(2,1)}, bf16[512,1024]{1,0:T(8,128)(2,1)}) fusion(pred[]{:T(512)S(6)} %eq.10, bf16[1024,512]{0,1:T(8,128)(2,1)S(1)} %copy.11, bf16[512,1024]{1,0:T(8,128)(2,1)} %collective-permute-done.5, bf16[1024,512]{0,1:T(8,128)(2,1)} %collective-permute-done.2, pred[]{:T(512)S(6)} %eq.11), kind=kLoop, calls=%fused_computation.5 | loop fusion | flops 1048576 | bytes 5242882 | tf_op jit(solution)/shard_map/jit(_where)/select_n | solution.py:311
  78.4 0.5 collective-permute-start.6
  78.9 3.7 %update.6 = (bf16[8192,512]{1,0:T(8,128)(2,1)}, bf16[512,512]{1,0:T(8,128)(2,1)S(1)}) custom-call(s32[1]{0:T(128)} %bitcast.8.first_ref, bf16[64,136,128]{2,1,0:T(8,128)(2,1)S(1)} %all-to-all-done.got_ref, bf16[8192,512]{1,0:T(8,128)(2,1)} %old_ref.11), custom_call_target="tpu_custom_call" | custom-call | flops 1073741824 | bytes 3801088 | tf_op jit(solution)/shard_map/update/pallas_call | solution.py:158
  82.6 2.0 collective-permute-start.12
  84.6 5.5 %update.7 = (bf16[8192,512]{1,0:T(8,128)(2,1)}, bf16[1024,512]{1,0:T(8,128)(2,1)S(1)}) custom-call(s32[1]{0:T(128)} %bitcast.7.first_ref, bf16[64,136,128]{2,1,0:T(8,128)(2,1)S(1)} %all-to-all-done.got_ref, bf16[8192,512]{1,0:T(8,128)(2,1)} %old_ref.11, bf16[8192,512]{1,0:T(8,128)(2,1)} %get-tuple-element.17.refs_0_), custom_call_target="tpu_custom_call", output_to_operand_aliasing={{0}: (3, {})} | custom-call | flops 2147483648 | bytes 5373952 | tf_op jit(solution)/shard_map/update/pallas_call | solution.py:158
  90.1 1.6 collective-permute-start.11
  91.6 5.5 %update.8 = (bf16[8192,512]{1,0:T(8,128)(2,1)}, bf16[1024,512]{1,0:T(8,128)(2,1)S(1)}) custom-call(s32[1]{0:T(128)} %bitcast.6.first_ref, bf16[64,136,128]{2,1,0:T(8,128)(2,1)S(1)} %all-to-all-done.got_ref, bf16[8192,512]{1,0:T(8,128)(2,1)} %old_ref.11, bf16[8192,512]{1,0:T(8,128)(2,1)} %get-tuple-element.18.refs_0_), custom_call_target="tpu_custom_call", output_to_operand_aliasing={{0}: (3, {})} | custom-call | flops 2147483648 | bytes 5373952 | tf_op jit(solution)/shard_map/update/pallas_call | solution.py:158
  97.2 2.0 collective-permute-start.10
  99.2 5.5 %update.9 = (bf16[8192,512]{1,0:T(8,128)(2,1)}, bf16[1024,512]{1,0:T(8,128)(2,1)S(1)}) custom-call(s32[1]{0:T(128)} %bitcast.5.first_ref, bf16[64,136,128]{2,1,0:T(8,128)(2,1)S(1)} %all-to-all-done.got_ref, bf16[8192,512]{1,0:T(8,128)(2,1)} %old_ref.11, bf16[8192,512]{1,0:T(8,128)(2,1)} %get-tuple-element.19.refs_0_), custom_call_target="tpu_custom_call", output_to_operand_aliasing={{0}: (3, {})} | custom-call | flops 2147483648 | bytes 5373952 | tf_op jit(solution)/shard_map/update/pallas_call | solution.py:158
  104.7 3.7 %update.10 = (bf16[8192,512]{1,0:T(8,128)(2,1)}, bf16[512,512]{1,0:T(8,128)(2,1)S(1)}) custom-call(s32[1]{0:T(128)} %bitcast.4.first_ref, bf16[64,136,128]{2,1,0:T(8,128)(2,1)S(1)} %all-to-all-done.got_ref, bf16[8192,512]{1,0:T(8,128)(2,1)} %old_ref.11, bf16[8192,512]{1,0:T(8,128)(2,1)} %get-tuple-element.20.refs_0_), custom_call_target="tpu_custom_call", output_to_operand_aliasing={{0}: (3, {})} | custom-call | flops 1073741824 | bytes 3801088 | tf_op jit(solution)/shard_map/update/pallas_call | solution.py:158
  108.4 16.8 %update.11 = (bf16[8192,512]{1,0:T(8,128)(2,1)}, bf16[4096,512]{1,0:T(8,128)(2,1)S(1)}) custom-call(s32[1]{0:T(128)} %bitcast.first_ref, bf16[64,136,128]{2,1,0:T(8,128)(2,1)S(1)} %all-to-all-done.got_ref, bf16[8192,512]{1,0:T(8,128)(2,1)} %old_ref.11, bf16[8192,512]{1,0:T(8,128)(2,1)} %get-tuple-element.21.refs_0_), custom_call_target="tpu_custom_call", output_to_operand_aliasing={{0}: (3, {})} | custom-call | flops 8589934592 | bytes 14811136 | tf_op jit(solution)/shard_map/update/pallas_call | solution.py:158
  125.2 1.6 collective-permute-start.9
  126.8 1.9 collective-permute-start.4
  128.8 5.0 %search.5.refs_6_ = f32[8,3072]{1,0:T(8,128)S(1)} custom-call(bf16[4096,512]{1,0:T(8,128)(2,1)S(1)} %get-tuple-element.23.own_ref, bf16[512,512]{1,0:T(8,128)(2,1)S(1)} %collective-permute-done.12.other_ref, bf16[512,1024]{1,0:T(8,128)(2,1)S(1)} %bitcast.21, bf16[512,1024]{1,0:T(8,128)(2,1)S(1)} %copy-done.1, ...), custom_call_target="tpu_custom_call" | custom-call | flops 3221225472 | bytes 7340032 | tf_op jit(solution)/shard_map/search/pallas_call | solution.py:255
  133.8 8.7 %search.6.refs_6_ = f32[8,3072]{1,0:T(8,128)S(1)} custom-call(bf16[4096,512]{1,0:T(8,128)(2,1)S(1)} %get-tuple-element.23.own_ref, bf16[1024,512]{1,0:T(8,128)(2,1)S(1)} %collective-permute-done.11.other_ref, bf16[512,1024]{1,0:T(8,128)(2,1)S(1)} %bitcast.22, bf16[512,1024]{1,0:T(8,128)(2,1)S(1)} %copy-done.1, ...), custom_call_target="tpu_custom_call" | custom-call | flops 6442450944 | bytes 8388608 | tf_op jit(solution)/shard_map/search/pallas_call | solution.py:255
  142.5 1.4 collective-permute-done.10.other_ref
  143.8 8.4 %search.7.refs_6_ = f32[8,3072]{1,0:T(8,128)S(1)} custom-call(bf16[4096,512]{1,0:T(8,128)(2,1)S(1)} %get-tuple-element.23.own_ref, bf16[1024,512]{1,0:T(8,128)(2,1)S(1)} %collective-permute-done.10.other_ref, bf16[512,1024]{1,0:T(8,128)(2,1)S(1)} %bitcast.23, bf16[512,1024]{1,0:T(8,128)(2,1)S(1)} %copy-done.1, ...), custom_call_target="tpu_custom_call" | custom-call | flops 6442450944 | bytes 8388608 | tf_op jit(solution)/shard_map/search/pallas_call | solution.py:255
  152.3 14.0 %collective-permute-done.9.other_ref = bf16[1024,512]{1,0:T(8,128)(2,1)S(1)} collective-permute-done((bf16[1024,512]{1,0:T(8,128)(2,1)S(1)}, bf16[1024,512]{1,0:T(8,128)(2,1)S(1)}, u32[]{:S(2)}, u32[]{:S(2)}) %collective-permute-start.9) | collective-permute-done | bytes 1048608 | tf_op jit(solution)/shard_map/ppermute | solution.py:291
  166.3 8.4 %search.8.refs_6_ = f32[8,3072]{1,0:T(8,128)S(1)} custom-call(bf16[4096,512]{1,0:T(8,128)(2,1)S(1)} %get-tuple-element.23.own_ref, bf16[1024,512]{1,0:T(8,128)(2,1)S(1)} %collective-permute-done.9.other_ref, bf16[512,1024]{1,0:T(8,128)(2,1)S(1)} %bitcast.24, bf16[512,1024]{1,0:T(8,128)(2,1)S(1)} %copy-done.1, ...), custom_call_target="tpu_custom_call" | custom-call | flops 6442450944 | bytes 8388608 | tf_op jit(solution)/shard_map/search/pallas_call | solution.py:255
  174.7 1.8 collective-permute-done.4.other_ref
  176.6 5.0 %search.9 = (f32[1,1024]{1,0:T(1,128)S(1)}, f32[1,1024]{1,0:T(1,128)S(1)}, f32[1,1024]{1,0:T(1,128)S(1)}) custom-call(bf16[4096,512]{1,0:T(8,128)(2,1)S(1)} %get-tuple-element.23.own_ref, bf16[512,512]{1,0:T(8,128)(2,1)S(1)} %collective-permute-done.4.other_ref, bf16[512,1024]{1,0:T(8,128)(2,1)S(1)} %bitcast.25, bf16[512,1024]{1,0:T(8,128)(2,1)S(1)} %copy-done.1, ...), custom_call_target="tpu_custom_call" | custom-call | flops 3221225472 | bytes 7340032 | tf_op jit(solution)/shard_map/search/pallas_call | solution.py:255
  181.6 0.1 collective-permute-start.14
  181.6 19.1 %collective-permute-start.15 = (f32[1024]{0:T(1024)S(1)}, f32[1024]{0:T(1024)S(1)}, u32[]{:S(2)}, u32[]{:S(2)}) collective-permute-start(f32[1024]{0:T(1024)S(1)} %bitcast.31), channel_id=1, source_target_pairs={{127,0},{126,1},{1,2},{0,3},{3,4},{2,5},{5,6},{4,7},{7,8},{6,9},{9... | collective-permute-start | bytes 12296 | tf_op jit(solution)/shard_map/ppermute | solution.py:291
  200.7 4.6 %collective-permute-start.17 = (f32[1024]{0:T(1024)S(1)}, f32[1024]{0:T(1024)S(1)}, u32[]{:S(2)}, u32[]{:S(2)}) collective-permute-start(f32[1024]{0:T(1024)S(1)} %bitcast.29), channel_id=1, source_target_pairs={{125,0},{124,1},{127,2},{126,3},{1,4},{0,5},{3,6},{2,7},{5,8},{4,9... | collective-permute-start | bytes 12296 | tf_op jit(solution)/shard_map/ppermute | solution.py:291
  205.3 0.9 collective-permute-start.13
  206.2 0.2 multiply_reduce_fusion
  206.5 4.0 %collective-permute-done.13 = f32[1024]{0:T(1024)S(1)} collective-permute-done((f32[1024]{0:T(1024)S(1)}, f32[1024]{0:T(1024)S(1)}, u32[]{:S(2)}, u32[]{:S(2)}) %collective-permute-start.13) | collective-permute-done | bytes 4128 | tf_op jit(solution)/shard_map/ppermute | solution.py:291
  210.5 0.6 subtract_multiply_fusion
  (20 shorter events, 0.0 us)
Async XLA Ops:
  2.1 27.4 %collective-permute-start = (bf16[1024,512]{0,1:T(8,128)(2,1)S(1)}, bf16[1024,512]{0,1:T(8,128)(2,1)}, u32[]{:S(2)}, u32[]{:S(2)}) collective-permute-start(bf16[1024,512]{0,1:T(8,128)(2,1)S(1)} %copy.11), channel_id=1, source_target_pairs={{5,0},{4,1},{7,2},{6,3},{1,4},{0,5},{3,6},{2,7},{13,8},{12,9},{15,... | collective-permute-start | bytes 3145736 | tf_op jit(solution)/shard_map/ppermute | solution.py:291
  6.2 48.5 %collective-permute-start.2 = (bf16[1024,512]{0,1:T(8,128)(2,1)S(1)}, bf16[1024,512]{0,1:T(8,128)(2,1)}, u32[]{:S(2)}, u32[]{:S(2)}) collective-permute-start(bf16[1024,512]{0,1:T(8,128)(2,1)S(1)} %copy.11), channel_id=1, source_target_pairs={{4,0},{5,1},{6,2},{7,3},{0,4},{1,5},{2,6},{3,7},{12,8},{13,9},{14,... | collective-permute-start | bytes 3145736 | tf_op jit(solution)/shard_map/ppermute | solution.py:291
  11.6 67.2 %all-to-all-start = ((bf16[64,136,128]{2,1,0:T(8,128)(2,1)}), bf16[64,136,128]{2,1,0:T(8,128)(2,1)S(1)}, u32[]{:S(2)}, u32[]{:S(2)}) async-start(bf16[64,136,128]{2,1,0:T(8,128)(2,1)} %pack.1), calls=%async_computation | async-start | bytes 4456448 | tf_op jit(solution)/shard_map/all_to_all | solution.py:298
  29.5 42.8 %collective-permute-start.7 = (bf16[512,1024]{1,0:T(8,128)(2,1)}, bf16[512,1024]{1,0:T(8,128)(2,1)}, u32[]{:S(2)}, u32[]{:S(2)}) collective-permute-start(bf16[512,1024]{1,0:T(8,128)(2,1)} %bitcast.10), channel_id=1, source_target_pairs={{12,4},{13,5},{14,6},{15,7},{20,12},{21,13},{22,14},{23,15},{28,20... | collective-permute-start | bytes 3145736 | tf_op jit(solution)/shard_map/ppermute | solution.py:291
  33.0 33.1 %collective-permute-start.1 = (bf16[256,1024]{1,0:T(8,128)(2,1)}, bf16[256,1024]{1,0:T(8,128)(2,1)}, u32[]{:S(2)}, u32[]{:S(2)}) collective-permute-start(bf16[256,1024]{1,0:T(8,128)(2,1)} %slice.8), channel_id=1, source_target_pairs={{4,0},{5,1},{6,2},{7,3},{0,4},{1,5},{2,6},{3,7},{12,8},{13,9},{14,... | collective-permute-start | bytes 1572872 | tf_op jit(solution)/shard_map/ppermute | solution.py:291
  54.8 20.8 %collective-permute-start.5 = (bf16[512,1024]{1,0:T(8,128)(2,1)}, bf16[512,1024]{1,0:T(8,128)(2,1)}, u32[]{:S(2)}, u32[]{:S(2)}) collective-permute-start(bf16[512,1024]{1,0:T(8,128)(2,1)} %bitcast.11), channel_id=1, source_target_pairs={{12,4},{13,5},{14,6},{15,7},{20,12},{21,13},{22,14},{23,15},{28,20... | collective-permute-start | bytes 3145736 | tf_op jit(solution)/shard_map/ppermute | solution.py:291
  58.2 13.0 %collective-permute-start.3 = (bf16[256,1024]{1,0:T(8,128)(2,1)}, bf16[256,1024]{1,0:T(8,128)(2,1)}, u32[]{:S(2)}, u32[]{:S(2)}) collective-permute-start(bf16[256,1024]{1,0:T(8,128)(2,1)} %slice.9), channel_id=1, source_target_pairs={{5,0},{4,1},{7,2},{6,3},{1,4},{0,5},{3,6},{2,7},{13,8},{12,9},{15,... | collective-permute-start | bytes 1572872 | tf_op jit(solution)/shard_map/ppermute | solution.py:291
  72.3 6.0 %copy-start = (bf16[512,1024]{1,0:T(8,128)(2,1)}, bf16[512,1024]{1,0:T(8,128)(2,1)S(1)}, u32[]{:S(2)}) copy-start(bf16[512,1024]{1,0:T(8,128)(2,1)S(1)} %constant_dynamic-update-slice_fusion.refs_1_) | copy-start | bytes 3145732
  75.5 51.3 %collective-permute-start.8 = (bf16[512,1024]{1,0:T(8,128)(2,1)}, bf16[512,1024]{1,0:T(8,128)(2,1)}, u32[]{:S(2)}, u32[]{:S(2)}) collective-permute-start(bf16[512,1024]{1,0:T(8,128)(2,1)} %get-tuple-element.32), channel_id=1, source_target_pairs={{2,0},{3,1},{0,2},{1,3},{6,4},{7,5},{4,6},{5,7},{10,8},{11,9},{8,1... | collective-permute-start | bytes 3145736 | tf_op jit(solution)/shard_map/ppermute | solution.py:291
  78.4 50.4 %collective-permute-start.6 = (bf16[512,1024]{1,0:T(8,128)(2,1)}, bf16[512,1024]{1,0:T(8,128)(2,1)}, u32[]{:S(2)}, u32[]{:S(2)}) collective-permute-start(bf16[512,1024]{1,0:T(8,128)(2,1)} %get-tuple-element.34), channel_id=1, source_target_pairs={{2,0},{3,1},{0,2},{1,3},{6,4},{7,5},{4,6},{5,7},{10,8},{11,9},{8,1... | collective-permute-start | bytes 3145736 | tf_op jit(solution)/shard_map/ppermute | solution.py:291
  82.6 42.6 %collective-permute-start.12 = (bf16[512,512]{1,0:T(8,128)(2,1)S(1)}, bf16[512,512]{1,0:T(8,128)(2,1)S(1)}, u32[]{:S(2)}, u32[]{:S(2)}) collective-permute-start(bf16[512,512]{1,0:T(8,128)(2,1)S(1)} %get-tuple-element.28), channel_id=1, source_target_pairs={{1,0},{0,1},{3,2},{2,3},{5,4},{4,5},{7,6},{6,7},{9,8},{8,9},{11,10... | collective-permute-start | bytes 1572872 | tf_op jit(solution)/shard_map/ppermute | solution.py:291
  90.1 43.7 %collective-permute-start.11 = (bf16[1024,512]{1,0:T(8,128)(2,1)S(1)}, bf16[1024,512]{1,0:T(8,128)(2,1)S(1)}, u32[]{:S(2)}, u32[]{:S(2)}) collective-permute-start(bf16[1024,512]{1,0:T(8,128)(2,1)S(1)} %get-tuple-element.27), channel_id=1, source_target_pairs={{1,0},{0,1},{3,2},{2,3},{5,4},{4,5},{7,6},{6,7},{9,8},{8,9},{11,10... | collective-permute-start | bytes 3145736 | tf_op jit(solution)/shard_map/ppermute | solution.py:291
  97.2 46.6 %collective-permute-start.10 = (bf16[1024,512]{1,0:T(8,128)(2,1)S(1)}, bf16[1024,512]{1,0:T(8,128)(2,1)S(1)}, u32[]{:S(2)}, u32[]{:S(2)}) collective-permute-start(bf16[1024,512]{1,0:T(8,128)(2,1)S(1)} %get-tuple-element.26), channel_id=1, source_target_pairs={{1,0},{0,1},{3,2},{2,3},{5,4},{4,5},{7,6},{6,7},{9,8},{8,9},{11,10... | collective-permute-start | bytes 3145736 | tf_op jit(solution)/shard_map/ppermute | solution.py:291
  108.4 20.3 %copy-start.1 = (bf16[512,1024]{1,0:T(8,128)(2,1)S(1)}, bf16[512,1024]{1,0:T(8,128)(2,1)}, u32[]{:S(2)}) copy-start(bf16[512,1024]{1,0:T(8,128)(2,1)} %copy-done) | copy-start | bytes 3145732
  108.4 20.3 %copy-start.2 = (bf16[512,1024]{1,0:T(8,128)(2,1)S(1)}, bf16[512,1024]{1,0:T(8,128)(2,1)}, u32[]{:S(2)}) copy-start(bf16[512,1024]{1,0:T(8,128)(2,1)} %get-tuple-element.33.refs_5_) | copy-start | bytes 3145732
  108.4 20.3 %copy-start.3 = (bf16[512,1024]{1,0:T(8,128)(2,1)S(1)}, bf16[512,1024]{1,0:T(8,128)(2,1)}, u32[]{:S(2)}) copy-start(bf16[512,1024]{1,0:T(8,128)(2,1)} %get-tuple-element.35.refs_4_) | copy-start | bytes 3145732
  125.2 41.1 %collective-permute-start.9 = (bf16[1024,512]{1,0:T(8,128)(2,1)S(1)}, bf16[1024,512]{1,0:T(8,128)(2,1)S(1)}, u32[]{:S(2)}, u32[]{:S(2)}) collective-permute-start(bf16[1024,512]{1,0:T(8,128)(2,1)S(1)} %get-tuple-element.25), channel_id=1, source_target_pairs={{1,0},{0,1},{3,2},{2,3},{5,4},{4,5},{7,6},{6,7},{9,8},{8,9},{11,10... | collective-permute-start | bytes 3145736 | tf_op jit(solution)/shard_map/ppermute | solution.py:291
  126.8 49.8 %collective-permute-start.4 = (bf16[512,512]{1,0:T(8,128)(2,1)S(1)}, bf16[512,512]{1,0:T(8,128)(2,1)S(1)}, u32[]{:S(2)}, u32[]{:S(2)}) collective-permute-start(bf16[512,512]{1,0:T(8,128)(2,1)S(1)} %get-tuple-element.24), channel_id=1, source_target_pairs={{1,0},{0,1},{3,2},{2,3},{5,4},{4,5},{7,6},{6,7},{9,8},{8,9},{11,10... | collective-permute-start | bytes 1572872 | tf_op jit(solution)/shard_map/ppermute | solution.py:291
  181.6 28.9 %collective-permute-start.14 = (f32[1024]{0:T(1024)S(1)}, f32[1024]{0:T(1024)S(1)}, u32[]{:S(2)}, u32[]{:S(2)}) collective-permute-start(f32[1024]{0:T(1024)S(1)} %bitcast.30), channel_id=1, source_target_pairs={{126,0},{127,1},{0,2},{1,3},{2,4},{3,5},{4,6},{5,7},{6,8},{7,9},{8... | collective-permute-start | bytes 12296 | tf_op jit(solution)/shard_map/ppermute | solution.py:291
  181.6 28.8 %collective-permute-start.15 = (f32[1024]{0:T(1024)S(1)}, f32[1024]{0:T(1024)S(1)}, u32[]{:S(2)}, u32[]{:S(2)}) collective-permute-start(f32[1024]{0:T(1024)S(1)} %bitcast.31), channel_id=1, source_target_pairs={{127,0},{126,1},{1,2},{0,3},{3,4},{2,5},{5,6},{4,7},{7,8},{6,9},{9... | collective-permute-start | bytes 12296 | tf_op jit(solution)/shard_map/ppermute | solution.py:291
  200.7 9.7 %collective-permute-start.16 = (f32[1024]{0:T(1024)S(1)}, f32[1024]{0:T(1024)S(1)}, u32[]{:S(2)}, u32[]{:S(2)}) collective-permute-start(f32[1024]{0:T(1024)S(1)} %bitcast.28), channel_id=1, source_target_pairs={{124,0},{125,1},{126,2},{127,3},{0,4},{1,5},{2,6},{3,7},{4,8},{5,9... | collective-permute-start | bytes 12296 | tf_op jit(solution)/shard_map/ppermute | solution.py:291
  200.7 9.7 %collective-permute-start.17 = (f32[1024]{0:T(1024)S(1)}, f32[1024]{0:T(1024)S(1)}, u32[]{:S(2)}, u32[]{:S(2)}) collective-permute-start(f32[1024]{0:T(1024)S(1)} %bitcast.29), channel_id=1, source_target_pairs={{125,0},{124,1},{127,2},{126,3},{1,4},{0,5},{3,6},{2,7},{5,8},{4,9... | collective-permute-start | bytes 12296 | tf_op jit(solution)/shard_map/ppermute | solution.py:291
  205.3 5.1 %collective-permute-start.13 = (f32[1024]{0:T(1024)S(1)}, f32[1024]{0:T(1024)S(1)}, u32[]{:S(2)}, u32[]{:S(2)}) collective-permute-start(f32[1024]{0:T(1024)S(1)} %bitcast.26), channel_id=1, source_target_pairs={{1,0},{0,1},{3,2},{2,3},{5,4},{4,5},{7,6},{6,7},{9,8},{8,9},{11,10... | collective-permute-start | bytes 12296 | tf_op jit(solution)/shard_map/ppermute | solution.py:291

commit v2 on v1

--- a/solution.py
+++ b/solution.py
@@ -13,7 +13,7 @@
 LANES = 128
 META = 8
 TILE = 256
-CHUNKS = (512, 1024, 1024, 1024, 512)
+CHUNKS = (512, 1024, 1024, 512, 512, 256, 256)
 COLS = 512
 PACK_STEPS = 2
 BF16 = jnp.bfloat16
@@ -25,23 +25,35 @@
     return lax.broadcasted_iota(I32, shape, dim)
 
 
-def pack_kernel(lane_ref, owner_ref, member_ref, pts_ref, out_ref, slot_ref, high_ref, low_ref, *, slots):
+def pack_kernel(
+    lane_ref, plane_ref, block_ref, member_ref, pts_ref, out_ref, slot_ref, high_ref, low_ref, *, slots
+):
     count, width = pts_ref.shape
     tiles = width // LANES
-    blocks = high_ref.shape[0]
+    owners = high_ref.shape[0]
     group = out_ref.shape[0]
     step = pl.program_id(0)
 
     @pl.when(step == 0)
     def _():
-        owner = owner_ref[...]
-        is_owner = owner == iota((blocks, count), 0)
-        weights = jnp.where(is_owner, 1.0, 0.0).astype(BF16)
-        before = jnp.where(iota((count, count), 0) < iota((count, count), 1), 1.0, 0.0)
-        earlier = jnp.dot(weights, before.astype(BF16), preferred_element_type=F32)
+        block = block_ref[...]
+        member = member_ref[...]
+        here = ((block >> 1) & 1) == plane_ref[0]
+        owner = jnp.where(here, (block >> 2) * 2 + (block & 1), -1)
+        is_owner = owner == iota((owners, count), 0)
+        weights = jnp.where(is_owner, 1.0, 0.0)
+        before = jnp.where(iota((LANES, LANES), 0) < iota((LANES, LANES), 1), 1.0, 0.0).astype(BF16)
+        earlier = []
+        base = jnp.zeros((owners, 1), F32)
+        for c in range(0, count, LANES):
+            strip = weights[:, c : c + LANES]
+            earlier.append(
+                base + jnp.dot(strip.astype(BF16), before, preferred_element_type=F32)
+            )
+            base = base + jnp.sum(strip, axis=1, keepdims=True)
+        earlier = jnp.concatenate(earlier, axis=1)
         place = jnp.sum(jnp.where(is_owner, earlier, 0.0), axis=0, keepdims=True).astype(I32)
-        slot_ref[...] = owner * slots + place
-        member = member_ref[...]
+        slot_ref[...] = jnp.where(here, owner * slots + place, -1)
         lane = jnp.where(iota((LANES, count), 0) == place + lane_ref[0], 1.0, 0.0).astype(BF16)
 
         def spread(row):
@@ -73,16 +85,17 @@
                 ]
 
 
-def pack(lane, owner, member, points, blocks, slots):
+def pack(lane, plane, block, member, points, owners, slots):
     count, width = points.shape
     rows = slots * (width // LANES) + META
-    group = blocks // PACK_STEPS
+    group = owners // PACK_STEPS
     whole = lambda i: (0, 0)
     return pl.pallas_call(
         functools.partial(pack_kernel, slots=slots),
-        out_shape=jax.ShapeDtypeStruct((blocks, rows, LANES), BF16),
-        grid=(blocks // group,),
+        out_shape=jax.ShapeDtypeStruct((owners, rows, LANES), BF16),
+        grid=(PACK_STEPS,),
         in_specs=[
+            pl.BlockSpec(memory_space=pltpu.SMEM),
             pl.BlockSpec(memory_space=pltpu.SMEM),
             pl.BlockSpec((1, count), whole),
             pl.BlockSpec((1, count), whole),
@@ -91,48 +104,53 @@
         out_specs=pl.BlockSpec((group, rows, LANES), lambda i: (i, 0, 0)),
         scratch_shapes=[
             pltpu.VMEM((1, count), I32),
-            pltpu.VMEM((blocks, LANES), F32),
-            pltpu.VMEM((blocks, LANES), F32),
+            pltpu.VMEM((owners, LANES), F32),
+            pltpu.VMEM((owners, LANES), F32),
         ],
         compiler_params=pltpu.CompilerParams(
             dimension_semantics=("arbitrary",), vmem_limit_bytes=60 << 20
         ),
         cost_estimate=pl.CostEstimate(
-            flops=2 * blocks * slots * count * width, bytes_accessed=6 << 20, transcendentals=0
+            flops=2 * owners * slots * count * width, bytes_accessed=4 << 20, transcendentals=0
         ),
         name="pack",
-    )(lane, owner, member, points)
-
-
-def update_kernel(first_ref, got_ref, old_ref, *refs, blocks, slots, chained):
+    )(lane, plane, block, member, points)
+
+
+def update_kernel(first_ref, got_a_ref, got_b_ref, old_ref, *refs, owners, slots, chained):
     if chained:
         refs = refs[1:]
     out_ref, part_ref, rows_ref, list_ref = refs
     step = pl.program_id(0)
-    width = old_ref.shape[1]
+    size, width = old_ref.shape
     tiles = width // LANES
     share = LANES // slots
-    strips = blocks // share
+    strips = owners // share
 
     @pl.when(step == 0)
     def _():
-        for o in range(blocks):
-            for t in range(tiles):
-                rows_ref[o * slots : (o + 1) * slots, t * LANES : (t + 1) * LANES] = got_ref[
-                    o, t * slots : (t + 1) * slots, :
-                ]
-        meta = got_ref[:, slots * tiles :, :].astype(F32)
-        row = iota(meta.shape, 1)
-        number = jnp.sum(
-            jnp.where(row == 0, meta * 64.0, jnp.where(row == 1, meta, 0.0)), axis=1
-        )
-        number = jnp.sum(number.reshape(strips, share, LANES), axis=1)
-        list_ref[...] = number.astype(I32) - 64
-
-    want = iota((TILE, LANES), 0) + (first_ref[0] + step) * TILE
+        for n, got_ref in enumerate((got_a_ref, got_b_ref)):
+
+            @pl.loop(0, owners, unroll=4)
+            def _(o, n=n, got_ref=got_ref):
+                at = pl.ds(pl.multiple_of((n * owners + o) * slots, slots), slots)
+                for t in range(tiles):
+                    rows_ref[at, t * LANES : (t + 1) * LANES] = got_ref[
+                        o, t * slots : (t + 1) * slots, :
+                    ]
+
+            meta = got_ref[:, slots * tiles :, :].astype(F32)
+            row = iota(meta.shape, 1)
+            number = jnp.sum(
+                jnp.where(row == 0, meta * 64.0, jnp.where(row == 1, meta, 0.0)), axis=1
+            )
+            number = jnp.sum(number.reshape(strips, share, LANES), axis=1)
+            list_ref[n * strips : (n + 1) * strips, :] = number.astype(I32) - 64
+
+    want = iota((size, LANES), 0) + (first_ref[0] + step) * size
     picks = []
-    total = jnp.zeros((TILE, LANES), F32)
-    for g in range(strips):
+    total = jnp.zeros((size, LANES), F32)
+    for g in range(2 * strips):
         hit = jnp.where(list_ref[g : g + 1, :] == want, 1.0, 0.0)
         total = total + hit
         picks.append(hit.astype(BF16))
@@ -143,48 +161,78 @@
     part_ref[...] = new
 
 
-def update(first, got, centroids, so_far, count, blocks, slots):
+def update(first, got, centroids, so_far, count, slots, size=TILE):
     lists, width = centroids.shape
+    owners = got[0].shape[0]
     tile = lambda i, first: (first[0] + i, 0)
     chained = so_far is not None
     in_specs = [
-        pl.BlockSpec(got.shape, lambda i, first: (0, 0, 0), pipeline_mode=pl.Buffered(1)),
-        pl.BlockSpec((TILE, width), tile),
+        pl.BlockSpec(x.shape, lambda i, first: (0, 0, 0), pipeline_mode=pl.Buffered(1)) for x in got
     ]
-    args = [first, got, centroids]
+    in_specs.append(pl.BlockSpec((size, width), tile))
+    args = [first, *got, centroids]
     if chained:
         in_specs.append(pl.BlockSpec(memory_space=pl.ANY))
         args.append(so_far)
     return pl.pallas_call(
-        functools.partial(update_kernel, blocks=blocks, slots=slots, chained=chained),
+        functools.partial(update_kernel, owners=owners, slots=slots, chained=chained),
         out_shape=(
             jax.ShapeDtypeStruct((lists, width), BF16),
             jax.ShapeDtypeStruct((count, width), BF16),
         ),
         grid_spec=pltpu.PrefetchScalarGridSpec(
             num_scalar_prefetch=1,
-            grid=(count // TILE,),
+            grid=(count // size,),
             in_specs=in_specs,
             out_specs=(
-                pl.BlockSpec((TILE, width), tile),
-                pl.BlockSpec((TILE, width), lambda i, first: (i, 0)),
+                pl.BlockSpec((size, width), tile),
+                pl.BlockSpec((size, width), lambda i, first: (i, 0)),
             ),
             scratch_shapes=[
-                pltpu.VMEM((blocks * slots, width), BF16),
-                pltpu.VMEM((blocks * slots // LANES, LANES), I32),
+                pltpu.VMEM((2 * owners * slots, width), BF16),
+                pltpu.VMEM((2 * owners * slots // LANES, LANES), I32),
             ],
         ),
-        input_output_aliases={3: 0} if chained else {},
+        input_output_aliases={4: 0} if chained else {},
         compiler_params=pltpu.CompilerParams(
             dimension_semantics=("arbitrary",), vmem_limit_bytes=24 << 20
         ),
         cost_estimate=pl.CostEstimate(
-            flops=2 * count * blocks * slots * width,
-            bytes_accessed=got.size * 2 + count * width * 6,
+            flops=4 * count * owners * slots * width,
+            bytes_accessed=got[0].size * 4 + count * width * 6,
             transcendentals=0,
         ),
         name="update",
     )(*args)
+
+
+def turn_kernel(*refs):
+    out_ref = refs[-1]
+    at = 0
+    for ref in refs[:-1]:
+        rows = ref.shape[0]
+        out_ref[:, at : at + rows] = ref[...].T
+        at += rows
+
+
+def turn(*parts):
+    width = parts[0].shape[1]
+    half = width // 2
+    count = sum(x.shape[0] for x in parts)
+    return pl.pallas_call(
+        turn_kernel,
+        out_shape=jax.ShapeDtypeStruct((width, count), BF16),
+        grid=(2,),
+        in_specs=[pl.BlockSpec((x.shape[0], half), lambda i: (0, i)) for x in parts],
+        out_specs=pl.BlockSpec((half, count), lambda i: (i, 0)),
+        compiler_params=pltpu.CompilerParams(
+            dimension_semantics=("arbitrary",), vmem_limit_bytes=24 << 20
+        ),
+        cost_estimate=pl.CostEstimate(
+            flops=0, bytes_accessed=4 * width * count, transcendentals=0
+        ),
+        name="turn",
+    )(*parts)
 
 
 def search_kernel(own_ref, other_ref, *refs, first, last):
@@ -232,7 +280,7 @@
     chunk, width = other.shape
     sections = CYCLE + 1
     count = points[0].shape[1]
-    tile = TILE if chunk % (2 * TILE) else 2 * TILE
+    tile = TILE if chunk % (4 * TILE) else 2 * TILE
     whole = lambda i: (0, 0)
     in_specs = [
         pl.BlockSpec((tile, width), lambda i: (i + offset // tile, 0)),
@@ -272,7 +320,7 @@
 
 
 def step(points, owner, member, centroids):
-    lists, width = centroids.shape
+    lists, _ = centroids.shape
     count = points.shape[0]
     blocks = lax.axis_size("blk")
     slots = 2 * count // blocks
@@ -290,23 +338,40 @@
             route.append(((sb % blocks) * 2 + sd, b * 2 + d))
         return lax.ppermute(x, both, route)
 
+    near_owner = fetch(owner, lambda b, d: (b ^ 2, d))
+    near_member = fetch(member, lambda b, d: (b ^ 2, d))
     near_own = fetch(points, lambda b, d: (b ^ 2, d))
     near_other = fetch(points, lambda b, d: (b ^ 2, 1 - d))
 
-    lane = ((mine % (LANES // slots)) * slots).astype(I32).reshape(1)
-    sent = pack(lane, owner.reshape(1, count), member.reshape(1, count), points, blocks, slots)
-    got = lax.all_to_all(sent, "blk", split_axis=0, concat_axis=0, tiled=True)
-
-    own_0 = points.T
-    near_own, near_other = near_own.T, near_other.T
-    part = width // 2
-    first_part = fetch(near_other[:part], lambda b, d: (b ^ 2, d))
-    second_part = fetch(near_own[part:], lambda b, d: (b ^ 2, 1 - d))
+    planes = [[b for b in range(blocks) if (b >> 1) & 1 == z] for z in range(2)]
+    owners = blocks // 2
+    spot = (mine // 4) * 2 + mine % 2
+    lane = ((spot % (LANES // slots)) * slots).astype(I32).reshape(1)
+    plane = ((mine // 2) % 2).astype(I32).reshape(1)
+
+    def deliver(owner, member, rows):
+        sent = pack(
+            lane, plane, owner.reshape(1, count), member.reshape(1, count), rows, owners, slots
+        )
+        return lax.all_to_all(
+            sent, "blk", split_axis=0, concat_axis=0, axis_index_groups=planes, tiled=True
+        )
+
+    near_rows = pltpu.with_memory_space_constraint(near_own, pltpu.HBM)
+    got = [deliver(owner, member, points), deliver(near_owner, near_member, near_rows)]
+
+    own_0 = turn(points)
+    half = count // 2
+    other_0 = turn(
+        fetch(near_own[:half], lambda b, d: (b ^ 2, 1 - d)),
+        fetch(near_other[half:], lambda b, d: (b ^ 2, d)),
+    )
+    near_own = turn(near_own)
+    near_other = turn(near_other)
     far = lambda b, d: (b + 4, d)
     odd = (mine // 2) % 2 == 1
     own_2 = jnp.where(odd, fetch(near_own, far, odd=True), near_own)
     other_2 = jnp.where(odd, fetch(near_other, far, odd=True), near_other)
-    other_0 = jnp.concatenate([first_part, second_part], axis=0)
     even = mine % 2 == 0
     own_1 = fetch(jnp.where(even, own_2, own_0), lambda b, d: (b ^ 1, d))
     other_1 = fetch(jnp.where(even, other_2, other_0), lambda b, d: (b ^ 1, d))
@@ -316,19 +381,17 @@
     )
 
     old = pltpu.with_memory_space_constraint(centroids, pltpu.HBM)
-    half_tiles = lists // 2 // TILE
     new_centroids = None
     arrived = []
     done = 0
     for chunk in CHUNKS:
-        first = ((1 - side) * half_tiles + done // TILE).astype(I32).reshape(1)
-        new_centroids, part = update(first, got, old, new_centroids, chunk, blocks, slots)
+        size = TILE if chunk < 2 * TILE or done % (2 * TILE) else 2 * TILE
+        first = (((1 - side) * (lists // 2) + done) // size).astype(I32).reshape(1)
+        new_centroids, part = update(first, got, old, new_centroids, chunk, slots, size)
         arrived.append(fetch(part, lambda b, d: (b, 1 - d)))
         done += chunk
-    first = (side * half_tiles).astype(I32).reshape(1)
-    new_centroids, own_half = update(
-        first, got, old, new_centroids, lists // 2, blocks, slots
-    )
+    first = (side * (lists // 2) // (2 * TILE)).astype(I32).reshape(1)
+    new_centroids, own_half = update(first, got, old, new_centroids, lists // 2, slots, 2 * TILE)
 
     best = None
     done = 0

time: 212 us -> 210 us (level)
  the two profiles are of different devices: /device:TPU:8 before, /device:TPU:0 now
where the time goes in v2:
time: 210 us; the launch traced here: 209 us
  Pallas kernels  91.8 us (44%)
  starting transfers between devices  55.2 us (26%)
  waiting for transfers between devices  50.2 us (24%)
  other arithmetic  6.98 us (3%)
  local copies, waits for them, and re-layouts  3.53 us (2%)
    ppermute x22, starting transfers between devices, fetch(): return lax.ppermute(x, both, route)  44 us
    ppermute x22, waiting for transfers between devices, fetch(): return lax.ppermute(x, both, route)  42.2 us
    pallas_call x8, Pallas kernels, update(): pl.pallas_call(functools.partial(update_kernel, owners=owners, slots=slot...  39.9 us
    pallas_call x7, Pallas kernels, search(): pl.pallas_call(functools.partial(search_kernel, first=before is None, las...  39.2 us
    all_to_all x2, starting transfers between devices, deliver(): lax.all_to_all(sent, 'blk', split_axis=0, concat_axis=0, axis_index_group...  11.3 us
    all_to_all x2, waiting for transfers between devices, deliver(): lax.all_to_all(sent, 'blk', split_axis=0, concat_axis=0, axis_index_group...  7.96 us
    pallas_call x2, Pallas kernels, pack(): pl.pallas_call(functools.partial(pack_kernel, slots=slots), out_shape=jax...  7.91 us
    pallas_call x4, Pallas kernels, turn(): pl.pallas_call(turn_kernel, out_shape=jax.ShapeDtypeStruct((width, count)...  4.68 us
  transfers between devices with their start and end apart: 24, of which 13 were waited for; matrix products, arithmetic and copies ran while one was open for 4% of the time, Pallas kernels for 42%

profile of v2, /device:TPU:0, one launch (start us, length us, event | category | flops | bytes accessed | tf_op | source)
XLA Modules:
  0.0 208.6 jit_solution(9220181107767527299)
XLA Ops:
  0.6 4.2 %collective-permute-start.4 = (bf16[1024,512]{1,0:T(8,128)(2,1)}, bf16[1024,512]{1,0:T(8,128)(2,1)S(1)}, u32[]{:S(2)}, u32[]{:S(2)}) collective-permute-start(bf16[1024,512]{1,0:T(8,128)(2,1)} %refs_0_.1), channel_id=1, source_target_pairs={{5,0},{4,1},{7,2},{6,3},{1,4},{0,5},{3,6},{2,7},{13,8},{12,9},{15,... | collective-permute-start | bytes 3145736 | tf_op jit(solution)/shard_map/ppermute | solution.py:339
  4.9 4.0 %pack.2 = bf16[32,136,128]{2,1,0:T(8,128)(2,1)} custom-call(s32[1]{0:T(128)} %bitcast.1.lane_ref, s32[1]{0:T(128)} %bitcast.2.plane_ref, s32[1,1024]{1,0:T(1,128)} %bitcast.23, s32[1,1024]{1,0:T(1,128)} %bitcast.24, bf16[1024,512]{1,0:T(8,128)(2,1)} %refs_0_.1), custom_call_target="tpu_custom_call" | custom-call | flops 1073741824 | bytes 4194304 | tf_op jit(solution)/shard_map/pack/pallas_call | solution.py:93
  8.8 7.3 %all-to-all-start = ((bf16[32,136,128]{2,1,0:T(8,128)(2,1)}), bf16[32,136,128]{2,1,0:T(8,128)(2,1)S(1)}, u32[]{:S(2)}, u32[]{:S(2)}) async-start(bf16[32,136,128]{2,1,0:T(8,128)(2,1)} %pack.2), calls=%async_computation | async-start | bytes 2228224 | tf_op jit(solution)/shard_map/all_to_all | solution.py:356
  16.2 12.1 %collective-permute-done.4.refs_0_ = bf16[1024,512]{1,0:T(8,128)(2,1)S(1)} collective-permute-done((bf16[1024,512]{1,0:T(8,128)(2,1)}, bf16[1024,512]{1,0:T(8,128)(2,1)S(1)}, u32[]{:S(2)}, u32[]{:S(2)}) %collective-permute-start.4) | collective-permute-done | bytes 1048608 | tf_op jit(solution)/shard_map/ppermute | solution.py:339
  28.2 1.3 turn.7
  29.6 1.6 collective-permute-start.9
  31.2 1.4 turn.6
  32.6 1.6 collective-permute-start.7
  34.2 0.8 slice.8
  35.1 9.5 %collective-permute-start.3 = (bf16[512,512]{1,0:T(8,128)(2,1)}, bf16[512,512]{1,0:T(8,128)(2,1)}, u32[]{:S(2)}, u32[]{:S(2)}) collective-permute-start(bf16[512,512]{1,0:T(8,128)(2,1)} %slice.8), channel_id=1, source_target_pairs={{5,0},{4,1},{7,2},{6,3},{1,4},{0,5},{3,6},{2,7},{13,8},{12,9},{15,... | collective-permute-start | bytes 1572872 | tf_op jit(solution)/shard_map/ppermute | solution.py:339
  44.6 0.9 slice.9
  45.5 2.0 collective-permute-start
  47.5 10.3 %collective-permute-done = s32[1024,1]{0,1:T(1,128)S(1)} collective-permute-done((s32[1024,1]{0,1:T(1,128)S(1)}, s32[1024,1]{0,1:T(1,128)S(1)}, u32[]{:S(2)}, u32[]{:S(2)}) %collective-permute-start) | collective-permute-done | bytes 4128 | tf_op jit(solution)/shard_map/ppermute | solution.py:339
  58.1 3.3 %collective-permute-done.1 = s32[1024]{0:T(1024)S(1)} collective-permute-done((s32[1024]{0:T(1024)S(1)}, s32[1024]{0:T(1024)S(1)}, u32[]{:S(2)}, u32[]{:S(2)}) %collective-permute-start.1) | collective-permute-done | bytes 4128 | tf_op jit(solution)/shard_map/ppermute | solution.py:339
  62.0 4.0 %pack.3 = bf16[32,136,128]{2,1,0:T(8,128)(2,1)} custom-call(s32[1]{0:T(128)} %bitcast.1.lane_ref, s32[1]{0:T(128)} %bitcast.2.plane_ref, s32[1,1024]{1,0:T(1,128)} %bitcast.25, s32[1,1024]{1,0:T(1,128)} %bitcast.26, bf16[1024,512]{1,0:T(8,128)(2,1)} %copy-done.4), custom_call_target="tpu_custom_call" | custom-call | flops 1073741824 | bytes 4194304 | tf_op jit(solution)/shard_map/pack/pallas_call | solution.py:93
  66.0 3.9 %all-to-all-start.1 = ((bf16[32,136,128]{2,1,0:T(8,128)(2,1)}), bf16[32,136,128]{2,1,0:T(8,128)(2,1)S(1)}, u32[]{:S(2)}, u32[]{:S(2)}) async-start(bf16[32,136,128]{2,1,0:T(8,128)(2,1)} %pack.3), calls=%async_computation.1 | async-start | bytes 2228224 | tf_op jit(solution)/shard_map/all_to_all | solution.py:356
  69.9 1.2 copy-done.5
  72.0 1.5 turn.5.refs_1_
  73.5 3.1 %broadcast_select_fusion.2 = (bf16[512,1024]{1,0:T(8,128)(2,1)}, bf16[512,1024]{1,0:T(8,128)(2,1)}) fusion(bf16[512,1024]{1,0:T(8,128)(2,1)S(1)} %turn.5.refs_1_, pred[]{:T(512)S(6)} %eq.12, bf16[512,1024]{1,0:T(8,128)(2,1)} %collective-permute-done.9, bf16[512,1024]{1,0:T(8,128)(2,1)} %turn.7, pred[]{:T(512)S(6)} %eq.13), kind=kLoop, calls=%fused_computation.4 | loop fusion | flops 1048576 | bytes 5242882 | tf_op jit(solution)/shard_map/jit(_where)/select_n | solution.py:377
  76.7 2.8 %broadcast_select_fusion.3 = (bf16[512,1024]{1,0:T(8,128)(2,1)}, bf16[512,1024]{1,0:T(8,128)(2,1)}) fusion(bf16[512,1024]{1,0:T(8,128)(2,1)S(1)} %turn.4.refs_0_, pred[]{:T(512)S(6)} %eq.12, bf16[512,1024]{1,0:T(8,128)(2,1)} %collective-permute-done.7, bf16[512,1024]{1,0:T(8,128)(2,1)} %turn.6, pred[]{:T(512)S(6)} %eq.13), kind=kLoop, calls=%fused_computation.5 | loop fusion | flops 1048576 | bytes 5242882 | tf_op jit(solution)/shard_map/jit(_where)/select_n | solution.py:376
  79.9 8.0 %all-to-all-done.1.got_b_ref = bf16[32,136,128]{2,1,0:T(8,128)(2,1)S(1)} async-done(((bf16[32,136,128]{2,1,0:T(8,128)(2,1)}), bf16[32,136,128]{2,1,0:T(8,128)(2,1)S(1)}, u32[]{:S(2)}, u32[]{:S(2)}) %all-to-all-start.1) | async-done | bytes 1114144 | tf_op jit(solution)/shard_map/all_to_all | solution.py:356
  87.8 3.7 %update.8 = (bf16[8192,512]{1,0:T(8,128)(2,1)}, bf16[512,512]{1,0:T(8,128)(2,1)S(1)}) custom-call(s32[1]{0:T(128)} %bitcast.13.first_ref, bf16[32,136,128]{2,1,0:T(8,128)(2,1)S(1)} %all-to-all-done.got_a_ref, bf16[32,136,128]{2,1,0:T(8,128)(2,1)S(1)} %all-to-all-done.1.got_b_ref, bf16[8192,512]{1,0:T(8,128)(2,1)} %old_ref.15), custom_call_target="tpu_custom_call" | custom-call | flops 1073741824 | bytes 3801088 | tf_op jit(solution)/shard_map/update/pallas_call | solution.py:177
  91.5 5.0 %update.9 = (bf16[8192,512]{1,0:T(8,128)(2,1)}, bf16[1024,512]{1,0:T(8,128)(2,1)S(1)}) custom-call(s32[1]{0:T(128)} %bitcast.12.first_ref, bf16[32,136,128]{2,1,0:T(8,128)(2,1)S(1)} %all-to-all-done.got_a_ref, bf16[32,136,128]{2,1,0:T(8,128)(2,1)S(1)} %all-to-all-done.1.got_b_ref, bf16[8192,512]{1,0:T(8,128)(2,1)} %old_ref.15, ...), custom_call_target="tpu_custom_call", output_to_operand_aliasing={{0}: (4, {})} | custom-call | flops 2147483648 | bytes 5373952 | tf_op jit(solution)/shard_map/update/pallas_call | solution.py:177
  96.5 3.5 %collective-permute-start.15 = (bf16[1024,512]{1,0:T(8,128)(2,1)S(1)}, bf16[1024,512]{1,0:T(8,128)(2,1)S(1)}, u32[]{:S(2)}, u32[]{:S(2)}) collective-permute-start(bf16[1024,512]{1,0:T(8,128)(2,1)S(1)} %get-tuple-element.35), channel_id=1, source_target_pairs={{1,0},{0,1},{3,2},{2,3},{5,4},{4,5},{7,6},{6,7},{9,8},{8,9},{11,10... | collective-permute-start | bytes 3145736 | tf_op jit(solution)/shard_map/ppermute | solution.py:339
  100.0 5.0 %update.10 = (bf16[8192,512]{1,0:T(8,128)(2,1)}, bf16[1024,512]{1,0:T(8,128)(2,1)S(1)}) custom-call(s32[1]{0:T(128)} %bitcast.11.first_ref, bf16[32,136,128]{2,1,0:T(8,128)(2,1)S(1)} %all-to-all-done.got_a_ref, bf16[32,136,128]{2,1,0:T(8,128)(2,1)S(1)} %all-to-all-done.1.got_b_ref, bf16[8192,512]{1,0:T(8,128)(2,1)} %old_ref.15, ...), custom_call_target="tpu_custom_call", output_to_operand_aliasing={{0}: (4, {})} | custom-call | flops 2147483648 | bytes 5373952 | tf_op jit(solution)/shard_map/update/pallas_call | solution.py:177
  105.0 3.7 %update.11 = (bf16[8192,512]{1,0:T(8,128)(2,1)}, bf16[512,512]{1,0:T(8,128)(2,1)S(1)}) custom-call(s32[1]{0:T(128)} %bitcast.10.first_ref, bf16[32,136,128]{2,1,0:T(8,128)(2,1)S(1)} %all-to-all-done.got_a_ref, bf16[32,136,128]{2,1,0:T(8,128)(2,1)S(1)} %all-to-all-done.1.got_b_ref, bf16[8192,512]{1,0:T(8,128)(2,1)} %old_ref.15, ...), custom_call_target="tpu_custom_call", output_to_operand_aliasing={{0}: (4, {})} | custom-call | flops 1073741824 | bytes 3801088 | tf_op jit(solution)/shard_map/update/pallas_call | solution.py:177
  108.7 3.7 %update.12 = (bf16[8192,512]{1,0:T(8,128)(2,1)}, bf16[512,512]{1,0:T(8,128)(2,1)S(1)}) custom-call(s32[1]{0:T(128)} %bitcast.9.first_ref, bf16[32,136,128]{2,1,0:T(8,128)(2,1)S(1)} %all-to-all-done.got_a_ref, bf16[32,136,128]{2,1,0:T(8,128)(2,1)S(1)} %all-to-all-done.1.got_b_ref, bf16[8192,512]{1,0:T(8,128)(2,1)} %old_ref.15, ...), custom_call_target="tpu_custom_call", output_to_operand_aliasing={{0}: (4, {})} | custom-call | flops 1073741824 | bytes 3801088 | tf_op jit(solution)/shard_map/update/pallas_call | solution.py:177
  112.4 3.0 %update.13 = (bf16[8192,512]{1,0:T(8,128)(2,1)}, bf16[256,512]{1,0:T(8,128)(2,1)S(1)}) custom-call(s32[1]{0:T(128)} %bitcast.8.first_ref, bf16[32,136,128]{2,1,0:T(8,128)(2,1)S(1)} %all-to-all-done.got_a_ref, bf16[32,136,128]{2,1,0:T(8,128)(2,1)S(1)} %all-to-all-done.1.got_b_ref, bf16[8192,512]{1,0:T(8,128)(2,1)} %old_ref.15, ...), custom_call_target="tpu_custom_call", output_to_operand_aliasing={{0}: (4, {})} | custom-call | flops 536870912 | bytes 3014656 | tf_op jit(solution)/shard_map/update/pallas_call | solution.py:177
  115.3 3.0 %update.14 = (bf16[8192,512]{1,0:T(8,128)(2,1)}, bf16[256,512]{1,0:T(8,128)(2,1)S(1)}) custom-call(s32[1]{0:T(128)} %bitcast.7.first_ref, bf16[32,136,128]{2,1,0:T(8,128)(2,1)S(1)} %all-to-all-done.got_a_ref, bf16[32,136,128]{2,1,0:T(8,128)(2,1)S(1)} %all-to-all-done.1.got_b_ref, bf16[8192,512]{1,0:T(8,128)(2,1)} %old_ref.15, ...), custom_call_target="tpu_custom_call", output_to_operand_aliasing={{0}: (4, {})} | custom-call | flops 536870912 | bytes 3014656 | tf_op jit(solution)/shard_map/update/pallas_call | solution.py:177
  118.3 13.0 %update.15 = (bf16[8192,512]{1,0:T(8,128)(2,1)}, bf16[4096,512]{1,0:T(8,128)(2,1)S(1)}) custom-call(s32[1]{0:T(128)} %bitcast.first_ref, bf16[32,136,128]{2,1,0:T(8,128)(2,1)S(1)} %all-to-all-done.got_a_ref, bf16[32,136,128]{2,1,0:T(8,128)(2,1)S(1)} %all-to-all-done.1.got_b_ref, bf16[8192,512]{1,0:T(8,128)(2,1)} %old_ref.15, ...), custom_call_target="tpu_custom_call", output_to_operand_aliasing={{0}: (4, {})} | custom-call | flops 8589934592 | bytes 14811136 | tf_op jit(solution)/shard_map/update/pallas_call | solution.py:177
  131.3 3.5 %collective-permute-start.13 = (bf16[512,512]{1,0:T(8,128)(2,1)S(1)}, bf16[512,512]{1,0:T(8,128)(2,1)S(1)}, u32[]{:S(2)}, u32[]{:S(2)}) collective-permute-start(bf16[512,512]{1,0:T(8,128)(2,1)S(1)} %get-tuple-element.33), channel_id=1, source_target_pairs={{1,0},{0,1},{3,2},{2,3},{5,4},{4,5},{7,6},{6,7},{9,8},{8,9},{11,10... | collective-permute-start | bytes 1572872 | tf_op jit(solution)/shard_map/ppermute | solution.py:339
  134.9 3.4 %collective-permute-start.11 = (bf16[256,512]{1,0:T(8,128)(2,1)S(1)}, bf16[256,512]{1,0:T(8,128)(2,1)S(1)}, u32[]{:S(2)}, u32[]{:S(2)}) collective-permute-start(bf16[256,512]{1,0:T(8,128)(2,1)S(1)} %get-tuple-element.31), channel_id=1, source_target_pairs={{1,0},{0,1},{3,2},{2,3},{5,4},{4,5},{7,6},{6,7},{9,8},{8,9},{11,10... | collective-permute-start | bytes 786440 | tf_op jit(solution)/shard_map/ppermute | solution.py:339
  138.4 5.2 %search.7.refs_6_ = f32[8,3072]{1,0:T(8,128)S(1)} custom-call(bf16[4096,512]{1,0:T(8,128)(2,1)S(1)} %get-tuple-element.29.own_ref, bf16[512,512]{1,0:T(8,128)(2,1)S(1)} %collective-permute-done.16.other_ref, bf16[512,1024]{1,0:T(8,128)(2,1)S(1)} %turn.4.refs_0_, bf16[512,1024]{1,0:T(8,128)(2,1)S(1)} %copy-done.1, ...), custom_call_target="tpu_custom_call" | custom-call | flops 3221225472 | bytes 7340032 | tf_op jit(solution)/shard_map/search/pallas_call | solution.py:303
  144.0 8.4 %search.8.refs_6_ = f32[8,3072]{1,0:T(8,128)S(1)} custom-call(bf16[4096,512]{1,0:T(8,128)(2,1)S(1)} %get-tuple-element.29.own_ref, bf16[1024,512]{1,0:T(8,128)(2,1)S(1)} %collective-permute-done.15.other_ref, bf16[512,1024]{1,0:T(8,128)(2,1)S(1)} %turn.4.refs_0_, bf16[512,1024]{1,0:T(8,128)(2,1)S(1)} %copy-done.1, ...), custom_call_target="tpu_custom_call" | custom-call | flops 6442450944 | bytes 8388608 | tf_op jit(solution)/shard_map/search/pallas_call | solution.py:303
  152.7 8.4 %search.9.refs_6_ = f32[8,3072]{1,0:T(8,128)S(1)} custom-call(bf16[4096,512]{1,0:T(8,128)(2,1)S(1)} %get-tuple-element.29.own_ref, bf16[1024,512]{1,0:T(8,128)(2,1)S(1)} %collective-permute-done.14.other_ref, bf16[512,1024]{1,0:T(8,128)(2,1)S(1)} %turn.4.refs_0_, bf16[512,1024]{1,0:T(8,128)(2,1)S(1)} %copy-done.1, ...), custom_call_target="tpu_custom_call" | custom-call | flops 6442450944 | bytes 8388608 | tf_op jit(solution)/shard_map/search/pallas_call | solution.py:303
  161.2 2.8 %collective-permute-done.13.other_ref = bf16[512,512]{1,0:T(8,128)(2,1)S(1)} collective-permute-done((bf16[512,512]{1,0:T(8,128)(2,1)S(1)}, bf16[512,512]{1,0:T(8,128)(2,1)S(1)}, u32[]{:S(2)}, u32[]{:S(2)}) %collective-permute-start.13) | collective-permute-done | bytes 524320 | tf_op jit(solution)/shard_map/ppermute | solution.py:339
  164.0 5.2 %search.10.refs_6_ = f32[8,3072]{1,0:T(8,128)S(1)} custom-call(bf16[4096,512]{1,0:T(8,128)(2,1)S(1)} %get-tuple-element.29.own_ref, bf16[512,512]{1,0:T(8,128)(2,1)S(1)} %collective-permute-done.13.other_ref, bf16[512,1024]{1,0:T(8,128)(2,1)S(1)} %turn.4.refs_0_, bf16[512,1024]{1,0:T(8,128)(2,1)S(1)} %copy-done.1, ...), custom_call_target="tpu_custom_call" | custom-call | flops 3221225472 | bytes 7340032 | tf_op jit(solution)/shard_map/search/pallas_call | solution.py:303
  169.2 6.0 %collective-permute-done.12.other_ref = bf16[512,512]{1,0:T(8,128)(2,1)S(1)} collective-permute-done((bf16[512,512]{1,0:T(8,128)(2,1)S(1)}, bf16[512,512]{1,0:T(8,128)(2,1)S(1)}, u32[]{:S(2)}, u32[]{:S(2)}) %collective-permute-start.12) | collective-permute-done | bytes 524320 | tf_op jit(solution)/shard_map/ppermute | solution.py:339
  175.2 5.2 %search.11.refs_6_ = f32[8,3072]{1,0:T(8,128)S(1)} custom-call(bf16[4096,512]{1,0:T(8,128)(2,1)S(1)} %get-tuple-element.29.own_ref, bf16[512,512]{1,0:T(8,128)(2,1)S(1)} %collective-permute-done.12.other_ref, bf16[512,1024]{1,0:T(8,128)(2,1)S(1)} %turn.4.refs_0_, bf16[512,1024]{1,0:T(8,128)(2,1)S(1)} %copy-done.1, ...), custom_call_target="tpu_custom_call" | custom-call | flops 3221225472 | bytes 7340032 | tf_op jit(solution)/shard_map/search/pallas_call | solution.py:303
  180.8 3.4 %search.12.refs_6_ = f32[8,3072]{1,0:T(8,128)S(1)} custom-call(bf16[4096,512]{1,0:T(8,128)(2,1)S(1)} %get-tuple-element.29.own_ref, bf16[256,512]{1,0:T(8,128)(2,1)S(1)} %collective-permute-done.11.other_ref, bf16[512,1024]{1,0:T(8,128)(2,1)S(1)} %turn.4.refs_0_, bf16[512,1024]{1,0:T(8,128)(2,1)S(1)} %copy-done.1, ...), custom_call_target="tpu_custom_call" | custom-call | flops 1610612736 | bytes 6815744 | tf_op jit(solution)/shard_map/search/pallas_call | solution.py:303
  184.2 1.4 collective-permute-done.6.other_ref
  185.6 3.4 %search.13 = (f32[1,1024]{1,0:T(1,128)S(1)}, f32[1,1024]{1,0:T(1,128)S(1)}, f32[1,1024]{1,0:T(1,128)S(1)}) custom-call(bf16[4096,512]{1,0:T(8,128)(2,1)S(1)} %get-tuple-element.29.own_ref, bf16[256,512]{1,0:T(8,128)(2,1)S(1)} %collective-permute-done.6.other_ref, bf16[512,1024]{1,0:T(8,128)(2,1)S(1)} %turn.4.refs_0_, bf16[512,1024]{1,0:T(8,128)(2,1)S(1)} %copy-done.1, ...), custom_call_target="tpu_custom_call" | custom-call | flops 1610612736 | bytes 6815744 | tf_op jit(solution)/shard_map/search/pallas_call | solution.py:303
  189.0 9.9 %collective-permute-start.19 = (f32[1024]{0:T(1024)S(1)}, f32[1024]{0:T(1024)S(1)}, u32[]{:S(2)}, u32[]{:S(2)}) collective-permute-start(f32[1024]{0:T(1024)S(1)} %bitcast.22), channel_id=1, source_target_pairs={{127,0},{126,1},{1,2},{0,3},{3,4},{2,5},{5,6},{4,7},{7,8},{6,9},{9... | collective-permute-start | bytes 12296 | tf_op jit(solution)/shard_map/ppermute | solution.py:339
  198.9 3.2 %collective-permute-start.17 = (f32[1024]{0:T(1024)S(1)}, f32[1024]{0:T(1024)S(1)}, u32[]{:S(2)}, u32[]{:S(2)}) collective-permute-start(f32[1024]{0:T(1024)S(1)} %bitcast.17), channel_id=1, source_target_pairs={{1,0},{0,1},{3,2},{2,3},{5,4},{4,5},{7,6},{6,7},{9,8},{8,9},{11,10... | collective-permute-start | bytes 12296 | tf_op jit(solution)/shard_map/ppermute | solution.py:339
  202.3 1.7 collective-permute-done.17
  204.2 2.5 %collective-permute-done.20 = f32[1024]{0:T(1024)S(1)} collective-permute-done((f32[1024]{0:T(1024)S(1)}, f32[1024]{0:T(1024)S(1)}, u32[]{:S(2)}, u32[]{:S(2)}) %collective-permute-start.20) | collective-permute-done | bytes 4128 | tf_op jit(solution)/shard_map/ppermute | solution.py:339
  206.7 1.2 collective-permute-done.21
  208.0 0.6 subtract_multiply_fusion
  (48 shorter events, 3.9 us)
Async XLA Ops:
  0.6 44.8 %copy-start.6 = (s32[1024,1]{0,1:T(1,128)S(1)}, s32[1024,1]{0,1:T(1,128)}, u32[]{:S(2)}) copy-start(s32[1024,1]{0,1:T(1,128)} %param.5) | copy-start | bytes 12292
  0.6 57.2 %copy-start.7 = (s32[1024]{0:T(1024)S(1)}, s32[1024]{0:T(1024)}, u32[]{:S(2)}) copy-start(s32[1024]{0:T(1024)} %param.6) | copy-start | bytes 12292
  0.6 27.6 %collective-permute-start.4 = (bf16[1024,512]{1,0:T(8,128)(2,1)}, bf16[1024,512]{1,0:T(8,128)(2,1)S(1)}, u32[]{:S(2)}, u32[]{:S(2)}) collective-permute-start(bf16[1024,512]{1,0:T(8,128)(2,1)} %refs_0_.1), channel_id=1, source_target_pairs={{5,0},{4,1},{7,2},{6,3},{1,4},{0,5},{3,6},{2,7},{13,8},{12,9},{15,... | collective-permute-start | bytes 3145736 | tf_op jit(solution)/shard_map/ppermute | solution.py:339
  4.9 26.3 %collective-permute-start.2 = (bf16[1024,512]{1,0:T(8,128)(2,1)}, bf16[1024,512]{1,0:T(8,128)(2,1)S(1)}, u32[]{:S(2)}, u32[]{:S(2)}) collective-permute-start(bf16[1024,512]{1,0:T(8,128)(2,1)} %refs_0_.1), channel_id=1, source_target_pairs={{4,0},{5,1},{6,2},{7,3},{0,4},{1,5},{2,6},{3,7},{12,8},{13,9},{14,... | collective-permute-start | bytes 3145736 | tf_op jit(solution)/shard_map/ppermute | solution.py:339
  8.8 57.1 %all-to-all-start = ((bf16[32,136,128]{2,1,0:T(8,128)(2,1)}), bf16[32,136,128]{2,1,0:T(8,128)(2,1)S(1)}, u32[]{:S(2)}, u32[]{:S(2)}) async-start(bf16[32,136,128]{2,1,0:T(8,128)(2,1)} %pack.2), calls=%async_computation | async-start | bytes 2228224 | tf_op jit(solution)/shard_map/all_to_all | solution.py:356
  29.6 43.9 %collective-permute-start.9 = (bf16[512,1024]{1,0:T(8,128)(2,1)}, bf16[512,1024]{1,0:T(8,128)(2,1)}, u32[]{:S(2)}, u32[]{:S(2)}) collective-permute-start(bf16[512,1024]{1,0:T(8,128)(2,1)} %turn.7), channel_id=1, source_target_pairs={{12,4},{13,5},{14,6},{15,7},{20,12},{21,13},{22,14},{23,15},{28,20... | collective-permute-start | bytes 3145736 | tf_op jit(solution)/shard_map/ppermute | solution.py:339
  31.2 30.2 %copy-start.4 = (bf16[1024,512]{1,0:T(8,128)(2,1)}, bf16[1024,512]{1,0:T(8,128)(2,1)S(1)}, u32[]{:S(2)}) copy-start(bf16[1024,512]{1,0:T(8,128)(2,1)S(1)} %collective-permute-done.2.pts_ref.refs_0_) | copy-start | bytes 3145732
  32.6 44.1 %collective-permute-start.7 = (bf16[512,1024]{1,0:T(8,128)(2,1)}, bf16[512,1024]{1,0:T(8,128)(2,1)}, u32[]{:S(2)}, u32[]{:S(2)}) collective-permute-start(bf16[512,1024]{1,0:T(8,128)(2,1)} %turn.6), channel_id=1, source_target_pairs={{12,4},{13,5},{14,6},{15,7},{20,12},{21,13},{22,14},{23,15},{28,20... | collective-permute-start | bytes 3145736 | tf_op jit(solution)/shard_map/ppermute | solution.py:339
  35.1 36.9 %collective-permute-start.3 = (bf16[512,512]{1,0:T(8,128)(2,1)}, bf16[512,512]{1,0:T(8,128)(2,1)}, u32[]{:S(2)}, u32[]{:S(2)}) collective-permute-start(bf16[512,512]{1,0:T(8,128)(2,1)} %slice.8), channel_id=1, source_target_pairs={{5,0},{4,1},{7,2},{6,3},{1,4},{0,5},{3,6},{2,7},{13,8},{12,9},{15,... | collective-permute-start | bytes 1572872 | tf_op jit(solution)/shard_map/ppermute | solution.py:339
  45.5 26.5 %collective-permute-start.5 = (bf16[512,512]{1,0:T(8,128)(2,1)}, bf16[512,512]{1,0:T(8,128)(2,1)}, u32[]{:S(2)}, u32[]{:S(2)}) collective-permute-start(bf16[512,512]{1,0:T(8,128)(2,1)} %slice.9), channel_id=1, source_target_pairs={{4,0},{5,1},{6,2},{7,3},{0,4},{1,5},{2,6},{3,7},{12,8},{13,9},{14,... | collective-permute-start | bytes 1572872 | tf_op jit(solution)/shard_map/ppermute | solution.py:339
  45.5 12.3 %collective-permute-start = (s32[1024,1]{0,1:T(1,128)S(1)}, s32[1024,1]{0,1:T(1,128)S(1)}, u32[]{:S(2)}, u32[]{:S(2)}) collective-permute-start(s32[1024,1]{0,1:T(1,128)S(1)} %copy-done.6), channel_id=1, source_target_pairs={{4,0},{5,1},{6,2},{7,3},{0,4},{1,5},{2,6},{3,7},{12,8},{13,9},{14,... | collective-permute-start | bytes 12296 | tf_op jit(solution)/shard_map/ppermute | solution.py:339
  57.8 3.6 %copy-start.8 = (s32[1024,1]{0,1:T(1,128)}, s32[1024,1]{0,1:T(1,128)S(1)}, u32[]{:S(2)}) copy-start(s32[1024,1]{0,1:T(1,128)S(1)} %collective-permute-done) | copy-start | bytes 12292
  57.8 3.6 %collective-permute-start.1 = (s32[1024]{0:T(1024)S(1)}, s32[1024]{0:T(1024)S(1)}, u32[]{:S(2)}, u32[]{:S(2)}) collective-permute-start(s32[1024]{0:T(1024)S(1)} %copy-done.7), channel_id=1, source_target_pairs={{4,0},{5,1},{6,2},{7,3},{0,4},{1,5},{2,6},{3,7},{12,8},{13,9},{14,... | collective-permute-start | bytes 12296 | tf_op jit(solution)/shard_map/ppermute | solution.py:339
  61.4 0.6 copy-start.9
  66.0 21.9 %all-to-all-start.1 = ((bf16[32,136,128]{2,1,0:T(8,128)(2,1)}), bf16[32,136,128]{2,1,0:T(8,128)(2,1)S(1)}, u32[]{:S(2)}, u32[]{:S(2)}) async-start(bf16[32,136,128]{2,1,0:T(8,128)(2,1)} %pack.3), calls=%async_computation.1 | async-start | bytes 2228224 | tf_op jit(solution)/shard_map/all_to_all | solution.py:356
  69.9 1.2 copy-start.5
  73.4 6.1 %copy-start = (bf16[512,1024]{1,0:T(8,128)(2,1)}, bf16[512,1024]{1,0:T(8,128)(2,1)S(1)}, u32[]{:S(2)}) copy-start(bf16[512,1024]{1,0:T(8,128)(2,1)S(1)} %turn.5.refs_1_) | copy-start | bytes 3145732
  76.5 58.3 %collective-permute-start.10 = (bf16[512,1024]{1,0:T(8,128)(2,1)}, bf16[512,1024]{1,0:T(8,128)(2,1)}, u32[]{:S(2)}, u32[]{:S(2)}) collective-permute-start(bf16[512,1024]{1,0:T(8,128)(2,1)} %get-tuple-element.40), channel_id=1, source_target_pairs={{2,0},{3,1},{0,2},{1,3},{6,4},{7,5},{4,6},{5,7},{10,8},{11,9},{8,1... | collective-permute-start | bytes 3145736 | tf_op jit(solution)/shard_map/ppermute | solution.py:339
  79.5 55.4 %collective-permute-start.8 = (bf16[512,1024]{1,0:T(8,128)(2,1)}, bf16[512,1024]{1,0:T(8,128)(2,1)}, u32[]{:S(2)}, u32[]{:S(2)}) collective-permute-start(bf16[512,1024]{1,0:T(8,128)(2,1)} %get-tuple-element.42), channel_id=1, source_target_pairs={{2,0},{3,1},{0,2},{1,3},{6,4},{7,5},{4,6},{5,7},{10,8},{11,9},{8,1... | collective-permute-start | bytes 3145736 | tf_op jit(solution)/shard_map/ppermute | solution.py:339
  91.5 39.8 %collective-permute-start.16 = (bf16[512,512]{1,0:T(8,128)(2,1)S(1)}, bf16[512,512]{1,0:T(8,128)(2,1)S(1)}, u32[]{:S(2)}, u32[]{:S(2)}) collective-permute-start(bf16[512,512]{1,0:T(8,128)(2,1)S(1)} %get-tuple-element.36), channel_id=1, source_target_pairs={{1,0},{0,1},{3,2},{2,3},{5,4},{4,5},{7,6},{6,7},{9,8},{8,9},{11,10... | collective-permute-start | bytes 1572872 | tf_op jit(solution)/shard_map/ppermute | solution.py:339
  96.5 47.2 %collective-permute-start.15 = (bf16[1024,512]{1,0:T(8,128)(2,1)S(1)}, bf16[1024,512]{1,0:T(8,128)(2,1)S(1)}, u32[]{:S(2)}, u32[]{:S(2)}) collective-permute-start(bf16[1024,512]{1,0:T(8,128)(2,1)S(1)} %get-tuple-element.35), channel_id=1, source_target_pairs={{1,0},{0,1},{3,2},{2,3},{5,4},{4,5},{7,6},{6,7},{9,8},{8,9},{11,10... | collective-permute-start | bytes 3145736 | tf_op jit(solution)/shard_map/ppermute | solution.py:339
  105.0 47.7 %collective-permute-start.14 = (bf16[1024,512]{1,0:T(8,128)(2,1)S(1)}, bf16[1024,512]{1,0:T(8,128)(2,1)S(1)}, u32[]{:S(2)}, u32[]{:S(2)}) collective-permute-start(bf16[1024,512]{1,0:T(8,128)(2,1)S(1)} %get-tuple-element.34), channel_id=1, source_target_pairs={{1,0},{0,1},{3,2},{2,3},{5,4},{4,5},{7,6},{6,7},{9,8},{8,9},{11,10... | collective-permute-start | bytes 3145736 | tf_op jit(solution)/shard_map/ppermute | solution.py:339
  118.3 20.1 %copy-start.1 = (bf16[512,1024]{1,0:T(8,128)(2,1)S(1)}, bf16[512,1024]{1,0:T(8,128)(2,1)}, u32[]{:S(2)}) copy-start(bf16[512,1024]{1,0:T(8,128)(2,1)} %copy-done) | copy-start | bytes 3145732
  118.3 20.1 %copy-start.2 = (bf16[512,1024]{1,0:T(8,128)(2,1)S(1)}, bf16[512,1024]{1,0:T(8,128)(2,1)}, u32[]{:S(2)}) copy-start(bf16[512,1024]{1,0:T(8,128)(2,1)} %get-tuple-element.41.refs_5_) | copy-start | bytes 3145732
  118.3 20.1 %copy-start.3 = (bf16[512,1024]{1,0:T(8,128)(2,1)S(1)}, bf16[512,1024]{1,0:T(8,128)(2,1)}, u32[]{:S(2)}) copy-start(bf16[512,1024]{1,0:T(8,128)(2,1)} %get-tuple-element.43.refs_4_) | copy-start | bytes 3145732
  131.3 32.7 %collective-permute-start.13 = (bf16[512,512]{1,0:T(8,128)(2,1)S(1)}, bf16[512,512]{1,0:T(8,128)(2,1)S(1)}, u32[]{:S(2)}, u32[]{:S(2)}) collective-permute-start(bf16[512,512]{1,0:T(8,128)(2,1)S(1)} %get-tuple-element.33), channel_id=1, source_target_pairs={{1,0},{0,1},{3,2},{2,3},{5,4},{4,5},{7,6},{6,7},{9,8},{8,9},{11,10... | collective-permute-start | bytes 1572872 | tf_op jit(solution)/shard_map/ppermute | solution.py:339
  134.9 40.4 %collective-permute-start.12 = (bf16[512,512]{1,0:T(8,128)(2,1)S(1)}, bf16[512,512]{1,0:T(8,128)(2,1)S(1)}, u32[]{:S(2)}, u32[]{:S(2)}) collective-permute-start(bf16[512,512]{1,0:T(8,128)(2,1)S(1)} %get-tuple-element.32), channel_id=1, source_target_pairs={{1,0},{0,1},{3,2},{2,3},{5,4},{4,5},{7,6},{6,7},{9,8},{8,9},{11,10... | collective-permute-start | bytes 1572872 | tf_op jit(solution)/shard_map/ppermute | solution.py:339
  134.9 45.9 %collective-permute-start.11 = (bf16[256,512]{1,0:T(8,128)(2,1)S(1)}, bf16[256,512]{1,0:T(8,128)(2,1)S(1)}, u32[]{:S(2)}, u32[]{:S(2)}) collective-permute-start(bf16[256,512]{1,0:T(8,128)(2,1)S(1)} %get-tuple-element.31), channel_id=1, source_target_pairs={{1,0},{0,1},{3,2},{2,3},{5,4},{4,5},{7,6},{6,7},{9,8},{8,9},{11,10... | collective-permute-start | bytes 786440 | tf_op jit(solution)/shard_map/ppermute | solution.py:339
  143.6 41.9 %collective-permute-start.6 = (bf16[256,512]{1,0:T(8,128)(2,1)S(1)}, bf16[256,512]{1,0:T(8,128)(2,1)S(1)}, u32[]{:S(2)}, u32[]{:S(2)}) collective-permute-start(bf16[256,512]{1,0:T(8,128)(2,1)S(1)} %get-tuple-element.30), channel_id=1, source_target_pairs={{1,0},{0,1},{3,2},{2,3},{5,4},{4,5},{7,6},{6,7},{9,8},{8,9},{11,10... | collective-permute-start | bytes 786440 | tf_op jit(solution)/shard_map/ppermute | solution.py:339
  189.0 15.1 %collective-permute-start.18 = (f32[1024]{0:T(1024)S(1)}, f32[1024]{0:T(1024)S(1)}, u32[]{:S(2)}, u32[]{:S(2)}) collective-permute-start(f32[1024]{0:T(1024)S(1)} %bitcast.21), channel_id=1, source_target_pairs={{126,0},{127,1},{0,2},{1,3},{2,4},{3,5},{4,6},{5,7},{6,8},{7,9},{8... | collective-permute-start | bytes 12296 | tf_op jit(solution)/shard_map/ppermute | solution.py:339
  189.0 15.2 %collective-permute-start.19 = (f32[1024]{0:T(1024)S(1)}, f32[1024]{0:T(1024)S(1)}, u32[]{:S(2)}, u32[]{:S(2)}) collective-permute-start(f32[1024]{0:T(1024)S(1)} %bitcast.22), channel_id=1, source_target_pairs={{127,0},{126,1},{1,2},{0,3},{3,4},{2,5},{5,6},{4,7},{7,8},{6,9},{9... | collective-permute-start | bytes 12296 | tf_op jit(solution)/shard_map/ppermute | solution.py:339
  198.9 7.8 %collective-permute-start.20 = (f32[1024]{0:T(1024)S(1)}, f32[1024]{0:T(1024)S(1)}, u32[]{:S(2)}, u32[]{:S(2)}) collective-permute-start(f32[1024]{0:T(1024)S(1)} %bitcast.19), channel_id=1, source_target_pairs={{124,0},{125,1},{126,2},{127,3},{0,4},{1,5},{2,6},{3,7},{4,8},{5,9... | collective-permute-start | bytes 12296 | tf_op jit(solution)/shard_map/ppermute | solution.py:339
  198.9 9.0 %collective-permute-start.21 = (f32[1024]{0:T(1024)S(1)}, f32[1024]{0:T(1024)S(1)}, u32[]{:S(2)}, u32[]{:S(2)}) collective-permute-start(f32[1024]{0:T(1024)S(1)} %bitcast.20), channel_id=1, source_target_pairs={{125,0},{124,1},{127,2},{126,3},{1,4},{0,5},{3,6},{2,7},{5,8},{4,9... | collective-permute-start | bytes 12296 | tf_op jit(solution)/shard_map/ppermute | solution.py:339
  198.9 5.1 %collective-permute-start.17 = (f32[1024]{0:T(1024)S(1)}, f32[1024]{0:T(1024)S(1)}, u32[]{:S(2)}, u32[]{:S(2)}) collective-permute-start(f32[1024]{0:T(1024)S(1)} %bitcast.17), channel_id=1, source_target_pairs={{1,0},{0,1},{3,2},{2,3},{5,4},{4,5},{7,6},{6,7},{9,8},{8,9},{11,10... | collective-permute-start | bytes 12296 | tf_op jit(solution)/shard_map/ppermute | solution.py:339

commit v3 on v2

--- a/solution.py
+++ b/solution.py
@@ -280,7 +280,7 @@
     chunk, width = other.shape
     sections = CYCLE + 1
     count = points[0].shape[1]
-    tile = TILE if chunk % (4 * TILE) else 2 * TILE
+    tile = TILE if chunk % (4 * TILE) or offset % (2 * TILE) else 2 * TILE
     whole = lambda i: (0, 0)
     in_specs = [
         pl.BlockSpec((tile, width), lambda i: (i + offset // tile, 0)),
@@ -399,10 +399,12 @@
         best = search(own_half, done, arrived[n], visitors, best, n == len(CHUNKS) - 1)
         done += chunk
     best = [x.reshape(count) for x in best]
-    top = jnp.maximum(best[0], fetch(best[0], lambda b, d: (b, 1 - d)))
-    for s in range(1, CYCLE + 1):
-        for flip in (0, 1):
-            top = jnp.maximum(top, fetch(best[s], lambda b, d: (b - s, d ^ flip)))
+    other_core = fetch(best[1], lambda b, d: (b ^ 1, d))
+    here = jnp.where(even, best[0], jnp.maximum(best[0], other_core))
+    onward = jnp.where(even, jnp.maximum(best[2], other_core), best[2])
+    top = jnp.maximum(here, fetch(here, lambda b, d: (b, 1 - d)))
+    for flip in (0, 1):
+        top = jnp.maximum(top, fetch(onward, lambda b, d: (b - 2, d ^ flip)))
     nearest = (squares - 2.0 * top) / D
     return new_centroids, nearest
 

time: 210 us -> 208 us (level)
  the two profiles are of different devices: /device:TPU:0 before, /device:TPU:7 now
where the time goes in v3:
time: 208 us; the launch traced here: 204 us
  Pallas kernels  91.8 us (44%)
  starting transfers between devices  55.6 us (27%)
  waiting for transfers between devices  45.6 us (22%)
  other arithmetic  6.98 us (3%)
  local copies, waits for them, and re-layouts  3.53 us (2%)
    pallas_call x8, Pallas kernels, update(): pl.pallas_call(functools.partial(update_kernel, owners=owners, slots=slot...  39.9 us
    pallas_call x7, Pallas kernels, search(): pl.pallas_call(functools.partial(search_kernel, first=before is None, las...  39.2 us
    ppermute x21, waiting for transfers between devices, fetch(): return lax.ppermute(x, both, route)  38.6 us
    ppermute x21, starting transfers between devices, fetch(): return lax.ppermute(x, both, route)  35.1 us
    all_to_all x2, starting transfers between devices, deliver(): lax.all_to_all(sent, 'blk', split_axis=0, concat_axis=0, axis_index_group...  20.5 us
    pallas_call x2, Pallas kernels, pack(): pl.pallas_call(functools.partial(pack_kernel, slots=slots), out_shape=jax...  7.92 us
    all_to_all x2, waiting for transfers between devices, deliver(): lax.all_to_all(sent, 'blk', split_axis=0, concat_axis=0, axis_index_group...  6.94 us
    pallas_call x4, Pallas kernels, turn(): pl.pallas_call(turn_kernel, out_shape=jax.ShapeDtypeStruct((width, count)...  4.68 us
  transfers between devices with their start and end apart: 23, of which 11 were waited for; matrix products, arithmetic and copies ran while one was open for 4% of the time, Pallas kernels for 43%

profile of v3, /device:TPU:7, one launch (start us, length us, event | category | flops | bytes accessed | tf_op | source)
XLA Modules:
  0.0 204.4 jit_solution(18327335226525113684)
XLA Ops:
  0.6 3.8 %collective-permute-start.4 = (bf16[1024,512]{1,0:T(8,128)(2,1)}, bf16[1024,512]{1,0:T(8,128)(2,1)S(1)}, u32[]{:S(2)}, u32[]{:S(2)}) collective-permute-start(bf16[1024,512]{1,0:T(8,128)(2,1)} %refs_0_.1), channel_id=1, source_target_pairs={{5,0},{4,1},{7,2},{6,3},{1,4},{0,5},{3,6},{2,7},{13,8},{12,9},{15,... | collective-permute-start | bytes 3145736 | tf_op jit(solution)/shard_map/ppermute | solution.py:339
  4.5 4.0 %pack.2 = bf16[32,136,128]{2,1,0:T(8,128)(2,1)} custom-call(s32[1]{0:T(128)} %bitcast.1.lane_ref, s32[1]{0:T(128)} %bitcast.2.plane_ref, s32[1,1024]{1,0:T(1,128)} %bitcast.20, s32[1,1024]{1,0:T(1,128)} %bitcast.21, bf16[1024,512]{1,0:T(8,128)(2,1)} %refs_0_.1), custom_call_target="tpu_custom_call" | custom-call | flops 1073741824 | bytes 4194304 | tf_op jit(solution)/shard_map/pack/pallas_call | solution.py:93
  8.5 8.1 %all-to-all-start = ((bf16[32,136,128]{2,1,0:T(8,128)(2,1)}), bf16[32,136,128]{2,1,0:T(8,128)(2,1)S(1)}, u32[]{:S(2)}, u32[]{:S(2)}) async-start(bf16[32,136,128]{2,1,0:T(8,128)(2,1)} %pack.2), calls=%async_computation | async-start | bytes 2228224 | tf_op jit(solution)/shard_map/all_to_all | solution.py:356
  16.6 11.0 %collective-permute-done.4.refs_0_ = bf16[1024,512]{1,0:T(8,128)(2,1)S(1)} collective-permute-done((bf16[1024,512]{1,0:T(8,128)(2,1)}, bf16[1024,512]{1,0:T(8,128)(2,1)S(1)}, u32[]{:S(2)}, u32[]{:S(2)}) %collective-permute-start.4) | collective-permute-done | bytes 1048608 | tf_op jit(solution)/shard_map/ppermute | solution.py:339
  27.6 1.3 turn.7
  28.9 1.6 collective-permute-start.9
  30.5 1.4 turn.6
  31.9 1.6 collective-permute-start.7
  33.6 0.8 slice.8
  34.4 3.7 %collective-permute-start.3 = (bf16[512,512]{1,0:T(8,128)(2,1)}, bf16[512,512]{1,0:T(8,128)(2,1)}, u32[]{:S(2)}, u32[]{:S(2)}) collective-permute-start(bf16[512,512]{1,0:T(8,128)(2,1)} %slice.8), channel_id=1, source_target_pairs={{5,0},{4,1},{7,2},{6,3},{1,4},{0,5},{3,6},{2,7},{13,8},{12,9},{15,... | collective-permute-start | bytes 1572872 | tf_op jit(solution)/shard_map/ppermute | solution.py:339
  38.1 0.9 slice.9
  39.0 1.5 collective-permute-start
  40.5 10.0 %collective-permute-done = s32[1024,1]{0,1:T(1,128)S(1)} collective-permute-done((s32[1024,1]{0,1:T(1,128)S(1)}, s32[1024,1]{0,1:T(1,128)S(1)}, u32[]{:S(2)}, u32[]{:S(2)}) %collective-permute-start) | collective-permute-done | bytes 4128 | tf_op jit(solution)/shard_map/ppermute | solution.py:339
  50.8 2.5 %collective-permute-done.1 = s32[1024]{0:T(1024)S(1)} collective-permute-done((s32[1024]{0:T(1024)S(1)}, s32[1024]{0:T(1024)S(1)}, u32[]{:S(2)}, u32[]{:S(2)}) %collective-permute-start.1) | collective-permute-done | bytes 4128 | tf_op jit(solution)/shard_map/ppermute | solution.py:339
  53.9 4.0 %pack.3 = bf16[32,136,128]{2,1,0:T(8,128)(2,1)} custom-call(s32[1]{0:T(128)} %bitcast.1.lane_ref, s32[1]{0:T(128)} %bitcast.2.plane_ref, s32[1,1024]{1,0:T(1,128)} %bitcast.22, s32[1,1024]{1,0:T(1,128)} %bitcast.23, bf16[1024,512]{1,0:T(8,128)(2,1)} %copy-done.4), custom_call_target="tpu_custom_call" | custom-call | flops 1073741824 | bytes 4194304 | tf_op jit(solution)/shard_map/pack/pallas_call | solution.py:93
  57.8 12.4 %all-to-all-start.1 = ((bf16[32,136,128]{2,1,0:T(8,128)(2,1)}), bf16[32,136,128]{2,1,0:T(8,128)(2,1)S(1)}, u32[]{:S(2)}, u32[]{:S(2)}) async-start(bf16[32,136,128]{2,1,0:T(8,128)(2,1)} %pack.3), calls=%async_computation.1 | async-start | bytes 2228224 | tf_op jit(solution)/shard_map/all_to_all | solution.py:356
  70.3 1.2 copy-done.5
  72.1 1.5 turn.5.refs_1_
  73.5 3.1 %broadcast_select_fusion.2 = (bf16[512,1024]{1,0:T(8,128)(2,1)}, bf16[512,1024]{1,0:T(8,128)(2,1)}) fusion(bf16[512,1024]{1,0:T(8,128)(2,1)S(1)} %turn.5.refs_1_, pred[]{:T(512)S(6)} %eq.12, bf16[512,1024]{1,0:T(8,128)(2,1)} %collective-permute-done.9, bf16[512,1024]{1,0:T(8,128)(2,1)} %turn.7, pred[]{:T(512)S(6)} %eq.13), kind=kLoop, calls=%fused_computation.4 | loop fusion | flops 1048576 | bytes 5242882 | tf_op jit(solution)/shard_map/jit(_where)/select_n | solution.py:377
  77.0 2.8 %broadcast_select_fusion.3 = (bf16[512,1024]{1,0:T(8,128)(2,1)}, bf16[512,1024]{1,0:T(8,128)(2,1)}) fusion(bf16[512,1024]{1,0:T(8,128)(2,1)S(1)} %turn.4.refs_0_, pred[]{:T(512)S(6)} %eq.12, bf16[512,1024]{1,0:T(8,128)(2,1)} %collective-permute-done.7, bf16[512,1024]{1,0:T(8,128)(2,1)} %turn.6, pred[]{:T(512)S(6)} %eq.13), kind=kLoop, calls=%fused_computation.5 | loop fusion | flops 1048576 | bytes 5242882 | tf_op jit(solution)/shard_map/jit(_where)/select_n | solution.py:376
  80.0 6.9 %all-to-all-done.1.got_b_ref = bf16[32,136,128]{2,1,0:T(8,128)(2,1)S(1)} async-done(((bf16[32,136,128]{2,1,0:T(8,128)(2,1)}), bf16[32,136,128]{2,1,0:T(8,128)(2,1)S(1)}, u32[]{:S(2)}, u32[]{:S(2)}) %all-to-all-start.1) | async-done | bytes 1114144 | tf_op jit(solution)/shard_map/all_to_all | solution.py:356
  86.9 3.7 %update.8 = (bf16[8192,512]{1,0:T(8,128)(2,1)}, bf16[512,512]{1,0:T(8,128)(2,1)S(1)}) custom-call(s32[1]{0:T(128)} %bitcast.13.first_ref, bf16[32,136,128]{2,1,0:T(8,128)(2,1)S(1)} %all-to-all-done.got_a_ref, bf16[32,136,128]{2,1,0:T(8,128)(2,1)S(1)} %all-to-all-done.1.got_b_ref, bf16[8192,512]{1,0:T(8,128)(2,1)} %old_ref.15), custom_call_target="tpu_custom_call" | custom-call | flops 1073741824 | bytes 3801088 | tf_op jit(solution)/shard_map/update/pallas_call | solution.py:177
  90.6 5.0 %update.9 = (bf16[8192,512]{1,0:T(8,128)(2,1)}, bf16[1024,512]{1,0:T(8,128)(2,1)S(1)}) custom-call(s32[1]{0:T(128)} %bitcast.12.first_ref, bf16[32,136,128]{2,1,0:T(8,128)(2,1)S(1)} %all-to-all-done.got_a_ref, bf16[32,136,128]{2,1,0:T(8,128)(2,1)S(1)} %all-to-all-done.1.got_b_ref, bf16[8192,512]{1,0:T(8,128)(2,1)} %old_ref.15, ...), custom_call_target="tpu_custom_call", output_to_operand_aliasing={{0}: (4, {})} | custom-call | flops 2147483648 | bytes 5373952 | tf_op jit(solution)/shard_map/update/pallas_call | solution.py:177
  95.6 3.0 %collective-permute-start.15 = (bf16[1024,512]{1,0:T(8,128)(2,1)S(1)}, bf16[1024,512]{1,0:T(8,128)(2,1)S(1)}, u32[]{:S(2)}, u32[]{:S(2)}) collective-permute-start(bf16[1024,512]{1,0:T(8,128)(2,1)S(1)} %get-tuple-element.35), channel_id=1, source_target_pairs={{1,0},{0,1},{3,2},{2,3},{5,4},{4,5},{7,6},{6,7},{9,8},{8,9},{11,10... | collective-permute-start | bytes 3145736 | tf_op jit(solution)/shard_map/ppermute | solution.py:339
  98.5 5.0 %update.10 = (bf16[8192,512]{1,0:T(8,128)(2,1)}, bf16[1024,512]{1,0:T(8,128)(2,1)S(1)}) custom-call(s32[1]{0:T(128)} %bitcast.11.first_ref, bf16[32,136,128]{2,1,0:T(8,128)(2,1)S(1)} %all-to-all-done.got_a_ref, bf16[32,136,128]{2,1,0:T(8,128)(2,1)S(1)} %all-to-all-done.1.got_b_ref, bf16[8192,512]{1,0:T(8,128)(2,1)} %old_ref.15, ...), custom_call_target="tpu_custom_call", output_to_operand_aliasing={{0}: (4, {})} | custom-call | flops 2147483648 | bytes 5373952 | tf_op jit(solution)/shard_map/update/pallas_call | solution.py:177
  103.5 3.7 %update.11 = (bf16[8192,512]{1,0:T(8,128)(2,1)}, bf16[512,512]{1,0:T(8,128)(2,1)S(1)}) custom-call(s32[1]{0:T(128)} %bitcast.10.first_ref, bf16[32,136,128]{2,1,0:T(8,128)(2,1)S(1)} %all-to-all-done.got_a_ref, bf16[32,136,128]{2,1,0:T(8,128)(2,1)S(1)} %all-to-all-done.1.got_b_ref, bf16[8192,512]{1,0:T(8,128)(2,1)} %old_ref.15, ...), custom_call_target="tpu_custom_call", output_to_operand_aliasing={{0}: (4, {})} | custom-call | flops 1073741824 | bytes 3801088 | tf_op jit(solution)/shard_map/update/pallas_call | solution.py:177
  107.2 3.7 %update.12 = (bf16[8192,512]{1,0:T(8,128)(2,1)}, bf16[512,512]{1,0:T(8,128)(2,1)S(1)}) custom-call(s32[1]{0:T(128)} %bitcast.9.first_ref, bf16[32,136,128]{2,1,0:T(8,128)(2,1)S(1)} %all-to-all-done.got_a_ref, bf16[32,136,128]{2,1,0:T(8,128)(2,1)S(1)} %all-to-all-done.1.got_b_ref, bf16[8192,512]{1,0:T(8,128)(2,1)} %old_ref.15, ...), custom_call_target="tpu_custom_call", output_to_operand_aliasing={{0}: (4, {})} | custom-call | flops 1073741824 | bytes 3801088 | tf_op jit(solution)/shard_map/update/pallas_call | solution.py:177
  110.9 3.0 %update.13 = (bf16[8192,512]{1,0:T(8,128)(2,1)}, bf16[256,512]{1,0:T(8,128)(2,1)S(1)}) custom-call(s32[1]{0:T(128)} %bitcast.8.first_ref, bf16[32,136,128]{2,1,0:T(8,128)(2,1)S(1)} %all-to-all-done.got_a_ref, bf16[32,136,128]{2,1,0:T(8,128)(2,1)S(1)} %all-to-all-done.1.got_b_ref, bf16[8192,512]{1,0:T(8,128)(2,1)} %old_ref.15, ...), custom_call_target="tpu_custom_call", output_to_operand_aliasing={{0}: (4, {})} | custom-call | flops 536870912 | bytes 3014656 | tf_op jit(solution)/shard_map/update/pallas_call | solution.py:177
  113.9 3.0 %update.14 = (bf16[8192,512]{1,0:T(8,128)(2,1)}, bf16[256,512]{1,0:T(8,128)(2,1)S(1)}) custom-call(s32[1]{0:T(128)} %bitcast.7.first_ref, bf16[32,136,128]{2,1,0:T(8,128)(2,1)S(1)} %all-to-all-done.got_a_ref, bf16[32,136,128]{2,1,0:T(8,128)(2,1)S(1)} %all-to-all-done.1.got_b_ref, bf16[8192,512]{1,0:T(8,128)(2,1)} %old_ref.15, ...), custom_call_target="tpu_custom_call", output_to_operand_aliasing={{0}: (4, {})} | custom-call | flops 536870912 | bytes 3014656 | tf_op jit(solution)/shard_map/update/pallas_call | solution.py:177
  116.8 13.0 %update.15 = (bf16[8192,512]{1,0:T(8,128)(2,1)}, bf16[4096,512]{1,0:T(8,128)(2,1)S(1)}) custom-call(s32[1]{0:T(128)} %bitcast.first_ref, bf16[32,136,128]{2,1,0:T(8,128)(2,1)S(1)} %all-to-all-done.got_a_ref, bf16[32,136,128]{2,1,0:T(8,128)(2,1)S(1)} %all-to-all-done.1.got_b_ref, bf16[8192,512]{1,0:T(8,128)(2,1)} %old_ref.15, ...), custom_call_target="tpu_custom_call", output_to_operand_aliasing={{0}: (4, {})} | custom-call | flops 8589934592 | bytes 14811136 | tf_op jit(solution)/shard_map/update/pallas_call | solution.py:177
  129.8 3.0 %collective-permute-start.13 = (bf16[512,512]{1,0:T(8,128)(2,1)S(1)}, bf16[512,512]{1,0:T(8,128)(2,1)S(1)}, u32[]{:S(2)}, u32[]{:S(2)}) collective-permute-start(bf16[512,512]{1,0:T(8,128)(2,1)S(1)} %get-tuple-element.33), channel_id=1, source_target_pairs={{1,0},{0,1},{3,2},{2,3},{5,4},{4,5},{7,6},{6,7},{9,8},{8,9},{11,10... | collective-permute-start | bytes 1572872 | tf_op jit(solution)/shard_map/ppermute | solution.py:339
  132.9 2.9 %collective-permute-start.11 = (bf16[256,512]{1,0:T(8,128)(2,1)S(1)}, bf16[256,512]{1,0:T(8,128)(2,1)S(1)}, u32[]{:S(2)}, u32[]{:S(2)}) collective-permute-start(bf16[256,512]{1,0:T(8,128)(2,1)S(1)} %get-tuple-element.31), channel_id=1, source_target_pairs={{1,0},{0,1},{3,2},{2,3},{5,4},{4,5},{7,6},{6,7},{9,8},{8,9},{11,10... | collective-permute-start | bytes 786440 | tf_op jit(solution)/shard_map/ppermute | solution.py:339
  135.8 5.2 %search.7.refs_6_ = f32[8,3072]{1,0:T(8,128)S(1)} custom-call(bf16[4096,512]{1,0:T(8,128)(2,1)S(1)} %get-tuple-element.29.own_ref, bf16[512,512]{1,0:T(8,128)(2,1)S(1)} %collective-permute-done.16.other_ref, bf16[512,1024]{1,0:T(8,128)(2,1)S(1)} %turn.4.refs_0_, bf16[512,1024]{1,0:T(8,128)(2,1)S(1)} %copy-done.1, ...), custom_call_target="tpu_custom_call" | custom-call | flops 3221225472 | bytes 7340032 | tf_op jit(solution)/shard_map/search/pallas_call | solution.py:303
  141.4 8.4 %search.8.refs_6_ = f32[8,3072]{1,0:T(8,128)S(1)} custom-call(bf16[4096,512]{1,0:T(8,128)(2,1)S(1)} %get-tuple-element.29.own_ref, bf16[1024,512]{1,0:T(8,128)(2,1)S(1)} %collective-permute-done.15.other_ref, bf16[512,1024]{1,0:T(8,128)(2,1)S(1)} %turn.4.refs_0_, bf16[512,1024]{1,0:T(8,128)(2,1)S(1)} %copy-done.1, ...), custom_call_target="tpu_custom_call" | custom-call | flops 6442450944 | bytes 8388608 | tf_op jit(solution)/shard_map/search/pallas_call | solution.py:303
  149.8 1.1 collective-permute-done.14.other_ref
  151.0 8.4 %search.9.refs_6_ = f32[8,3072]{1,0:T(8,128)S(1)} custom-call(bf16[4096,512]{1,0:T(8,128)(2,1)S(1)} %get-tuple-element.29.own_ref, bf16[1024,512]{1,0:T(8,128)(2,1)S(1)} %collective-permute-done.14.other_ref, bf16[512,1024]{1,0:T(8,128)(2,1)S(1)} %turn.4.refs_0_, bf16[512,1024]{1,0:T(8,128)(2,1)S(1)} %copy-done.1, ...), custom_call_target="tpu_custom_call" | custom-call | flops 6442450944 | bytes 8388608 | tf_op jit(solution)/shard_map/search/pallas_call | solution.py:303
  159.4 2.8 %collective-permute-done.13.other_ref = bf16[512,512]{1,0:T(8,128)(2,1)S(1)} collective-permute-done((bf16[512,512]{1,0:T(8,128)(2,1)S(1)}, bf16[512,512]{1,0:T(8,128)(2,1)S(1)}, u32[]{:S(2)}, u32[]{:S(2)}) %collective-permute-start.13) | collective-permute-done | bytes 524320 | tf_op jit(solution)/shard_map/ppermute | solution.py:339
  162.2 5.2 %search.10.refs_6_ = f32[8,3072]{1,0:T(8,128)S(1)} custom-call(bf16[4096,512]{1,0:T(8,128)(2,1)S(1)} %get-tuple-element.29.own_ref, bf16[512,512]{1,0:T(8,128)(2,1)S(1)} %collective-permute-done.13.other_ref, bf16[512,1024]{1,0:T(8,128)(2,1)S(1)} %turn.4.refs_0_, bf16[512,1024]{1,0:T(8,128)(2,1)S(1)} %copy-done.1, ...), custom_call_target="tpu_custom_call" | custom-call | flops 3221225472 | bytes 7340032 | tf_op jit(solution)/shard_map/search/pallas_call | solution.py:303
  167.4 6.0 %collective-permute-done.12.other_ref = bf16[512,512]{1,0:T(8,128)(2,1)S(1)} collective-permute-done((bf16[512,512]{1,0:T(8,128)(2,1)S(1)}, bf16[512,512]{1,0:T(8,128)(2,1)S(1)}, u32[]{:S(2)}, u32[]{:S(2)}) %collective-permute-start.12) | collective-permute-done | bytes 524320 | tf_op jit(solution)/shard_map/ppermute | solution.py:339
  173.4 5.2 %search.11.refs_6_ = f32[8,3072]{1,0:T(8,128)S(1)} custom-call(bf16[4096,512]{1,0:T(8,128)(2,1)S(1)} %get-tuple-element.29.own_ref, bf16[512,512]{1,0:T(8,128)(2,1)S(1)} %collective-permute-done.12.other_ref, bf16[512,1024]{1,0:T(8,128)(2,1)S(1)} %turn.4.refs_0_, bf16[512,1024]{1,0:T(8,128)(2,1)S(1)} %copy-done.1, ...), custom_call_target="tpu_custom_call" | custom-call | flops 3221225472 | bytes 7340032 | tf_op jit(solution)/shard_map/search/pallas_call | solution.py:303
  179.0 3.4 %search.12.refs_6_ = f32[8,3072]{1,0:T(8,128)S(1)} custom-call(bf16[4096,512]{1,0:T(8,128)(2,1)S(1)} %get-tuple-element.29.own_ref, bf16[256,512]{1,0:T(8,128)(2,1)S(1)} %collective-permute-done.11.other_ref, bf16[512,1024]{1,0:T(8,128)(2,1)S(1)} %turn.4.refs_0_, bf16[512,1024]{1,0:T(8,128)(2,1)S(1)} %copy-done.1, ...), custom_call_target="tpu_custom_call" | custom-call | flops 1610612736 | bytes 6815744 | tf_op jit(solution)/shard_map/search/pallas_call | solution.py:303
  182.4 1.5 collective-permute-done.6.other_ref
  183.9 3.4 %search.13 = (f32[1,1024]{1,0:T(1,128)S(1)}, f32[1,1024]{1,0:T(1,128)S(1)}, f32[1,1024]{1,0:T(1,128)S(1)}) custom-call(bf16[4096,512]{1,0:T(8,128)(2,1)S(1)} %get-tuple-element.29.own_ref, bf16[256,512]{1,0:T(8,128)(2,1)S(1)} %collective-permute-done.6.other_ref, bf16[512,1024]{1,0:T(8,128)(2,1)S(1)} %turn.4.refs_0_, bf16[512,1024]{1,0:T(8,128)(2,1)S(1)} %copy-done.1, ...), custom_call_target="tpu_custom_call" | custom-call | flops 1610612736 | bytes 6815744 | tf_op jit(solution)/shard_map/search/pallas_call | solution.py:303
  187.8 0.7 collective-permute-done.17
  188.5 8.3 %collective-permute-start.19 = (f32[1024]{0:T(1024)S(1)}, f32[1024]{0:T(1024)S(1)}, u32[]{:S(2)}, u32[]{:S(2)}) collective-permute-start(f32[1024]{0:T(1024)S(1)} %get-tuple-element.45), channel_id=1, source_target_pairs={{124,0},{125,1},{126,2},{127,3},{0,4},{1,5},{2,6},{3,7},{4,8},{5,9... | collective-permute-start | bytes 12296 | tf_op jit(solution)/shard_map/ppermute | solution.py:339
  196.8 2.9 %collective-permute-start.20 = (f32[1024]{0:T(1024)S(1)}, f32[1024]{0:T(1024)S(1)}, u32[]{:S(2)}, u32[]{:S(2)}) collective-permute-start(f32[1024]{0:T(1024)S(1)} %get-tuple-element.45), channel_id=1, source_target_pairs={{125,0},{124,1},{127,2},{126,3},{1,4},{0,5},{3,6},{2,7},{5,8},{4,9... | collective-permute-start | bytes 12296 | tf_op jit(solution)/shard_map/ppermute | solution.py:339
  199.8 1.1 collective-permute-start.18
  201.2 2.6 %collective-permute-done.18 = f32[1024]{0:T(1024)S(1)} collective-permute-done((f32[1024]{0:T(1024)S(1)}, f32[1024]{0:T(1024)S(1)}, u32[]{:S(2)}, u32[]{:S(2)}) %collective-permute-start.18) | collective-permute-done | bytes 4128 | tf_op jit(solution)/shard_map/ppermute | solution.py:339
  (47 shorter events, 4.2 us)
Async XLA Ops:
  0.6 38.4 %copy-start.6 = (s32[1024,1]{0,1:T(1,128)S(1)}, s32[1024,1]{0,1:T(1,128)}, u32[]{:S(2)}) copy-start(s32[1024,1]{0,1:T(1,128)} %param.5) | copy-start | bytes 12292
  0.6 49.9 %copy-start.7 = (s32[1024]{0:T(1024)S(1)}, s32[1024]{0:T(1024)}, u32[]{:S(2)}) copy-start(s32[1024]{0:T(1024)} %param.6) | copy-start | bytes 12292
  0.6 26.9 %collective-permute-start.4 = (bf16[1024,512]{1,0:T(8,128)(2,1)}, bf16[1024,512]{1,0:T(8,128)(2,1)S(1)}, u32[]{:S(2)}, u32[]{:S(2)}) collective-permute-start(bf16[1024,512]{1,0:T(8,128)(2,1)} %refs_0_.1), channel_id=1, source_target_pairs={{5,0},{4,1},{7,2},{6,3},{1,4},{0,5},{3,6},{2,7},{13,8},{12,9},{15,... | collective-permute-start | bytes 3145736 | tf_op jit(solution)/shard_map/ppermute | solution.py:339
  4.5 26.0 %collective-permute-start.2 = (bf16[1024,512]{1,0:T(8,128)(2,1)}, bf16[1024,512]{1,0:T(8,128)(2,1)S(1)}, u32[]{:S(2)}, u32[]{:S(2)}) collective-permute-start(bf16[1024,512]{1,0:T(8,128)(2,1)} %refs_0_.1), channel_id=1, source_target_pairs={{4,0},{5,1},{6,2},{7,3},{0,4},{1,5},{2,6},{3,7},{12,8},{13,9},{14,... | collective-permute-start | bytes 3145736 | tf_op jit(solution)/shard_map/ppermute | solution.py:339
  8.5 49.4 %all-to-all-start = ((bf16[32,136,128]{2,1,0:T(8,128)(2,1)}), bf16[32,136,128]{2,1,0:T(8,128)(2,1)S(1)}, u32[]{:S(2)}, u32[]{:S(2)}) async-start(bf16[32,136,128]{2,1,0:T(8,128)(2,1)} %pack.2), calls=%async_computation | async-start | bytes 2228224 | tf_op jit(solution)/shard_map/all_to_all | solution.py:356
  28.9 44.6 %collective-permute-start.9 = (bf16[512,1024]{1,0:T(8,128)(2,1)}, bf16[512,1024]{1,0:T(8,128)(2,1)}, u32[]{:S(2)}, u32[]{:S(2)}) collective-permute-start(bf16[512,1024]{1,0:T(8,128)(2,1)} %turn.7), channel_id=1, source_target_pairs={{12,4},{13,5},{14,6},{15,7},{20,12},{21,13},{22,14},{23,15},{28,20... | collective-permute-start | bytes 3145736 | tf_op jit(solution)/shard_map/ppermute | solution.py:339
  30.5 22.8 %copy-start.4 = (bf16[1024,512]{1,0:T(8,128)(2,1)}, bf16[1024,512]{1,0:T(8,128)(2,1)S(1)}, u32[]{:S(2)}) copy-start(bf16[1024,512]{1,0:T(8,128)(2,1)S(1)} %collective-permute-done.2.pts_ref.refs_0_) | copy-start | bytes 3145732
  31.9 45.1 %collective-permute-start.7 = (bf16[512,1024]{1,0:T(8,128)(2,1)}, bf16[512,1024]{1,0:T(8,128)(2,1)}, u32[]{:S(2)}, u32[]{:S(2)}) collective-permute-start(bf16[512,1024]{1,0:T(8,128)(2,1)} %turn.6), channel_id=1, source_target_pairs={{12,4},{13,5},{14,6},{15,7},{20,12},{21,13},{22,14},{23,15},{28,20... | collective-permute-start | bytes 3145736 | tf_op jit(solution)/shard_map/ppermute | solution.py:339
  34.4 37.7 %collective-permute-start.3 = (bf16[512,512]{1,0:T(8,128)(2,1)}, bf16[512,512]{1,0:T(8,128)(2,1)}, u32[]{:S(2)}, u32[]{:S(2)}) collective-permute-start(bf16[512,512]{1,0:T(8,128)(2,1)} %slice.8), channel_id=1, source_target_pairs={{5,0},{4,1},{7,2},{6,3},{1,4},{0,5},{3,6},{2,7},{13,8},{12,9},{15,... | collective-permute-start | bytes 1572872 | tf_op jit(solution)/shard_map/ppermute | solution.py:339
  39.0 33.1 %collective-permute-start.5 = (bf16[512,512]{1,0:T(8,128)(2,1)}, bf16[512,512]{1,0:T(8,128)(2,1)}, u32[]{:S(2)}, u32[]{:S(2)}) collective-permute-start(bf16[512,512]{1,0:T(8,128)(2,1)} %slice.9), channel_id=1, source_target_pairs={{4,0},{5,1},{6,2},{7,3},{0,4},{1,5},{2,6},{3,7},{12,8},{13,9},{14,... | collective-permute-start | bytes 1572872 | tf_op jit(solution)/shard_map/ppermute | solution.py:339
  39.0 11.5 %collective-permute-start = (s32[1024,1]{0,1:T(1,128)S(1)}, s32[1024,1]{0,1:T(1,128)S(1)}, u32[]{:S(2)}, u32[]{:S(2)}) collective-permute-start(s32[1024,1]{0,1:T(1,128)S(1)} %copy-done.6), channel_id=1, source_target_pairs={{4,0},{5,1},{6,2},{7,3},{0,4},{1,5},{2,6},{3,7},{12,8},{13,9},{14,... | collective-permute-start | bytes 12296 | tf_op jit(solution)/shard_map/ppermute | solution.py:339
  50.5 2.8 %copy-start.8 = (s32[1024,1]{0,1:T(1,128)}, s32[1024,1]{0,1:T(1,128)S(1)}, u32[]{:S(2)}) copy-start(s32[1024,1]{0,1:T(1,128)S(1)} %collective-permute-done) | copy-start | bytes 12292
  50.5 2.8 %collective-permute-start.1 = (s32[1024]{0:T(1024)S(1)}, s32[1024]{0:T(1024)S(1)}, u32[]{:S(2)}, u32[]{:S(2)}) collective-permute-start(s32[1024]{0:T(1024)S(1)} %copy-done.7), channel_id=1, source_target_pairs={{4,0},{5,1},{6,2},{7,3},{0,4},{1,5},{2,6},{3,7},{12,8},{13,9},{14,... | collective-permute-start | bytes 12296 | tf_op jit(solution)/shard_map/ppermute | solution.py:339
  53.3 0.6 copy-start.9
  57.8 29.0 %all-to-all-start.1 = ((bf16[32,136,128]{2,1,0:T(8,128)(2,1)}), bf16[32,136,128]{2,1,0:T(8,128)(2,1)S(1)}, u32[]{:S(2)}, u32[]{:S(2)}) async-start(bf16[32,136,128]{2,1,0:T(8,128)(2,1)} %pack.3), calls=%async_computation.1 | async-start | bytes 2228224 | tf_op jit(solution)/shard_map/all_to_all | solution.py:356
  70.3 1.2 copy-start.5
  73.5 6.3 %copy-start = (bf16[512,1024]{1,0:T(8,128)(2,1)}, bf16[512,1024]{1,0:T(8,128)(2,1)S(1)}, u32[]{:S(2)}) copy-start(bf16[512,1024]{1,0:T(8,128)(2,1)S(1)} %turn.5.refs_1_) | copy-start | bytes 3145732
  76.6 56.1 %collective-permute-start.10 = (bf16[512,1024]{1,0:T(8,128)(2,1)}, bf16[512,1024]{1,0:T(8,128)(2,1)}, u32[]{:S(2)}, u32[]{:S(2)}) collective-permute-start(bf16[512,1024]{1,0:T(8,128)(2,1)} %get-tuple-element.40), channel_id=1, source_target_pairs={{2,0},{3,1},{0,2},{1,3},{6,4},{7,5},{4,6},{5,7},{10,8},{11,9},{8,1... | collective-permute-start | bytes 3145736 | tf_op jit(solution)/shard_map/ppermute | solution.py:339
  79.8 53.0 %collective-permute-start.8 = (bf16[512,1024]{1,0:T(8,128)(2,1)}, bf16[512,1024]{1,0:T(8,128)(2,1)}, u32[]{:S(2)}, u32[]{:S(2)}) collective-permute-start(bf16[512,1024]{1,0:T(8,128)(2,1)} %get-tuple-element.42), channel_id=1, source_target_pairs={{2,0},{3,1},{0,2},{1,3},{6,4},{7,5},{4,6},{5,7},{10,8},{11,9},{8,1... | collective-permute-start | bytes 3145736 | tf_op jit(solution)/shard_map/ppermute | solution.py:339
  90.6 39.3 %collective-permute-start.16 = (bf16[512,512]{1,0:T(8,128)(2,1)S(1)}, bf16[512,512]{1,0:T(8,128)(2,1)S(1)}, u32[]{:S(2)}, u32[]{:S(2)}) collective-permute-start(bf16[512,512]{1,0:T(8,128)(2,1)S(1)} %get-tuple-element.36), channel_id=1, source_target_pairs={{1,0},{0,1},{3,2},{2,3},{5,4},{4,5},{7,6},{6,7},{9,8},{8,9},{11,10... | collective-permute-start | bytes 1572872 | tf_op jit(solution)/shard_map/ppermute | solution.py:339
  95.6 45.4 %collective-permute-start.15 = (bf16[1024,512]{1,0:T(8,128)(2,1)S(1)}, bf16[1024,512]{1,0:T(8,128)(2,1)S(1)}, u32[]{:S(2)}, u32[]{:S(2)}) collective-permute-start(bf16[1024,512]{1,0:T(8,128)(2,1)S(1)} %get-tuple-element.35), channel_id=1, source_target_pairs={{1,0},{0,1},{3,2},{2,3},{5,4},{4,5},{7,6},{6,7},{9,8},{8,9},{11,10... | collective-permute-start | bytes 3145736 | tf_op jit(solution)/shard_map/ppermute | solution.py:339
  103.5 47.4 %collective-permute-start.14 = (bf16[1024,512]{1,0:T(8,128)(2,1)S(1)}, bf16[1024,512]{1,0:T(8,128)(2,1)S(1)}, u32[]{:S(2)}, u32[]{:S(2)}) collective-permute-start(bf16[1024,512]{1,0:T(8,128)(2,1)S(1)} %get-tuple-element.34), channel_id=1, source_target_pairs={{1,0},{0,1},{3,2},{2,3},{5,4},{4,5},{7,6},{6,7},{9,8},{8,9},{11,10... | collective-permute-start | bytes 3145736 | tf_op jit(solution)/shard_map/ppermute | solution.py:339
  116.8 18.9 %copy-start.1 = (bf16[512,1024]{1,0:T(8,128)(2,1)S(1)}, bf16[512,1024]{1,0:T(8,128)(2,1)}, u32[]{:S(2)}) copy-start(bf16[512,1024]{1,0:T(8,128)(2,1)} %copy-done) | copy-start | bytes 3145732
  116.8 18.9 %copy-start.2 = (bf16[512,1024]{1,0:T(8,128)(2,1)S(1)}, bf16[512,1024]{1,0:T(8,128)(2,1)}, u32[]{:S(2)}) copy-start(bf16[512,1024]{1,0:T(8,128)(2,1)} %get-tuple-element.41.refs_5_) | copy-start | bytes 3145732
  116.8 18.9 %copy-start.3 = (bf16[512,1024]{1,0:T(8,128)(2,1)S(1)}, bf16[512,1024]{1,0:T(8,128)(2,1)}, u32[]{:S(2)}) copy-start(bf16[512,1024]{1,0:T(8,128)(2,1)} %get-tuple-element.43.refs_4_) | copy-start | bytes 3145732
  129.8 32.4 %collective-permute-start.13 = (bf16[512,512]{1,0:T(8,128)(2,1)S(1)}, bf16[512,512]{1,0:T(8,128)(2,1)S(1)}, u32[]{:S(2)}, u32[]{:S(2)}) collective-permute-start(bf16[512,512]{1,0:T(8,128)(2,1)S(1)} %get-tuple-element.33), channel_id=1, source_target_pairs={{1,0},{0,1},{3,2},{2,3},{5,4},{4,5},{7,6},{6,7},{9,8},{8,9},{11,10... | collective-permute-start | bytes 1572872 | tf_op jit(solution)/shard_map/ppermute | solution.py:339
  132.8 40.6 %collective-permute-start.12 = (bf16[512,512]{1,0:T(8,128)(2,1)S(1)}, bf16[512,512]{1,0:T(8,128)(2,1)S(1)}, u32[]{:S(2)}, u32[]{:S(2)}) collective-permute-start(bf16[512,512]{1,0:T(8,128)(2,1)S(1)} %get-tuple-element.32), channel_id=1, source_target_pairs={{1,0},{0,1},{3,2},{2,3},{5,4},{4,5},{7,6},{6,7},{9,8},{8,9},{11,10... | collective-permute-start | bytes 1572872 | tf_op jit(solution)/shard_map/ppermute | solution.py:339
  132.9 46.2 %collective-permute-start.11 = (bf16[256,512]{1,0:T(8,128)(2,1)S(1)}, bf16[256,512]{1,0:T(8,128)(2,1)S(1)}, u32[]{:S(2)}, u32[]{:S(2)}) collective-permute-start(bf16[256,512]{1,0:T(8,128)(2,1)S(1)} %get-tuple-element.31), channel_id=1, source_target_pairs={{1,0},{0,1},{3,2},{2,3},{5,4},{4,5},{7,6},{6,7},{9,8},{8,9},{11,10... | collective-permute-start | bytes 786440 | tf_op jit(solution)/shard_map/ppermute | solution.py:339
  141.0 42.9 %collective-permute-start.6 = (bf16[256,512]{1,0:T(8,128)(2,1)S(1)}, bf16[256,512]{1,0:T(8,128)(2,1)S(1)}, u32[]{:S(2)}, u32[]{:S(2)}) collective-permute-start(bf16[256,512]{1,0:T(8,128)(2,1)S(1)} %get-tuple-element.30), channel_id=1, source_target_pairs={{1,0},{0,1},{3,2},{2,3},{5,4},{4,5},{7,6},{6,7},{9,8},{8,9},{11,10... | collective-permute-start | bytes 786440 | tf_op jit(solution)/shard_map/ppermute | solution.py:339
  187.3 1.2 collective-permute-start.17
  188.5 15.2 %collective-permute-start.19 = (f32[1024]{0:T(1024)S(1)}, f32[1024]{0:T(1024)S(1)}, u32[]{:S(2)}, u32[]{:S(2)}) collective-permute-start(f32[1024]{0:T(1024)S(1)} %get-tuple-element.45), channel_id=1, source_target_pairs={{124,0},{125,1},{126,2},{127,3},{0,4},{1,5},{2,6},{3,7},{4,8},{5,9... | collective-permute-start | bytes 12296 | tf_op jit(solution)/shard_map/ppermute | solution.py:339
  196.8 6.9 %collective-permute-start.20 = (f32[1024]{0:T(1024)S(1)}, f32[1024]{0:T(1024)S(1)}, u32[]{:S(2)}, u32[]{:S(2)}) collective-permute-start(f32[1024]{0:T(1024)S(1)} %get-tuple-element.45), channel_id=1, source_target_pairs={{125,0},{124,1},{127,2},{126,3},{1,4},{0,5},{3,6},{2,7},{5,8},{4,9... | collective-permute-start | bytes 12296 | tf_op jit(solution)/shard_map/ppermute | solution.py:339
  199.8 4.0 %collective-permute-start.18 = (f32[1024]{0:T(1024)S(1)}, f32[1024]{0:T(1024)S(1)}, u32[]{:S(2)}, u32[]{:S(2)}) collective-permute-start(f32[1024]{0:T(1024)S(1)} %get-tuple-element.44), channel_id=1, source_target_pairs={{1,0},{0,1},{3,2},{2,3},{5,4},{4,5},{7,6},{6,7},{9,8},{8,9},{11,10... | collective-permute-start | bytes 12296 | tf_op jit(solution)/shard_map/ppermute | solution.py:339

commit v4 on v3

--- a/solution.py
+++ b/solution.py
@@ -15,7 +15,7 @@
 TILE = 256
 CHUNKS = (512, 1024, 1024, 512, 512, 256, 256)
 COLS = 512
-PACK_STEPS = 2
+PACK_STEPS = 1
 BF16 = jnp.bfloat16
 F32 = jnp.float32
 I32 = jnp.int32
@@ -85,7 +85,7 @@
                 ]
 
 
-def pack(lane, plane, block, member, points, owners, slots):
+def pack(lane, plane, block, member, points, owners, slots, limit):
     count, width = points.shape
     rows = slots * (width // LANES) + META
     group = owners // PACK_STEPS
@@ -108,7 +108,7 @@
             pltpu.VMEM((owners, LANES), F32),
         ],
         compiler_params=pltpu.CompilerParams(
-            dimension_semantics=("arbitrary",), vmem_limit_bytes=60 << 20
+            dimension_semantics=("arbitrary",), vmem_limit_bytes=limit
         ),
         cost_estimate=pl.CostEstimate(
             flops=2 * owners * slots * count * width, bytes_accessed=4 << 20, transcendentals=0
@@ -349,16 +349,18 @@
     lane = ((spot % (LANES // slots)) * slots).astype(I32).reshape(1)
     plane = ((mine // 2) % 2).astype(I32).reshape(1)
 
-    def deliver(owner, member, rows):
+    def deliver(owner, member, rows, limit):
         sent = pack(
-            lane, plane, owner.reshape(1, count), member.reshape(1, count), rows, owners, slots
+            lane, plane, owner.reshape(1, count), member.reshape(1, count), rows, owners, slots, limit
         )
         return lax.all_to_all(
             sent, "blk", split_axis=0, concat_axis=0, axis_index_groups=planes, tiled=True
         )
 
-    near_rows = pltpu.with_memory_space_constraint(near_own, pltpu.HBM)
-    got = [deliver(owner, member, points), deliver(near_owner, near_member, near_rows)]
+    got = [
+        deliver(owner, member, points, 60 << 20),
+        deliver(near_owner, near_member, near_own, 20 << 20),
+    ]
 
     own_0 = turn(points)
     half = count // 2

time: 208 us -> 209 us (level)
  starting transfers between devices: 55.6 us -> 58.5 us
    ppermute x21, starting transfers between devices: 35.1 us -> 38 us  [fetch(): return lax.ppermute(x, both, route)]
  transfers between devices with their start and end apart: 23 -> 23, of which waited for: 11 -> 11; matrix products, arithmetic and copies ran while one was open for 4% -> 4% of each run, Pallas kernels for 43% -> 42%
where the time goes in v4:
time: 209 us; the launch traced here: 205 us
  Pallas kernels  90.3 us (43%)
  starting transfers between devices  58.5 us (28%)
  waiting for transfers between devices  45.6 us (22%)
  other arithmetic  7.04 us (3%)
  local copies, waits for them, and re-layouts  2.93 us (1%)
    pallas_call x8, Pallas kernels, update(): pl.pallas_call(functools.partial(update_kernel, owners=owners, slots=slot...  40 us
    pallas_call x7, Pallas kernels, search(): pl.pallas_call(functools.partial(search_kernel, first=before is None, las...  39.2 us
    ppermute x21, waiting for transfers between devices, fetch(): return lax.ppermute(x, both, route)  38.7 us
    ppermute x21, starting transfers between devices, fetch(): return lax.ppermute(x, both, route)  38 us
    all_to_all x2, starting transfers between devices, deliver(): lax.all_to_all(sent, 'blk', split_axis=0, concat_axis=0, axis_index_group...  20.5 us
    all_to_all x2, waiting for transfers between devices, deliver(): lax.all_to_all(sent, 'blk', split_axis=0, concat_axis=0, axis_index_group...  6.88 us
    pallas_call x2, Pallas kernels, pack(): pl.pallas_call(functools.partial(pack_kernel, slots=slots), out_shape=jax...  6.52 us
    pallas_call x4, Pallas kernels, turn(): pl.pallas_call(turn_kernel, out_shape=jax.ShapeDtypeStruct((width, count)...  4.59 us
  transfers between devices with their start and end apart: 23, of which 11 were waited for; matrix products, arithmetic and copies ran while one was open for 4% of the time, Pallas kernels for 42%

profile of v4, /device:TPU:7, one launch (start us, length us, event | category | flops | bytes accessed | tf_op | source)
XLA Modules:
  0.0 205.2 jit_solution(2185886112545034910)
XLA Ops:
  0.6 3.8 %collective-permute-start.4 = (bf16[1024,512]{1,0:T(8,128)(2,1)}, bf16[1024,512]{1,0:T(8,128)(2,1)S(1)}, u32[]{:S(2)}, u32[]{:S(2)}) collective-permute-start(bf16[1024,512]{1,0:T(8,128)(2,1)} %refs_0_.1), channel_id=1, source_target_pairs={{5,0},{4,1},{7,2},{6,3},{1,4},{0,5},{3,6},{2,7},{13,8},{12,9},{15,... | collective-permute-start | bytes 3145736 | tf_op jit(solution)/shard_map/ppermute | solution.py:339
  4.5 3.9 %pack.2 = bf16[32,136,128]{2,1,0:T(8,128)(2,1)} custom-call(s32[1]{0:T(128)} %bitcast.1.lane_ref, s32[1]{0:T(128)} %bitcast.2.plane_ref, s32[1,1024]{1,0:T(1,128)} %bitcast.22, s32[1,1024]{1,0:T(1,128)} %bitcast.23, bf16[1024,512]{1,0:T(8,128)(2,1)} %refs_0_.1), custom_call_target="tpu_custom_call" | custom-call | flops 1073741824 | bytes 4194304 | tf_op jit(solution)/shard_map/pack/pallas_call | solution.py:93
  8.4 8.1 %all-to-all-start = ((bf16[32,136,128]{2,1,0:T(8,128)(2,1)}), bf16[32,136,128]{2,1,0:T(8,128)(2,1)S(1)}, u32[]{:S(2)}, u32[]{:S(2)}) async-start(bf16[32,136,128]{2,1,0:T(8,128)(2,1)} %pack.2), calls=%async_computation | async-start | bytes 2228224 | tf_op jit(solution)/shard_map/all_to_all | solution.py:356
  16.5 11.0 %collective-permute-done.4.refs_0_ = bf16[1024,512]{1,0:T(8,128)(2,1)S(1)} collective-permute-done((bf16[1024,512]{1,0:T(8,128)(2,1)}, bf16[1024,512]{1,0:T(8,128)(2,1)S(1)}, u32[]{:S(2)}, u32[]{:S(2)}) %collective-permute-start.4) | collective-permute-done | bytes 1048608 | tf_op jit(solution)/shard_map/ppermute | solution.py:339
  27.6 1.3 turn.7
  28.9 1.7 collective-permute-start.9
  30.6 1.3 turn.6
  31.9 1.6 collective-permute-start.7
  33.5 0.9 slice.8
  34.3 3.7 %collective-permute-start.3 = (bf16[512,512]{1,0:T(8,128)(2,1)}, bf16[512,512]{1,0:T(8,128)(2,1)}, u32[]{:S(2)}, u32[]{:S(2)}) collective-permute-start(bf16[512,512]{1,0:T(8,128)(2,1)} %slice.8), channel_id=1, source_target_pairs={{5,0},{4,1},{7,2},{6,3},{1,4},{0,5},{3,6},{2,7},{13,8},{12,9},{15,... | collective-permute-start | bytes 1572872 | tf_op jit(solution)/shard_map/ppermute | solution.py:339
  38.1 0.8 slice.9
  38.9 1.5 collective-permute-start
  40.4 10.0 %collective-permute-done = s32[1024,1]{0,1:T(1,128)S(1)} collective-permute-done((s32[1024,1]{0,1:T(1,128)S(1)}, s32[1024,1]{0,1:T(1,128)S(1)}, u32[]{:S(2)}, u32[]{:S(2)}) %collective-permute-start) | collective-permute-done | bytes 4128 | tf_op jit(solution)/shard_map/ppermute | solution.py:339
  50.7 2.5 %collective-permute-done.1 = s32[1024]{0:T(1024)S(1)} collective-permute-done((s32[1024]{0:T(1024)S(1)}, s32[1024]{0:T(1024)S(1)}, u32[]{:S(2)}, u32[]{:S(2)}) %collective-permute-start.1) | collective-permute-done | bytes 4128 | tf_op jit(solution)/shard_map/ppermute | solution.py:339
  53.2 2.6 %pack.3 = bf16[32,136,128]{2,1,0:T(8,128)(2,1)} custom-call(s32[1]{0:T(128)} %bitcast.1.lane_ref, s32[1]{0:T(128)} %bitcast.2.plane_ref, s32[1,1024]{1,0:T(1,128)S(1)} %bitcast.20, s32[1,1024]{1,0:T(1,128)S(1)} %bitcast.21, bf16[1024,512]{1,0:T(8,128)(2,1)S(1)} %collective-permute-done.2.pts_ref.refs_0_), custom_call_target="tpu_custom_call" | custom-call | flops 1073741824 | bytes 4194304 | tf_op jit(solution)/shard_map/pack/pallas_call | solution.py:93
  55.8 12.4 %all-to-all-start.1 = ((bf16[32,136,128]{2,1,0:T(8,128)(2,1)}), bf16[32,136,128]{2,1,0:T(8,128)(2,1)S(1)}, u32[]{:S(2)}, u32[]{:S(2)}) async-start(bf16[32,136,128]{2,1,0:T(8,128)(2,1)} %pack.3), calls=%async_computation.1 | async-start | bytes 2228224 | tf_op jit(solution)/shard_map/all_to_all | solution.py:356
  68.3 1.2 copy-done.4
  70.1 1.5 turn.5.refs_1_
  71.6 3.1 %broadcast_select_fusion.2 = (bf16[512,1024]{1,0:T(8,128)(2,1)}, bf16[512,1024]{1,0:T(8,128)(2,1)}) fusion(bf16[512,1024]{1,0:T(8,128)(2,1)S(1)} %turn.5.refs_1_, pred[]{:T(512)S(6)} %eq.12, bf16[512,1024]{1,0:T(8,128)(2,1)} %collective-permute-done.9, bf16[512,1024]{1,0:T(8,128)(2,1)} %turn.7, pred[]{:T(512)S(6)} %eq.13), kind=kLoop, calls=%fused_computation.4 | loop fusion | flops 1048576 | bytes 5242882 | tf_op jit(solution)/shard_map/jit(_where)/select_n | solution.py:379
  75.1 2.8 %broadcast_select_fusion.3 = (bf16[512,1024]{1,0:T(8,128)(2,1)}, bf16[512,1024]{1,0:T(8,128)(2,1)}) fusion(bf16[512,1024]{1,0:T(8,128)(2,1)S(1)} %turn.4.refs_0_, pred[]{:T(512)S(6)} %eq.12, bf16[512,1024]{1,0:T(8,128)(2,1)} %collective-permute-done.7, bf16[512,1024]{1,0:T(8,128)(2,1)} %turn.6, pred[]{:T(512)S(6)} %eq.13), kind=kLoop, calls=%fused_computation.5 | loop fusion | flops 1048576 | bytes 5242882 | tf_op jit(solution)/shard_map/jit(_where)/select_n | solution.py:378
  78.0 6.9 %all-to-all-done.1.got_b_ref = bf16[32,136,128]{2,1,0:T(8,128)(2,1)S(1)} async-done(((bf16[32,136,128]{2,1,0:T(8,128)(2,1)}), bf16[32,136,128]{2,1,0:T(8,128)(2,1)S(1)}, u32[]{:S(2)}, u32[]{:S(2)}) %all-to-all-start.1) | async-done | bytes 1114144 | tf_op jit(solution)/shard_map/all_to_all | solution.py:356
  84.9 3.7 %update.8 = (bf16[8192,512]{1,0:T(8,128)(2,1)}, bf16[512,512]{1,0:T(8,128)(2,1)S(1)}) custom-call(s32[1]{0:T(128)} %bitcast.13.first_ref, bf16[32,136,128]{2,1,0:T(8,128)(2,1)S(1)} %all-to-all-done.got_a_ref, bf16[32,136,128]{2,1,0:T(8,128)(2,1)S(1)} %all-to-all-done.1.got_b_ref, bf16[8192,512]{1,0:T(8,128)(2,1)} %old_ref.15), custom_call_target="tpu_custom_call" | custom-call | flops 1073741824 | bytes 3801088 | tf_op jit(solution)/shard_map/update/pallas_call | solution.py:177
  88.6 5.0 %update.9 = (bf16[8192,512]{1,0:T(8,128)(2,1)}, bf16[1024,512]{1,0:T(8,128)(2,1)S(1)}) custom-call(s32[1]{0:T(128)} %bitcast.12.first_ref, bf16[32,136,128]{2,1,0:T(8,128)(2,1)S(1)} %all-to-all-done.got_a_ref, bf16[32,136,128]{2,1,0:T(8,128)(2,1)S(1)} %all-to-all-done.1.got_b_ref, bf16[8192,512]{1,0:T(8,128)(2,1)} %old_ref.15, ...), custom_call_target="tpu_custom_call", output_to_operand_aliasing={{0}: (4, {})} | custom-call | flops 2147483648 | bytes 5373952 | tf_op jit(solution)/shard_map/update/pallas_call | solution.py:177
  93.6 3.0 %collective-permute-start.15 = (bf16[1024,512]{1,0:T(8,128)(2,1)S(1)}, bf16[1024,512]{1,0:T(8,128)(2,1)S(1)}, u32[]{:S(2)}, u32[]{:S(2)}) collective-permute-start(bf16[1024,512]{1,0:T(8,128)(2,1)S(1)} %get-tuple-element.35), channel_id=1, source_target_pairs={{1,0},{0,1},{3,2},{2,3},{5,4},{4,5},{7,6},{6,7},{9,8},{8,9},{11,10... | collective-permute-start | bytes 3145736 | tf_op jit(solution)/shard_map/ppermute | solution.py:339
  96.5 5.0 %update.10 = (bf16[8192,512]{1,0:T(8,128)(2,1)}, bf16[1024,512]{1,0:T(8,128)(2,1)S(1)}) custom-call(s32[1]{0:T(128)} %bitcast.11.first_ref, bf16[32,136,128]{2,1,0:T(8,128)(2,1)S(1)} %all-to-all-done.got_a_ref, bf16[32,136,128]{2,1,0:T(8,128)(2,1)S(1)} %all-to-all-done.1.got_b_ref, bf16[8192,512]{1,0:T(8,128)(2,1)} %old_ref.15, ...), custom_call_target="tpu_custom_call", output_to_operand_aliasing={{0}: (4, {})} | custom-call | flops 2147483648 | bytes 5373952 | tf_op jit(solution)/shard_map/update/pallas_call | solution.py:177
  101.5 3.7 %update.11 = (bf16[8192,512]{1,0:T(8,128)(2,1)}, bf16[512,512]{1,0:T(8,128)(2,1)S(1)}) custom-call(s32[1]{0:T(128)} %bitcast.10.first_ref, bf16[32,136,128]{2,1,0:T(8,128)(2,1)S(1)} %all-to-all-done.got_a_ref, bf16[32,136,128]{2,1,0:T(8,128)(2,1)S(1)} %all-to-all-done.1.got_b_ref, bf16[8192,512]{1,0:T(8,128)(2,1)} %old_ref.15, ...), custom_call_target="tpu_custom_call", output_to_operand_aliasing={{0}: (4, {})} | custom-call | flops 1073741824 | bytes 3801088 | tf_op jit(solution)/shard_map/update/pallas_call | solution.py:177
  105.2 3.7 %update.12 = (bf16[8192,512]{1,0:T(8,128)(2,1)}, bf16[512,512]{1,0:T(8,128)(2,1)S(1)}) custom-call(s32[1]{0:T(128)} %bitcast.9.first_ref, bf16[32,136,128]{2,1,0:T(8,128)(2,1)S(1)} %all-to-all-done.got_a_ref, bf16[32,136,128]{2,1,0:T(8,128)(2,1)S(1)} %all-to-all-done.1.got_b_ref, bf16[8192,512]{1,0:T(8,128)(2,1)} %old_ref.15, ...), custom_call_target="tpu_custom_call", output_to_operand_aliasing={{0}: (4, {})} | custom-call | flops 1073741824 | bytes 3801088 | tf_op jit(solution)/shard_map/update/pallas_call | solution.py:177
  108.9 3.0 %update.13 = (bf16[8192,512]{1,0:T(8,128)(2,1)}, bf16[256,512]{1,0:T(8,128)(2,1)S(1)}) custom-call(s32[1]{0:T(128)} %bitcast.8.first_ref, bf16[32,136,128]{2,1,0:T(8,128)(2,1)S(1)} %all-to-all-done.got_a_ref, bf16[32,136,128]{2,1,0:T(8,128)(2,1)S(1)} %all-to-all-done.1.got_b_ref, bf16[8192,512]{1,0:T(8,128)(2,1)} %old_ref.15, ...), custom_call_target="tpu_custom_call", output_to_operand_aliasing={{0}: (4, {})} | custom-call | flops 536870912 | bytes 3014656 | tf_op jit(solution)/shard_map/update/pallas_call | solution.py:177
  111.9 3.0 %update.14 = (bf16[8192,512]{1,0:T(8,128)(2,1)}, bf16[256,512]{1,0:T(8,128)(2,1)S(1)}) custom-call(s32[1]{0:T(128)} %bitcast.7.first_ref, bf16[32,136,128]{2,1,0:T(8,128)(2,1)S(1)} %all-to-all-done.got_a_ref, bf16[32,136,128]{2,1,0:T(8,128)(2,1)S(1)} %all-to-all-done.1.got_b_ref, bf16[8192,512]{1,0:T(8,128)(2,1)} %old_ref.15, ...), custom_call_target="tpu_custom_call", output_to_operand_aliasing={{0}: (4, {})} | custom-call | flops 536870912 | bytes 3014656 | tf_op jit(solution)/shard_map/update/pallas_call | solution.py:177
  114.9 13.0 %update.15 = (bf16[8192,512]{1,0:T(8,128)(2,1)}, bf16[4096,512]{1,0:T(8,128)(2,1)S(1)}) custom-call(s32[1]{0:T(128)} %bitcast.first_ref, bf16[32,136,128]{2,1,0:T(8,128)(2,1)S(1)} %all-to-all-done.got_a_ref, bf16[32,136,128]{2,1,0:T(8,128)(2,1)S(1)} %all-to-all-done.1.got_b_ref, bf16[8192,512]{1,0:T(8,128)(2,1)} %old_ref.15, ...), custom_call_target="tpu_custom_call", output_to_operand_aliasing={{0}: (4, {})} | custom-call | flops 8589934592 | bytes 14811136 | tf_op jit(solution)/shard_map/update/pallas_call | solution.py:177
  127.8 3.0 %collective-permute-start.13 = (bf16[512,512]{1,0:T(8,128)(2,1)S(1)}, bf16[512,512]{1,0:T(8,128)(2,1)S(1)}, u32[]{:S(2)}, u32[]{:S(2)}) collective-permute-start(bf16[512,512]{1,0:T(8,128)(2,1)S(1)} %get-tuple-element.33), channel_id=1, source_target_pairs={{1,0},{0,1},{3,2},{2,3},{5,4},{4,5},{7,6},{6,7},{9,8},{8,9},{11,10... | collective-permute-start | bytes 1572872 | tf_op jit(solution)/shard_map/ppermute | solution.py:339
  130.9 2.9 %collective-permute-start.11 = (bf16[256,512]{1,0:T(8,128)(2,1)S(1)}, bf16[256,512]{1,0:T(8,128)(2,1)S(1)}, u32[]{:S(2)}, u32[]{:S(2)}) collective-permute-start(bf16[256,512]{1,0:T(8,128)(2,1)S(1)} %get-tuple-element.31), channel_id=1, source_target_pairs={{1,0},{0,1},{3,2},{2,3},{5,4},{4,5},{7,6},{6,7},{9,8},{8,9},{11,10... | collective-permute-start | bytes 786440 | tf_op jit(solution)/shard_map/ppermute | solution.py:339
  133.8 5.2 %search.7.refs_6_ = f32[8,3072]{1,0:T(8,128)S(1)} custom-call(bf16[4096,512]{1,0:T(8,128)(2,1)S(1)} %get-tuple-element.29.own_ref, bf16[512,512]{1,0:T(8,128)(2,1)S(1)} %collective-permute-done.16.other_ref, bf16[512,1024]{1,0:T(8,128)(2,1)S(1)} %turn.4.refs_0_, bf16[512,1024]{1,0:T(8,128)(2,1)S(1)} %copy-done.1, ...), custom_call_target="tpu_custom_call" | custom-call | flops 3221225472 | bytes 7340032 | tf_op jit(solution)/shard_map/search/pallas_call | solution.py:303
  139.4 8.4 %search.8.refs_6_ = f32[8,3072]{1,0:T(8,128)S(1)} custom-call(bf16[4096,512]{1,0:T(8,128)(2,1)S(1)} %get-tuple-element.29.own_ref, bf16[1024,512]{1,0:T(8,128)(2,1)S(1)} %collective-permute-done.15.other_ref, bf16[512,1024]{1,0:T(8,128)(2,1)S(1)} %turn.4.refs_0_, bf16[512,1024]{1,0:T(8,128)(2,1)S(1)} %copy-done.1, ...), custom_call_target="tpu_custom_call" | custom-call | flops 6442450944 | bytes 8388608 | tf_op jit(solution)/shard_map/search/pallas_call | solution.py:303
  147.9 1.1 collective-permute-done.14.other_ref
  149.0 8.4 %search.9.refs_6_ = f32[8,3072]{1,0:T(8,128)S(1)} custom-call(bf16[4096,512]{1,0:T(8,128)(2,1)S(1)} %get-tuple-element.29.own_ref, bf16[1024,512]{1,0:T(8,128)(2,1)S(1)} %collective-permute-done.14.other_ref, bf16[512,1024]{1,0:T(8,128)(2,1)S(1)} %turn.4.refs_0_, bf16[512,1024]{1,0:T(8,128)(2,1)S(1)} %copy-done.1, ...), custom_call_target="tpu_custom_call" | custom-call | flops 6442450944 | bytes 8388608 | tf_op jit(solution)/shard_map/search/pallas_call | solution.py:303
  157.4 2.8 %collective-permute-done.13.other_ref = bf16[512,512]{1,0:T(8,128)(2,1)S(1)} collective-permute-done((bf16[512,512]{1,0:T(8,128)(2,1)S(1)}, bf16[512,512]{1,0:T(8,128)(2,1)S(1)}, u32[]{:S(2)}, u32[]{:S(2)}) %collective-permute-start.13) | collective-permute-done | bytes 524320 | tf_op jit(solution)/shard_map/ppermute | solution.py:339
  160.2 5.2 %search.10.refs_6_ = f32[8,3072]{1,0:T(8,128)S(1)} custom-call(bf16[4096,512]{1,0:T(8,128)(2,1)S(1)} %get-tuple-element.29.own_ref, bf16[512,512]{1,0:T(8,128)(2,1)S(1)} %collective-permute-done.13.other_ref, bf16[512,1024]{1,0:T(8,128)(2,1)S(1)} %turn.4.refs_0_, bf16[512,1024]{1,0:T(8,128)(2,1)S(1)} %copy-done.1, ...), custom_call_target="tpu_custom_call" | custom-call | flops 3221225472 | bytes 7340032 | tf_op jit(solution)/shard_map/search/pallas_call | solution.py:303
  165.4 6.0 %collective-permute-done.12.other_ref = bf16[512,512]{1,0:T(8,128)(2,1)S(1)} collective-permute-done((bf16[512,512]{1,0:T(8,128)(2,1)S(1)}, bf16[512,512]{1,0:T(8,128)(2,1)S(1)}, u32[]{:S(2)}, u32[]{:S(2)}) %collective-permute-start.12) | collective-permute-done | bytes 524320 | tf_op jit(solution)/shard_map/ppermute | solution.py:339
  171.4 5.2 %search.11.refs_6_ = f32[8,3072]{1,0:T(8,128)S(1)} custom-call(bf16[4096,512]{1,0:T(8,128)(2,1)S(1)} %get-tuple-element.29.own_ref, bf16[512,512]{1,0:T(8,128)(2,1)S(1)} %collective-permute-done.12.other_ref, bf16[512,1024]{1,0:T(8,128)(2,1)S(1)} %turn.4.refs_0_, bf16[512,1024]{1,0:T(8,128)(2,1)S(1)} %copy-done.1, ...), custom_call_target="tpu_custom_call" | custom-call | flops 3221225472 | bytes 7340032 | tf_op jit(solution)/shard_map/search/pallas_call | solution.py:303
  177.0 3.4 %search.12.refs_6_ = f32[8,3072]{1,0:T(8,128)S(1)} custom-call(bf16[4096,512]{1,0:T(8,128)(2,1)S(1)} %get-tuple-element.29.own_ref, bf16[256,512]{1,0:T(8,128)(2,1)S(1)} %collective-permute-done.11.other_ref, bf16[512,1024]{1,0:T(8,128)(2,1)S(1)} %turn.4.refs_0_, bf16[512,1024]{1,0:T(8,128)(2,1)S(1)} %copy-done.1, ...), custom_call_target="tpu_custom_call" | custom-call | flops 1610612736 | bytes 6815744 | tf_op jit(solution)/shard_map/search/pallas_call | solution.py:303
  180.4 1.5 collective-permute-done.6.other_ref
  181.9 3.4 %search.13 = (f32[1,1024]{1,0:T(1,128)S(1)}, f32[1,1024]{1,0:T(1,128)S(1)}, f32[1,1024]{1,0:T(1,128)S(1)}) custom-call(bf16[4096,512]{1,0:T(8,128)(2,1)S(1)} %get-tuple-element.29.own_ref, bf16[256,512]{1,0:T(8,128)(2,1)S(1)} %collective-permute-done.6.other_ref, bf16[512,1024]{1,0:T(8,128)(2,1)S(1)} %turn.4.refs_0_, bf16[512,1024]{1,0:T(8,128)(2,1)S(1)} %copy-done.1, ...), custom_call_target="tpu_custom_call" | custom-call | flops 1610612736 | bytes 6815744 | tf_op jit(solution)/shard_map/search/pallas_call | solution.py:303
  185.8 0.7 collective-permute-done.17
  186.5 11.3 %collective-permute-start.19 = (f32[1024]{0:T(1024)S(1)}, f32[1024]{0:T(1024)S(1)}, u32[]{:S(2)}, u32[]{:S(2)}) collective-permute-start(f32[1024]{0:T(1024)S(1)} %get-tuple-element.45), channel_id=1, source_target_pairs={{124,0},{125,1},{126,2},{127,3},{0,4},{1,5},{2,6},{3,7},{4,8},{5,9... | collective-permute-start | bytes 12296 | tf_op jit(solution)/shard_map/ppermute | solution.py:339
  197.8 2.8 %collective-permute-start.20 = (f32[1024]{0:T(1024)S(1)}, f32[1024]{0:T(1024)S(1)}, u32[]{:S(2)}, u32[]{:S(2)}) collective-permute-start(f32[1024]{0:T(1024)S(1)} %get-tuple-element.45), channel_id=1, source_target_pairs={{125,0},{124,1},{127,2},{126,3},{1,4},{0,5},{3,6},{2,7},{5,8},{4,9... | collective-permute-start | bytes 12296 | tf_op jit(solution)/shard_map/ppermute | solution.py:339
  200.7 1.1 collective-permute-start.18
  202.0 2.6 %collective-permute-done.18 = f32[1024]{0:T(1024)S(1)} collective-permute-done((f32[1024]{0:T(1024)S(1)}, f32[1024]{0:T(1024)S(1)}, u32[]{:S(2)}, u32[]{:S(2)}) %collective-permute-start.18) | collective-permute-done | bytes 4128 | tf_op jit(solution)/shard_map/ppermute | solution.py:339
  (41 shorter events, 3.6 us)
Async XLA Ops:
  0.6 38.3 %copy-start.5 = (s32[1024,1]{0,1:T(1,128)S(1)}, s32[1024,1]{0,1:T(1,128)}, u32[]{:S(2)}) copy-start(s32[1024,1]{0,1:T(1,128)} %param.5) | copy-start | bytes 12292
  0.6 49.8 %copy-start.6 = (s32[1024]{0:T(1024)S(1)}, s32[1024]{0:T(1024)}, u32[]{:S(2)}) copy-start(s32[1024]{0:T(1024)} %param.6) | copy-start | bytes 12292
  0.6 26.9 %collective-permute-start.4 = (bf16[1024,512]{1,0:T(8,128)(2,1)}, bf16[1024,512]{1,0:T(8,128)(2,1)S(1)}, u32[]{:S(2)}, u32[]{:S(2)}) collective-permute-start(bf16[1024,512]{1,0:T(8,128)(2,1)} %refs_0_.1), channel_id=1, source_target_pairs={{5,0},{4,1},{7,2},{6,3},{1,4},{0,5},{3,6},{2,7},{13,8},{12,9},{15,... | collective-permute-start | bytes 3145736 | tf_op jit(solution)/shard_map/ppermute | solution.py:339
  4.5 26.1 %collective-permute-start.2 = (bf16[1024,512]{1,0:T(8,128)(2,1)}, bf16[1024,512]{1,0:T(8,128)(2,1)S(1)}, u32[]{:S(2)}, u32[]{:S(2)}) collective-permute-start(bf16[1024,512]{1,0:T(8,128)(2,1)} %refs_0_.1), channel_id=1, source_target_pairs={{4,0},{5,1},{6,2},{7,3},{0,4},{1,5},{2,6},{3,7},{12,8},{13,9},{14,... | collective-permute-start | bytes 3145736 | tf_op jit(solution)/shard_map/ppermute | solution.py:339
  8.4 47.5 %all-to-all-start = ((bf16[32,136,128]{2,1,0:T(8,128)(2,1)}), bf16[32,136,128]{2,1,0:T(8,128)(2,1)S(1)}, u32[]{:S(2)}, u32[]{:S(2)}) async-start(bf16[32,136,128]{2,1,0:T(8,128)(2,1)} %pack.2), calls=%async_computation | async-start | bytes 2228224 | tf_op jit(solution)/shard_map/all_to_all | solution.py:356
  28.9 42.7 %collective-permute-start.9 = (bf16[512,1024]{1,0:T(8,128)(2,1)}, bf16[512,1024]{1,0:T(8,128)(2,1)}, u32[]{:S(2)}, u32[]{:S(2)}) collective-permute-start(bf16[512,1024]{1,0:T(8,128)(2,1)} %turn.7), channel_id=1, source_target_pairs={{12,4},{13,5},{14,6},{15,7},{20,12},{21,13},{22,14},{23,15},{28,20... | collective-permute-start | bytes 3145736 | tf_op jit(solution)/shard_map/ppermute | solution.py:339
  31.9 43.2 %collective-permute-start.7 = (bf16[512,1024]{1,0:T(8,128)(2,1)}, bf16[512,1024]{1,0:T(8,128)(2,1)}, u32[]{:S(2)}, u32[]{:S(2)}) collective-permute-start(bf16[512,1024]{1,0:T(8,128)(2,1)} %turn.6), channel_id=1, source_target_pairs={{12,4},{13,5},{14,6},{15,7},{20,12},{21,13},{22,14},{23,15},{28,20... | collective-permute-start | bytes 3145736 | tf_op jit(solution)/shard_map/ppermute | solution.py:339
  34.3 35.7 %collective-permute-start.3 = (bf16[512,512]{1,0:T(8,128)(2,1)}, bf16[512,512]{1,0:T(8,128)(2,1)}, u32[]{:S(2)}, u32[]{:S(2)}) collective-permute-start(bf16[512,512]{1,0:T(8,128)(2,1)} %slice.8), channel_id=1, source_target_pairs={{5,0},{4,1},{7,2},{6,3},{1,4},{0,5},{3,6},{2,7},{13,8},{12,9},{15,... | collective-permute-start | bytes 1572872 | tf_op jit(solution)/shard_map/ppermute | solution.py:339
  38.9 31.2 %collective-permute-start.5 = (bf16[512,512]{1,0:T(8,128)(2,1)}, bf16[512,512]{1,0:T(8,128)(2,1)}, u32[]{:S(2)}, u32[]{:S(2)}) collective-permute-start(bf16[512,512]{1,0:T(8,128)(2,1)} %slice.9), channel_id=1, source_target_pairs={{4,0},{5,1},{6,2},{7,3},{0,4},{1,5},{2,6},{3,7},{12,8},{13,9},{14,... | collective-permute-start | bytes 1572872 | tf_op jit(solution)/shard_map/ppermute | solution.py:339
  38.9 11.5 %collective-permute-start = (s32[1024,1]{0,1:T(1,128)S(1)}, s32[1024,1]{0,1:T(1,128)S(1)}, u32[]{:S(2)}, u32[]{:S(2)}) collective-permute-start(s32[1024,1]{0,1:T(1,128)S(1)} %copy-done.5), channel_id=1, source_target_pairs={{4,0},{5,1},{6,2},{7,3},{0,4},{1,5},{2,6},{3,7},{12,8},{13,9},{14,... | collective-permute-start | bytes 12296 | tf_op jit(solution)/shard_map/ppermute | solution.py:339
  50.4 2.8 %collective-permute-start.1 = (s32[1024]{0:T(1024)S(1)}, s32[1024]{0:T(1024)S(1)}, u32[]{:S(2)}, u32[]{:S(2)}) collective-permute-start(s32[1024]{0:T(1024)S(1)} %copy-done.6), channel_id=1, source_target_pairs={{4,0},{5,1},{6,2},{7,3},{0,4},{1,5},{2,6},{3,7},{12,8},{13,9},{14,... | collective-permute-start | bytes 12296 | tf_op jit(solution)/shard_map/ppermute | solution.py:339
  55.8 29.1 %all-to-all-start.1 = ((bf16[32,136,128]{2,1,0:T(8,128)(2,1)}), bf16[32,136,128]{2,1,0:T(8,128)(2,1)S(1)}, u32[]{:S(2)}, u32[]{:S(2)}) async-start(bf16[32,136,128]{2,1,0:T(8,128)(2,1)} %pack.3), calls=%async_computation.1 | async-start | bytes 2228224 | tf_op jit(solution)/shard_map/all_to_all | solution.py:356
  68.3 1.2 copy-start.4
  71.5 6.4 %copy-start = (bf16[512,1024]{1,0:T(8,128)(2,1)}, bf16[512,1024]{1,0:T(8,128)(2,1)S(1)}, u32[]{:S(2)}) copy-start(bf16[512,1024]{1,0:T(8,128)(2,1)S(1)} %turn.5.refs_1_) | copy-start | bytes 3145732
  74.7 56.1 %collective-permute-start.10 = (bf16[512,1024]{1,0:T(8,128)(2,1)}, bf16[512,1024]{1,0:T(8,128)(2,1)}, u32[]{:S(2)}, u32[]{:S(2)}) collective-permute-start(bf16[512,1024]{1,0:T(8,128)(2,1)} %get-tuple-element.40), channel_id=1, source_target_pairs={{2,0},{3,1},{0,2},{1,3},{6,4},{7,5},{4,6},{5,7},{10,8},{11,9},{8,1... | collective-permute-start | bytes 3145736 | tf_op jit(solution)/shard_map/ppermute | solution.py:339
  77.9 53.0 %collective-permute-start.8 = (bf16[512,1024]{1,0:T(8,128)(2,1)}, bf16[512,1024]{1,0:T(8,128)(2,1)}, u32[]{:S(2)}, u32[]{:S(2)}) collective-permute-start(bf16[512,1024]{1,0:T(8,128)(2,1)} %get-tuple-element.42), channel_id=1, source_target_pairs={{2,0},{3,1},{0,2},{1,3},{6,4},{7,5},{4,6},{5,7},{10,8},{11,9},{8,1... | collective-permute-start | bytes 3145736 | tf_op jit(solution)/shard_map/ppermute | solution.py:339
  88.6 39.3 %collective-permute-start.16 = (bf16[512,512]{1,0:T(8,128)(2,1)S(1)}, bf16[512,512]{1,0:T(8,128)(2,1)S(1)}, u32[]{:S(2)}, u32[]{:S(2)}) collective-permute-start(bf16[512,512]{1,0:T(8,128)(2,1)S(1)} %get-tuple-element.36), channel_id=1, source_target_pairs={{1,0},{0,1},{3,2},{2,3},{5,4},{4,5},{7,6},{6,7},{9,8},{8,9},{11,10... | collective-permute-start | bytes 1572872 | tf_op jit(solution)/shard_map/ppermute | solution.py:339
  93.6 45.5 %collective-permute-start.15 = (bf16[1024,512]{1,0:T(8,128)(2,1)S(1)}, bf16[1024,512]{1,0:T(8,128)(2,1)S(1)}, u32[]{:S(2)}, u32[]{:S(2)}) collective-permute-start(bf16[1024,512]{1,0:T(8,128)(2,1)S(1)} %get-tuple-element.35), channel_id=1, source_target_pairs={{1,0},{0,1},{3,2},{2,3},{5,4},{4,5},{7,6},{6,7},{9,8},{8,9},{11,10... | collective-permute-start | bytes 3145736 | tf_op jit(solution)/shard_map/ppermute | solution.py:339
  101.5 47.4 %collective-permute-start.14 = (bf16[1024,512]{1,0:T(8,128)(2,1)S(1)}, bf16[1024,512]{1,0:T(8,128)(2,1)S(1)}, u32[]{:S(2)}, u32[]{:S(2)}) collective-permute-start(bf16[1024,512]{1,0:T(8,128)(2,1)S(1)} %get-tuple-element.34), channel_id=1, source_target_pairs={{1,0},{0,1},{3,2},{2,3},{5,4},{4,5},{7,6},{6,7},{9,8},{8,9},{11,10... | collective-permute-start | bytes 3145736 | tf_op jit(solution)/shard_map/ppermute | solution.py:339
  114.9 18.9 %copy-start.1 = (bf16[512,1024]{1,0:T(8,128)(2,1)S(1)}, bf16[512,1024]{1,0:T(8,128)(2,1)}, u32[]{:S(2)}) copy-start(bf16[512,1024]{1,0:T(8,128)(2,1)} %copy-done) | copy-start | bytes 3145732
  114.9 18.9 %copy-start.2 = (bf16[512,1024]{1,0:T(8,128)(2,1)S(1)}, bf16[512,1024]{1,0:T(8,128)(2,1)}, u32[]{:S(2)}) copy-start(bf16[512,1024]{1,0:T(8,128)(2,1)} %get-tuple-element.41.refs_5_) | copy-start | bytes 3145732
  114.9 18.9 %copy-start.3 = (bf16[512,1024]{1,0:T(8,128)(2,1)S(1)}, bf16[512,1024]{1,0:T(8,128)(2,1)}, u32[]{:S(2)}) copy-start(bf16[512,1024]{1,0:T(8,128)(2,1)} %get-tuple-element.43.refs_4_) | copy-start | bytes 3145732
  127.8 32.3 %collective-permute-start.13 = (bf16[512,512]{1,0:T(8,128)(2,1)S(1)}, bf16[512,512]{1,0:T(8,128)(2,1)S(1)}, u32[]{:S(2)}, u32[]{:S(2)}) collective-permute-start(bf16[512,512]{1,0:T(8,128)(2,1)S(1)} %get-tuple-element.33), channel_id=1, source_target_pairs={{1,0},{0,1},{3,2},{2,3},{5,4},{4,5},{7,6},{6,7},{9,8},{8,9},{11,10... | collective-permute-start | bytes 1572872 | tf_op jit(solution)/shard_map/ppermute | solution.py:339
  130.8 40.6 %collective-permute-start.12 = (bf16[512,512]{1,0:T(8,128)(2,1)S(1)}, bf16[512,512]{1,0:T(8,128)(2,1)S(1)}, u32[]{:S(2)}, u32[]{:S(2)}) collective-permute-start(bf16[512,512]{1,0:T(8,128)(2,1)S(1)} %get-tuple-element.32), channel_id=1, source_target_pairs={{1,0},{0,1},{3,2},{2,3},{5,4},{4,5},{7,6},{6,7},{9,8},{8,9},{11,10... | collective-permute-start | bytes 1572872 | tf_op jit(solution)/shard_map/ppermute | solution.py:339
  130.9 46.1 %collective-permute-start.11 = (bf16[256,512]{1,0:T(8,128)(2,1)S(1)}, bf16[256,512]{1,0:T(8,128)(2,1)S(1)}, u32[]{:S(2)}, u32[]{:S(2)}) collective-permute-start(bf16[256,512]{1,0:T(8,128)(2,1)S(1)} %get-tuple-element.31), channel_id=1, source_target_pairs={{1,0},{0,1},{3,2},{2,3},{5,4},{4,5},{7,6},{6,7},{9,8},{8,9},{11,10... | collective-permute-start | bytes 786440 | tf_op jit(solution)/shard_map/ppermute | solution.py:339
  139.0 42.9 %collective-permute-start.6 = (bf16[256,512]{1,0:T(8,128)(2,1)S(1)}, bf16[256,512]{1,0:T(8,128)(2,1)S(1)}, u32[]{:S(2)}, u32[]{:S(2)}) collective-permute-start(bf16[256,512]{1,0:T(8,128)(2,1)S(1)} %get-tuple-element.30), channel_id=1, source_target_pairs={{1,0},{0,1},{3,2},{2,3},{5,4},{4,5},{7,6},{6,7},{9,8},{8,9},{11,10... | collective-permute-start | bytes 786440 | tf_op jit(solution)/shard_map/ppermute | solution.py:339
  185.3 1.2 collective-permute-start.17
  186.5 18.1 %collective-permute-start.19 = (f32[1024]{0:T(1024)S(1)}, f32[1024]{0:T(1024)S(1)}, u32[]{:S(2)}, u32[]{:S(2)}) collective-permute-start(f32[1024]{0:T(1024)S(1)} %get-tuple-element.45), channel_id=1, source_target_pairs={{124,0},{125,1},{126,2},{127,3},{0,4},{1,5},{2,6},{3,7},{4,8},{5,9... | collective-permute-start | bytes 12296 | tf_op jit(solution)/shard_map/ppermute | solution.py:339
  197.8 6.8 %collective-permute-start.20 = (f32[1024]{0:T(1024)S(1)}, f32[1024]{0:T(1024)S(1)}, u32[]{:S(2)}, u32[]{:S(2)}) collective-permute-start(f32[1024]{0:T(1024)S(1)} %get-tuple-element.45), channel_id=1, source_target_pairs={{125,0},{124,1},{127,2},{126,3},{1,4},{0,5},{3,6},{2,7},{5,8},{4,9... | collective-permute-start | bytes 12296 | tf_op jit(solution)/shard_map/ppermute | solution.py:339
  200.7 4.0 %collective-permute-start.18 = (f32[1024]{0:T(1024)S(1)}, f32[1024]{0:T(1024)S(1)}, u32[]{:S(2)}, u32[]{:S(2)}) collective-permute-start(f32[1024]{0:T(1024)S(1)} %get-tuple-element.44), channel_id=1, source_target_pairs={{1,0},{0,1},{3,2},{2,3},{5,4},{4,5},{7,6},{6,7},{9,8},{8,9},{11,10... | collective-permute-start | bytes 12296 | tf_op jit(solution)/shard_map/ppermute | solution.py:339
